TPU v7x, 32 devices: a whole 2x2x4 slice. The times are simulated.
32 devices in a mesh: gx: 4 (over z), gy: 4 (over y, x), gz: 2 (over core).
Axes of the slice: x: 2, y: 2, z: 4, core: 2. Of those that a mesh axis runs over, the one named last changes fastest.
Arguments:
- old_state: float32 [5, 64, 16384], P(None, None, ('gx', 'gy', 'gz')), may hold values from -0.5 to 3.5, as said below
- element_size: float32 [8192], P(('gx', 'gy', 'gz')), may hold values from 0.5 to 2
- old_start: int32 [33], replicated, may hold values from 0 to 8192, as said below
- neighbour: int32 [6, 8192], P(None, ('gx', 'gy', 'gz')), may hold values from 0 to 8191, as said below
- orientation: int32 [6, 8192], P(None, ('gx', 'gy', 'gz')), may hold values from 0 to 7
Outputs:
- final_state: float32 [5, 64, 8192], P(None, None, ('gx', 'gy', 'gz'))
Inputs may be any that keep to these rules, and one draw needn't show every extreme that they name: `old_state`: A gas with density and pressure between 0.85 and 1.15 and each velocity component below 0.3 in magnitude at every node, in conserved form. old_start[0] is 0 and old_start[32] is 8192; old_start[d] differs from d * 256 by at most 128, so a device's old range holds at most 512 elements. `neighbour`: after repartitioning, the element behind a face is owned by the owner of the element itself or by the device just before or just after it along the curve, counted cyclically; of the 1536 faces of each device's elements exactly 32 lead to the device before and exactly 32 to the device after.
All inputs are finite; a program needn't handle non-finite values.
Results may differ from a plain program's by a relative error of at most 0.0001.
Values sent between devices are 32-bit elements; how exact they have to be, the bound alone decides.
No kernel may reach another device: no remote copies, remote signals or barrier semaphores. Data moves between devices by JAX's collectives and lax.ppermute only.
A program may use at most 128 MiB of HBM per device.

v0:
```python
import functools

import jax
import jax.numpy as jnp
import numpy as np
from jax import lax
from jax.experimental import pallas as pl
from jax.experimental.pallas import tpu as pltpu
from jax.sharding import PartitionSpec as P

AXES = ("gx", "gy", "gz")
TIME_STEP = 0.03
LIFT = 6.0
VARS = 5
NODES = 64
EL = 256
LANES = 128
REMOTE = 32
FACES = 6
ROWS = VARS * NODES
BF = jnp.bfloat16
F32 = jnp.float32
I32 = jnp.int32


def gll_derivative():
    points = np.array([-1.0, -1.0 / np.sqrt(5.0), 1.0 / np.sqrt(5.0), 1.0])
    weights = np.array(
        [1.0 / np.prod([points[c] - points[p] for p in range(4) if p != c]) for c in range(4)]
    )
    matrix = np.zeros((4, 4))
    for row in range(4):
        for col in range(4):
            if row != col:
                matrix[row, col] = weights[col] / weights[row] / (points[row] - points[col])
        matrix[row, row] = -np.sum(matrix[row])
    return matrix


def node_derivatives():
    d, one = gll_derivative(), np.eye(4)
    parts = [
        np.kron(np.kron(d, one), one),
        np.kron(np.kron(one, d), one),
        np.kron(np.kron(one, one), d),
    ]
    return np.concatenate(parts, axis=1).astype(np.float32)


def iota(shape, dim):
    return lax.broadcasted_iota(I32, shape, dim)


def split(x):
    hi = x.astype(BF)
    return hi, (x - hi.astype(F32)).astype(BF)


def mm(a, b):
    return jnp.dot(a, b, preferred_element_type=F32)


def face_rows(ref, h, v, f):
    base = v * NODES
    if f < 2:
        return ref[h, base + 48 * f : base + 48 * f + 16, :]
    if f < 4:
        first = base + 12 * (f - 2)
        return jnp.concatenate([ref[h, first + 16 * i : first + 16 * i + 4, :] for i in range(4)], 0)
    return ref[h, pl.ds(base + 3 * (f - 4), 16, stride=4), :]


def add_face_rows(ref, lead, base, f, val):
    at = (lambda r: (lead, r)) if lead is not None else (lambda r: (r,))
    if f < 2:
        r = at(pl.ds(base + 48 * f, 16)) + (slice(None),)
        ref[r] = ref[r] + val
    elif f < 4:
        for i in range(4):
            r = at(pl.ds(base + 12 * (f - 2) + 16 * i, 4)) + (slice(None),)
            ref[r] = ref[r] + val[4 * i : 4 * i + 4, :]
    else:
        r = at(pl.ds(base + 3 * (f - 4), 16, stride=4)) + (slice(None),)
        ref[r] = ref[r] + val


def rank_of(sizes):
    return (lax.axis_index("gx") * sizes[1] + lax.axis_index("gy")) * sizes[2] + lax.axis_index("gz")


def send_kernel(sizes, start, old, nb_ref, ori_ref, s_a, s_b, rows_ref, col_ref, mk):
    n = sizes[0] * sizes[1] * sizes[2]
    d = rank_of(sizes)
    even = (d & 1) == 0
    up = jnp.where(d + 1 == n, 0, d + 1) * EL
    down = jnp.where(d == 0, n - 1, d - 1) * EL
    base_a = jnp.where(even, up, down)
    base_b = jnp.where(even, down, up)
    nb = nb_ref[...]
    rel = [nb - base_a, nb - base_b]
    mk[...] = jnp.zeros((16, EL), F32)
    for k in range(2):
        mk[8 * k : 8 * k + FACES, :] = jnp.where((rel[k] >= 0) & (rel[k] < EL), 1.0, 0.0)
    mask = mk[...]
    upper = jnp.where(iota((EL, EL), 0) <= iota((EL, EL), 1), 1.0, 0.0).astype(BF)
    inclusive = mm(mask.astype(BF), upper)
    total = jnp.broadcast_to(inclusive[:, EL - 1 : EL], (16, LANES)).astype(BF)
    r, c = iota((16, 16), 0), iota((16, 16), 1)
    lower = jnp.where((c < r) & ((c >> 3) == (r >> 3)), 1.0, 0.0).astype(BF)
    offset = mm(lower, total)[:, 0:1]
    place = jnp.where(mask > 0.5, inclusive + offset - 1.0, -1.0)
    face = iota((FACES, EL), 0)
    own = (face * EL + iota((FACES, EL), 1) + 2048 * ori_ref[...]).astype(F32)
    slot = iota((REMOTE, EL), 0).astype(F32)
    lists = []
    for k in range(2):
        req = ((face ^ 1) * EL + rel[k]).astype(F32)
        acc_r = jnp.zeros((REMOTE, EL), F32)
        acc_o = jnp.zeros((REMOTE, EL), F32)
        for f in range(FACES):
            hit = place[8 * k + f : 8 * k + f + 1, :] == slot
            acc_r = jnp.where(hit, req[f : f + 1, :], acc_r)
            acc_o = jnp.where(hit, own[f : f + 1, :], acc_o)
        lists.append((jnp.sum(acc_r, 1, keepdims=True), jnp.sum(acc_o, 1, keepdims=True)))
    col = jnp.concatenate([lists[0][0], lists[1][0], lists[0][1], lists[1][1]], 0)
    wide = jnp.broadcast_to(col, (LANES, LANES))
    row = jnp.transpose(wide)[0:8, :]
    turn = jnp.floor(row * (1.0 / 2048.0))
    code = row - 2048.0 * turn
    rows_ref[0:8, :] = code
    rows_ref[8:16, :] = turn
    col_ref[...] = wide[64:128, :]

    o = start[d] - d * EL
    first = EL - o
    q, rot = first >> 7, first & 127
    lane = iota((NODES, LANES), 1)
    keep = lane < LANES - rot
    back = (LANES - rot) & 127
    t0 = pl.ds(pl.multiple_of(q * LANES, LANES), LANES)
    t1 = pl.ds(pl.multiple_of(jnp.minimum(q + 1, 3) * LANES, LANES), LANES)

    def put(to_up, to_down):
        for v in range(VARS):
            rows = slice(v * NODES, v * NODES + NODES)
            to_up[rows, :] = jnp.where(
                keep, pltpu.roll(old[v, :, t0], back, 1), pltpu.roll(old[v, :, t1], back, 1)
            )
            to_down[rows, :] = pltpu.roll(old[v, :, 0:LANES], o & 127, 1)

    @pl.when(even)
    def _():
        put(s_a, s_b)

    @pl.when(jnp.logical_not(even))
    def _():
        put(s_b, s_a)

    s_a[ROWS : ROWS + 8, :] = code
    s_b[ROWS : ROWS + 8, :] = code


def own_kernel(sizes, start, old, col_ref, own, ohs):
    d = rank_of(sizes)
    s = d * EL - start[d]
    q, rot = s >> 7, s & 127
    keep = iota((NODES, LANES), 1) < LANES - rot
    back = (LANES - rot) & 127
    for v in range(VARS):
        rows = slice(v * NODES, v * NODES + NODES)
        t = [
            pltpu.roll(
                old[v, :, pl.ds(pl.multiple_of(jnp.maximum(q + i, 0) * LANES, LANES), LANES)], back, 1
            )
            for i in range(3)
        ]
        own[0, rows, :] = jnp.where(keep, t[0], t[1])
        own[1, rows, :] = jnp.where(keep, t[1], t[2])
    code = col_ref[...].astype(I32)
    lane = iota((64, LANES), 1)
    for h in range(2):
        hit = jnp.where((code & 255) == lane + h * LANES, 1.0, 0.0).astype(BF)
        ohs[0:64, h * LANES : h * LANES + LANES] = hit
        ohs[64:128, h * LANES : h * LANES + LANES] = jnp.zeros((64, LANES), BF)


def requested(fld, one_hot, g):
    acc = None
    for f in range(FACES):
        t = jnp.concatenate(
            [
                jnp.concatenate([face_rows(fld, h, v, f) for v in range(VARS)], 0)
                for h in range(2)
            ],
            1,
        )
        part = mm(jnp.concatenate(split(t), 0), one_hot(f))
        acc = part if acc is None else acc + part
    g[...] = acc[0:80, :] + acc[80:160, :]


def join_kernel(sizes, start, own, r_a, r_b, rows_ref, fld, ohg, g):
    d = rank_of(sizes)
    even = (d & 1) == 0
    o = start[d] - d * EL
    u = start[d + 1] - d * EL
    lane = iota((NODES, LANES), 1)
    for v in range(VARS):
        rows = slice(v * NODES, v * NODES + NODES)
        a, b = r_a[rows, :], r_b[rows, :]
        fld[0, rows, :] = jnp.where(lane < o, jnp.where(even, b, a), own[0, rows, :])
        fld[1, rows, :] = jnp.where(lane + LANES >= u, jnp.where(even, a, b), own[1, rows, :])
    lane8 = iota((8, LANES), 1)
    code = jnp.where(
        lane8 < 32,
        r_a[ROWS : ROWS + 8, :],
        jnp.where(lane8 < 64, r_b[ROWS : ROWS + 8, :], rows_ref[0:8, :]),
    ).astype(I32)
    line = jnp.broadcast_to(code[0:1, :], (EL, LANES)) - iota((EL, LANES), 0)

    def one_hot(f):
        hot = jnp.where(line == f * EL, 1.0, 0.0).astype(BF)
        ohg[f * EL : f * EL + EL, :] = hot
        return hot

    requested(fld, one_hot, g)


def fluxes(u, speeds, p):
    out = []
    for a in range(3):
        s = speeds[a]
        row = [u[0] * s, u[1] * s, u[2] * s, u[3] * s, (u[4] + p) * s]
        row[1 + a] = row[1 + a] + p
        out.append(row)
    return out


def directed(u, axis_is):
    inv = 1.0 / u[0]
    p = 0.4 * (u[4] - 0.5 * ((u[1] * u[1] + u[2] * u[2] + u[3] * u[3]) * inv))
    mom = jnp.where(axis_is[0], u[1], jnp.where(axis_is[1], u[2], u[3]))
    s = mom * inv
    flux = [u[0] * s] + [u[i] * s for i in range(1, 4)] + [(u[4] + p) * s]
    zero = jnp.zeros_like(p)
    flux[1] = flux[1] + jnp.where(axis_is[0], p, zero)
    flux[2] = flux[2] + jnp.where(axis_is[1], p, zero)
    flux[3] = flux[3] + jnp.where(axis_is[0] | axis_is[1], zero, p)
    return flux, jnp.abs(s) + jnp.sqrt(1.4 * p * inv)


def correction(inner, outer, axis_is, half_sign):
    fi, si = directed(inner, axis_is)
    fo, so = directed(outer, axis_is)
    lam = 0.5 * jnp.maximum(si, so)
    return [half_sign * (fo[v] - fi[v]) - lam * (outer[v] - inner[v]) for v in range(VARS)]


def turned(x, b0, b1, b2):
    x = [jnp.where(b1, x[4 * (3 - p) + q], x[4 * p + q]) for p in range(4) for q in range(4)]
    x = [jnp.where(b2, x[4 * p + 3 - q], x[4 * p + q]) for p in range(4) for q in range(4)]
    return [jnp.where(b0, x[4 * t + s], x[4 * s + t]) for s in range(4) for t in range(4)]


def local_kernel(sizes, last, fld, nb_ref, ori_ref, size_ref, d_ref, *rest):
    if last:
        old_fld, part, acc, xs, xg, xq, xo, xc, it = rest
    else:
        part, acc, xs, xg, xq, xo, xc, it = rest
    d = rank_of(sizes)
    dh, dl = split(d_ref[...])
    dd = jnp.concatenate([dh, dl], 0)
    pieces = [[[], []] for _ in range(VARS)]
    for h in range(2):
        u = [fld[h, v * NODES : v * NODES + NODES, :] for v in range(VARS)]
        inv = 1.0 / u[0]
        speeds = [u[i] * inv for i in range(1, 4)]
        p = 0.4 * (u[4] - 0.5 * (u[1] * speeds[0] + u[2] * speeds[1] + u[3] * speeds[2]))
        fl = fluxes(u, speeds, p)
        for v in range(VARS):
            hl = [split(fl[a][v]) for a in range(3)]
            pieces[v][0].append(jnp.concatenate([x[0] for x in hl], 0))
            pieces[v][1].append(jnp.concatenate([x[1] for x in hl], 0))
    for v in range(VARS):
        hi = mm(dd, jnp.concatenate(pieces[v][0], 1))
        lo = mm(dh, jnp.concatenate(pieces[v][1], 1))
        vol = hi[0:NODES, :] + hi[NODES : 2 * NODES, :] + lo
        for h in range(2):
            acc[h, v * NODES : v * NODES + NODES, :] = vol[:, h * LANES : h * LANES + LANES]
    for v in range(VARS):
        for f in range(FACES):
            for h in range(2):
                t = face_rows(fld, h, v, f)
                b = v * 256
                xs[pl.ds(b + 2 * f + h, 16, stride=16), :] = t
                xg[pl.ds(b + 2 * (f ^ 1) + h, 16, stride=16), :] = t
                xq[pl.ds(b + 2 * (f ^ 1) + 1 - h, 16, stride=16), :] = t
    it[...] = jnp.zeros((32, LANES), I32)
    for h in range(2):
        it[pl.ds(h, FACES, stride=2), :] = nb_ref[:, h * LANES : h * LANES + LANES]
        it[pl.ds(16 + h, FACES, stride=2), :] = ori_ref[:, h * LANES : h * LANES + LANES]
    t = it[0:16, :] - d * EL
    turn = it[16:32, :]
    row = iota((16, LANES), 0)
    local = (t >= 0) & (t < EL) & (row < 12)
    same = ((t >> 7) & 1) == (row & 1)
    idx = t & 127
    b0, b1, b2 = (turn & 1) != 0, (turn & 2) != 0, (turn & 4) != 0
    for v in range(VARS):
        got = []
        for m in range(16):
            rows = slice(v * 256 + m * 16, v * 256 + m * 16 + 16)
            ga = jnp.take_along_axis(xg[rows, :], idx, axis=1)
            gb = jnp.take_along_axis(xq[rows, :], idx, axis=1)
            got.append(jnp.where(same, ga, gb))
        for m, x in enumerate(turned(got, b0, b1, b2)):
            xo[v * 256 + m * 16 : v * 256 + m * 16 + 16, :] = x
    axis_is = (row < 4, (row >= 4) & (row < 8))
    half_sign = jnp.where((row & 2) != 0, 0.5, -0.5)
    for m in range(16):
        rows = [slice(v * 256 + m * 16, v * 256 + m * 16 + 16) for v in range(VARS)]
        cor = correction([xs[r, :] for r in rows], [xo[r, :] for r in rows], axis_is, half_sign)
        for v in range(VARS):
            xc[rows[v], :] = jnp.where(local, LIFT * cor[v], 0.0)
    for v in range(VARS):
        for f in range(FACES):
            for h in range(2):
                add_face_rows(
                    acc, h, v * NODES, f, xc[pl.ds(v * 256 + 2 * f + h, 16, stride=16), :]
                )
    for h in range(2):
        size = size_ref[0:1, h * LANES : h * LANES + LANES]
        coef = (TIME_STEP * 2.0) / size
        for v in range(VARS):
            rows = slice(v * NODES, v * NODES + NODES)
            new = fld[h, rows, :] - coef * acc[h, rows, :]
            if last:
                new = 0.5 * old_fld[h, rows, :] + 0.5 * new
            part[h, rows, :] = new


def finish_kernel(last, part, g, r_a, r_b, rows_ref, ohs, size_ref, *rest):
    if last:
        out, ro, y, e = rest
    else:
        ohg, out, g_next, ro, y, e = rest
    lane = iota((80, LANES), 1)
    ro[0:80, :] = jnp.where(lane < 32, r_a[...], r_b[...])
    ro[80:128, :] = jnp.zeros((48, LANES), F32)
    code = pltpu.roll(rows_ref[0:8, :], 64, 1).astype(I32)
    turn = pltpu.roll(rows_ref[8:16, :], 64, 1).astype(I32)
    x = [ro[pl.ds(m, 8, stride=16), :] for m in range(16)]
    for m, val in enumerate(turned(x, (turn & 1) != 0, (turn & 2) != 0, (turn & 4) != 0)):
        y[8 * m : 8 * m + 8, :] = val
    live = iota((16, LANES), 1) < 64
    face = jnp.where(live, jnp.broadcast_to(code[0:1, :], (16, LANES)) >> 8, 0)
    axis_is = (face < 2, (face >= 2) & (face < 4))
    half_sign = jnp.where((face & 1) != 0, 0.5, -0.5)
    inner = [pltpu.roll(g[16 * v : 16 * v + 16, :], 64, 1) for v in range(VARS)]
    outer = [y[pl.ds(v, 16, stride=8), :] for v in range(VARS)]
    cor = correction(inner, outer, axis_is, half_sign)
    e[...] = jnp.zeros((ROWS, LANES), F32)
    for v in range(VARS):
        for f in range(FACES):
            add_face_rows(
                e, None, v * NODES, f, jnp.where(live & (face == f), cor[v], 0.0)
            )
    spread = mm(jnp.concatenate(split(e[...]), 0), ohs[...])
    scale = (TIME_STEP * 2.0 * LIFT) * (0.5 if last else 1.0)
    for h in range(2):
        coef = scale / size_ref[0:1, h * LANES : h * LANES + LANES]
        lanes = slice(h * LANES, h * LANES + LANES)
        for v in range(VARS):
            rows = slice(v * NODES, v * NODES + NODES)
            low = slice(ROWS + v * NODES, ROWS + v * NODES + NODES)
            new = part[h, rows, :] - coef * (spread[rows, lanes] + spread[low, lanes])
            if last:
                out[v, :, lanes] = new
            else:
                out[h, rows, :] = new
    if not last:
        requested(out, lambda f: ohg[f * EL : f * EL + EL, :], g_next)


def call(body, out_shape, scratch, cost, *args):
    spec = pl.BlockSpec(memory_space=pltpu.VMEM)
    specs = [
        pl.BlockSpec(memory_space=pltpu.SMEM) if a.dtype == I32 and a.ndim == 1 else spec
        for a in args
    ]
    return pl.pallas_call(
        body,
        out_shape=out_shape,
        in_specs=specs,
        out_specs=jax.tree.map(lambda _: spec, out_shape),
        scratch_shapes=scratch,
        cost_estimate=pl.CostEstimate(flops=cost, bytes_accessed=cost, transcendentals=0),
        compiler_params=pltpu.CompilerParams(vmem_limit_bytes=32 * 1024 * 1024),
    )(*args)


def shape(*dims, dtype=F32):
    return jax.ShapeDtypeStruct(dims, dtype)


def per_device(sizes, old_state, element_size, old_start, neighbour, orientation):
    n = sizes[0] * sizes[1] * sizes[2]
    pairs_a = [(i, i ^ 1) for i in range(n)]
    pairs_b = [(i, (i + 1) % n if i % 2 else (i - 1) % n) for i in range(n)]

    def exchange(a, b):
        r_b = lax.ppermute(b, AXES, pairs_b)
        r_a = lax.ppermute(a, AXES, pairs_a)
        return r_a, r_b

    size = element_size.reshape(1, EL)
    deriv = jnp.asarray(node_derivatives())
    s_a, s_b, rows, col = call(
        functools.partial(send_kernel, sizes),
        (shape(ROWS + 8, LANES), shape(ROWS + 8, LANES), shape(16, LANES), shape(64, LANES)),
        [pltpu.VMEM((16, EL), F32)],
        10000,
        old_start,
        old_state,
        neighbour,
        orientation,
    )
    r_a, r_b = exchange(s_a, s_b)
    own, ohs = call(
        functools.partial(own_kernel, sizes),
        (shape(2, ROWS, LANES), shape(LANES, EL, dtype=BF)),
        [],
        10000,
        old_start,
        old_state,
        col,
    )
    fld, ohg, g = call(
        functools.partial(join_kernel, sizes),
        (shape(2, ROWS, LANES), shape(FACES * EL, LANES, dtype=BF), shape(80, LANES)),
        [],
        10000,
        old_start,
        own,
        r_a,
        r_b,
        rows,
    )

    def local(last, *args):
        table = pltpu.VMEM((VARS * 256, LANES), F32)
        return call(
            functools.partial(local_kernel, sizes, last),
            shape(2, ROWS, LANES),
            [pltpu.VMEM((2, ROWS, LANES), F32)] + [table] * 5 + [pltpu.VMEM((32, LANES), I32)],
            20000,
            *args,
        )

    scratch = [
        pltpu.VMEM((LANES, LANES), F32),
        pltpu.VMEM((LANES, LANES), F32),
        pltpu.VMEM((ROWS, LANES), F32),
    ]
    r_a, r_b = exchange(g, g)
    part = local(False, fld, neighbour, orientation, size, deriv)
    first, g2 = call(
        functools.partial(finish_kernel, False),
        (shape(2, ROWS, LANES), shape(80, LANES)),
        scratch,
        10000,
        part,
        g,
        r_a,
        r_b,
        rows,
        ohs,
        size,
        ohg,
    )
    r_a, r_b = exchange(g2, g2)
    part = local(True, first, neighbour, orientation, size, deriv, fld)
    return call(
        functools.partial(finish_kernel, True),
        shape(VARS, NODES, EL),
        scratch,
        10000,
        part,
        g2,
        r_a,
        r_b,
        rows,
        ohs,
        size,
    )


def solution(mesh):
    sizes = tuple(mesh.shape[a] for a in AXES)
    in_specs = (P(None, None, AXES), P(AXES), P(), P(None, AXES), P(None, AXES))
    return jax.shard_map(
        functools.partial(per_device, sizes),
        mesh=mesh,
        in_specs=in_specs,
        out_specs=P(None, None, AXES),
        check_vma=False,
    )
```

profile of v0, /device:TPU:0, one launch (start us, length us, event | category | flops | bytes accessed | tf_op | source)
XLA Modules:
  0.0 32.3 jit_solution(11747690285680028935)
XLA Ops:
  0.0 0.0 copy-start
  0.0 1.1 %copy-done = f32[5,64,512]{2,1,0:T(8,128)S(1)} copy-done((f32[5,64,512]{2,1,0:T(8,128)S(1)}, f32[5,64,512]{2,1,0:T(8,128)}, u32[]{:S(2)}) %copy-start) | copy-done | bytes 655384
  1.1 0.0 copy-start.2
  1.1 0.7 %copy-done.2 = s32[6,256]{1,0:T(8,128)S(1)} copy-done((s32[6,256]{1,0:T(8,128)S(1)}, s32[6,256]{1,0:T(8,128)}, u32[]{:S(2)}) %copy-start.2) | copy-done | bytes 6168
  1.8 0.0 copy-start.4
  1.8 0.7 %copy-done.4 = s32[6,256]{1,0:T(8,128)S(1)} copy-done((s32[6,256]{1,0:T(8,128)S(1)}, s32[6,256]{1,0:T(8,128)}, u32[]{:S(2)}) %copy-start.4) | copy-done | bytes 6168
  2.5 0.0 copy-start.7
  2.5 0.7 %copy-done.7 = s32[33]{0:T(128)S(1)} copy-done((s32[33]{0:T(128)S(1)}, s32[33]{0:T(128)}, u32[]{:S(2)}) %copy-start.7) | copy-done | bytes 156
  3.1 1.4 %shard_map.64 = (f32[328,128]{1,0:T(8,128)S(1)}, f32[328,128]{1,0:T(8,128)S(1)}, f32[16,128]{1,0:T(8,128)S(1)}, f32[64,128]{1,0:T(8,128)S(1)}) custom-call(s32[33]{0:T(128)S(1)} %copy-done.7, f32[5,64,512]{2,1,0:T(8,128)S(1)} %copy-done, s32[6,256]{1,0:T(8,128)S(1)} %copy-done.2, s32[6,256]{1,0:T(8,128)S(1)} %copy-done.4), custom_call_target="tpu_custom_call" | custom-call | flops 10000 | bytes 10000 | tf_op jit(solution)/shard_map/pallas_call | solution.py:391
  4.5 0.5 %collective-permute-start = (f32[328,128]{1,0:T(8,128)S(1)}, f32[328,128]{1,0:T(8,128)S(1)}, u32[]{:S(2)}, u32[]{:S(2)}) collective-permute-start(f32[328,128]{1,0:T(8,128)S(1)} %get-tuple-element.18), channel_id=1, source_target_pairs={{0,1},{1,0},{2,3},{3,2},{4,5},{5,4},{6,7},{7,6},{8,9},{9,8},{10,11... | collective-permute-start | bytes 503816 | tf_op jit(solution)/shard_map/ppermute | solution.py:413
  5.0 6.6 %collective-permute-start.1 = (f32[328,128]{1,0:T(8,128)S(1)}, f32[328,128]{1,0:T(8,128)S(1)}, u32[]{:S(2)}, u32[]{:S(2)}) collective-permute-start(f32[328,128]{1,0:T(8,128)S(1)} %get-tuple-element.19), channel_id=1, source_target_pairs={{0,31},{1,2},{2,1},{3,4},{4,3},{5,6},{6,5},{7,8},{8,7},{9,10},{10,... | collective-permute-start | bytes 503816 | tf_op jit(solution)/shard_map/ppermute | solution.py:412
  11.6 0.8 %shard_map.65 = (f32[2,320,128]{2,1,0:T(8,128)S(1)}, bf16[128,256]{1,0:T(8,128)(2,1)S(1)}) custom-call(s32[33]{0:T(128)S(1)} %copy-done.7, f32[5,64,512]{2,1,0:T(8,128)S(1)} %copy-done, f32[64,128]{1,0:T(8,128)S(1)} %get-tuple-element.16.col_ref), custom_call_target="tpu_custom_call" | custom-call | flops 10000 | bytes 10000 | tf_op jit(solution)/shard_map/pallas_call | solution.py:391
  12.4 0.0 collective-permute-done.r_a
  12.4 2.3 %collective-permute-done.1.r_b = f32[328,128]{1,0:T(8,128)S(1)} collective-permute-done((f32[328,128]{1,0:T(8,128)S(1)}, f32[328,128]{1,0:T(8,128)S(1)}, u32[]{:S(2)}, u32[]{:S(2)}) %collective-permute-start.1) | collective-permute-done | bytes 167968 | tf_op jit(solution)/shard_map/ppermute | solution.py:412
  14.7 0.0 copy-start.3
  14.7 0.9 %shard_map.66 = (f32[2,320,128]{2,1,0:T(8,128)S(1)}, bf16[1536,128]{1,0:T(8,128)(2,1)S(1)}, f32[80,128]{1,0:T(8,128)S(1)}) custom-call(s32[33]{0:T(128)S(1)} %copy-done.7, f32[2,320,128]{2,1,0:T(8,128)S(1)} %get-tuple-element.17.own, f32[328,128]{1,0:T(8,128)S(1)} %collective-permute-done.r_a, f32[328,128]{1,0:T(8,128)S(1)} %collective-permute-done.1.r_b, ...), custom_call_target="tpu_custom_call" | custom-call | flops 10000 | bytes 10000 | tf_op jit(solution)/shard_map/pallas_call | solution.py:391
  15.6 5.4 %collective-permute-start.3 = (f32[80,128]{1,0:T(8,128)S(1)}, f32[80,128]{1,0:T(8,128)S(1)}, u32[]{:S(2)}, u32[]{:S(2)}) collective-permute-start(f32[80,128]{1,0:T(8,128)S(1)} %get-tuple-element.22.g), channel_id=1, source_target_pairs={{0,31},{1,2},{2,1},{3,4},{4,3},{5,6},{6,5},{7,8},{8,7},{9,10},{10,... | collective-permute-start | bytes 122888 | tf_op jit(solution)/shard_map/ppermute | solution.py:412
  21.0 0.0 collective-permute-start.2
  21.0 0.0 copy-done.1
  21.0 0.0 copy-done.3
  21.0 0.0 copy-done.5
  21.0 0.7 %copy-done.6 = f32[256]{0:T(256)S(1)} copy-done((f32[256]{0:T(256)S(1)}, f32[256]{0:T(256)}, u32[]{:S(2)}) %copy-start.6) | copy-done | bytes 1048
  21.7 1.6 %shard_map.67.part = f32[2,320,128]{2,1,0:T(8,128)S(1)} custom-call(f32[2,320,128]{2,1,0:T(8,128)S(1)} %get-tuple-element.21.fld.rest_0_, s32[6,256]{1,0:T(8,128)S(1)} %copy-done.3, s32[6,256]{1,0:T(8,128)S(1)} %copy-done.5, f32[1,256]{1,0:T(1,128)S(1)} %bitcast.1, f32[64,192]{1,0:T(8,128)S(1)} %copy-done.1), custom_call_target="tpu_custom_call" | custom-call | flops 20000 | bytes 20000 | tf_op jit(solution)/shard_map/pallas_call | solution.py:391
  23.3 0.0 collective-permute-done.3.r_b
  23.3 0.0 collective-permute-done.2.r_a
  23.3 0.8 %shard_map.68 = (f32[2,320,128]{2,1,0:T(8,128)S(1)}, f32[80,128]{1,0:T(8,128)S(1)}) custom-call(f32[2,320,128]{2,1,0:T(8,128)S(1)} %shard_map.67.part, f32[80,128]{1,0:T(8,128)S(1)} %get-tuple-element.22.g, f32[80,128]{1,0:T(8,128)S(1)} %collective-permute-done.2.r_a, f32[80,128]{1,0:T(8,128)S(1)} %collective-permute-done.3.r_b, ...), custom_call_target="tpu_custom_call" | custom-call | flops 10000 | bytes 10000 | tf_op jit(solution)/shard_map/pallas_call | solution.py:391
  24.1 4.8 %collective-permute-start.5 = (f32[80,128]{1,0:T(8,128)S(1)}, f32[80,128]{1,0:T(8,128)S(1)}, u32[]{:S(2)}, u32[]{:S(2)}) collective-permute-start(f32[80,128]{1,0:T(8,128)S(1)} %get-tuple-element.26.g), channel_id=1, source_target_pairs={{0,31},{1,2},{2,1},{3,4},{4,3},{5,6},{6,5},{7,8},{8,7},{9,10},{10,... | collective-permute-start | bytes 122888 | tf_op jit(solution)/shard_map/ppermute | solution.py:412
  28.9 0.0 collective-permute-start.4
  28.9 1.6 %shard_map.69.part = f32[2,320,128]{2,1,0:T(8,128)S(1)} custom-call(f32[2,320,128]{2,1,0:T(8,128)S(1)} %get-tuple-element.25.fld, s32[6,256]{1,0:T(8,128)S(1)} %copy-done.3, s32[6,256]{1,0:T(8,128)S(1)} %copy-done.5, f32[1,256]{1,0:T(1,128)S(1)} %bitcast.3, f32[64,192]{1,0:T(8,128)S(1)} %copy-done.1, f32[2,320,128]{2,1,0:T(8,128)S(1)} %get-tuple-element.21.fld.rest_0_), custom_call_target="tpu_custom_call" | custom-call | flops 20000 | bytes 20000 | tf_op jit(solution)/shard_map/pallas_call | solution.py:391
  30.5 0.7 %collective-permute-done.5.r_b = f32[80,128]{1,0:T(8,128)S(1)} collective-permute-done((f32[80,128]{1,0:T(8,128)S(1)}, f32[80,128]{1,0:T(8,128)S(1)}, u32[]{:S(2)}, u32[]{:S(2)}) %collective-permute-start.5) | collective-permute-done | bytes 40992 | tf_op jit(solution)/shard_map/ppermute | solution.py:412
  31.2 0.0 collective-permute-done.4.r_a
  31.2 1.1 %shard_map.70 = f32[5,64,256]{2,1,0:T(8,128)} custom-call(f32[2,320,128]{2,1,0:T(8,128)S(1)} %shard_map.69.part, f32[80,128]{1,0:T(8,128)S(1)} %get-tuple-element.26.g, f32[80,128]{1,0:T(8,128)S(1)} %collective-permute-done.4.r_a, f32[80,128]{1,0:T(8,128)S(1)} %collective-permute-done.5.r_b, f32[16,128]{1,0:T(8,128)S(1)} %get-tuple-element.20.rows_ref, ...), custom_call_target="tpu_custom_call" | custom-call | flops 10000 | bytes 10000 | tf_op jit(solution)/shard_map/pallas_call | solution.py:391
  (3 shorter events, 0.0 us)
Async XLA Ops:
  0.0 1.1 %copy-start = (f32[5,64,512]{2,1,0:T(8,128)S(1)}, f32[5,64,512]{2,1,0:T(8,128)}, u32[]{:S(2)}) copy-start(f32[5,64,512]{2,1,0:T(8,128)} %old.3) | copy-start | bytes 1966084
  1.1 0.7 %copy-start.2 = (s32[6,256]{1,0:T(8,128)S(1)}, s32[6,256]{1,0:T(8,128)}, u32[]{:S(2)}) copy-start(s32[6,256]{1,0:T(8,128)} %nb_ref.5) | copy-start | bytes 18436
  1.8 0.7 %copy-start.4 = (s32[6,256]{1,0:T(8,128)S(1)}, s32[6,256]{1,0:T(8,128)}, u32[]{:S(2)}) copy-start(s32[6,256]{1,0:T(8,128)} %ori_ref.5) | copy-start | bytes 18436
  2.5 0.7 %copy-start.7 = (s32[33]{0:T(128)S(1)}, s32[33]{0:T(128)}, u32[]{:S(2)}) copy-start(s32[33]{0:T(128)} %start.5) | copy-start | bytes 400
  4.5 7.9 %collective-permute-start = (f32[328,128]{1,0:T(8,128)S(1)}, f32[328,128]{1,0:T(8,128)S(1)}, u32[]{:S(2)}, u32[]{:S(2)}) collective-permute-start(f32[328,128]{1,0:T(8,128)S(1)} %get-tuple-element.18), channel_id=1, source_target_pairs={{0,1},{1,0},{2,3},{3,2},{4,5},{5,4},{6,7},{7,6},{8,9},{9,8},{10,11... | collective-permute-start | bytes 503816 | tf_op jit(solution)/shard_map/ppermute | solution.py:413
  5.0 9.6 %collective-permute-start.1 = (f32[328,128]{1,0:T(8,128)S(1)}, f32[328,128]{1,0:T(8,128)S(1)}, u32[]{:S(2)}, u32[]{:S(2)}) collective-permute-start(f32[328,128]{1,0:T(8,128)S(1)} %get-tuple-element.19), channel_id=1, source_target_pairs={{0,31},{1,2},{2,1},{3,4},{4,3},{5,6},{6,5},{7,8},{8,7},{9,10},{10,... | collective-permute-start | bytes 503816 | tf_op jit(solution)/shard_map/ppermute | solution.py:412
  14.7 6.3 %copy-start.1 = (f32[64,192]{1,0:T(8,128)S(1)}, f32[64,192]{1,0:T(8,128)}, u32[]{:S(2)}) copy-start(f32[64,192]{1,0:T(8,128)} %constant.2.clone.d_ref) | copy-start | bytes 147460
  14.7 6.3 %copy-start.3 = (s32[6,256]{1,0:T(8,128)S(1)}, s32[6,256]{1,0:T(8,128)}, u32[]{:S(2)}) copy-start(s32[6,256]{1,0:T(8,128)} %nb_ref.5) | copy-start | bytes 18436
  14.7 6.3 %copy-start.5 = (s32[6,256]{1,0:T(8,128)S(1)}, s32[6,256]{1,0:T(8,128)}, u32[]{:S(2)}) copy-start(s32[6,256]{1,0:T(8,128)} %ori_ref.5) | copy-start | bytes 18436
  15.6 7.7 %collective-permute-start.3 = (f32[80,128]{1,0:T(8,128)S(1)}, f32[80,128]{1,0:T(8,128)S(1)}, u32[]{:S(2)}, u32[]{:S(2)}) collective-permute-start(f32[80,128]{1,0:T(8,128)S(1)} %get-tuple-element.22.g), channel_id=1, source_target_pairs={{0,31},{1,2},{2,1},{3,4},{4,3},{5,6},{6,5},{7,8},{8,7},{9,10},{10,... | collective-permute-start | bytes 122888 | tf_op jit(solution)/shard_map/ppermute | solution.py:412
  21.0 2.3 %collective-permute-start.2 = (f32[80,128]{1,0:T(8,128)S(1)}, f32[80,128]{1,0:T(8,128)S(1)}, u32[]{:S(2)}, u32[]{:S(2)}) collective-permute-start(f32[80,128]{1,0:T(8,128)S(1)} %get-tuple-element.22.g), channel_id=1, source_target_pairs={{0,1},{1,0},{2,3},{3,2},{4,5},{5,4},{6,7},{7,6},{8,9},{9,8},{10,11... | collective-permute-start | bytes 122888 | tf_op jit(solution)/shard_map/ppermute | solution.py:413
  21.0 0.7 %copy-start.6 = (f32[256]{0:T(256)S(1)}, f32[256]{0:T(256)}, u32[]{:S(2)}) copy-start(f32[256]{0:T(256)} %param.7) | copy-start | bytes 3076
  24.1 7.1 %collective-permute-start.5 = (f32[80,128]{1,0:T(8,128)S(1)}, f32[80,128]{1,0:T(8,128)S(1)}, u32[]{:S(2)}, u32[]{:S(2)}) collective-permute-start(f32[80,128]{1,0:T(8,128)S(1)} %get-tuple-element.26.g), channel_id=1, source_target_pairs={{0,31},{1,2},{2,1},{3,4},{4,3},{5,6},{6,5},{7,8},{8,7},{9,10},{10,... | collective-permute-start | bytes 122888 | tf_op jit(solution)/shard_map/ppermute | solution.py:412
  28.9 2.3 %collective-permute-start.4 = (f32[80,128]{1,0:T(8,128)S(1)}, f32[80,128]{1,0:T(8,128)S(1)}, u32[]{:S(2)}, u32[]{:S(2)}) collective-permute-start(f32[80,128]{1,0:T(8,128)S(1)} %get-tuple-element.26.g), channel_id=1, source_target_pairs={{0,1},{1,0},{2,3},{3,2},{4,5},{5,4},{6,7},{7,6},{8,9},{9,8},{10,11... | collective-permute-start | bytes 122888 | tf_op jit(solution)/shard_map/ppermute | solution.py:413
where the time goes:
time: 32.5 us; the launch traced here: 32.3 us
  starting transfers between devices  17.3 us (53%)
  Pallas kernels  8.07 us (25%)
  local copies, waits for them, and re-layouts  3.81 us (12%)
  waiting for transfers between devices  2.95 us (9%)
    ppermute x3, starting transfers between devices, exchange(): r_b = lax.ppermute(b, AXES, pairs_b)  16.8 us
    pallas_call x7, Pallas kernels, call(): pl.pallas_call(body, out_shape=out_shape, in_specs=specs, out_specs=jax.t...  8.07 us
    unnamed x16, local copies, waits for them, and re-layouts  3.81 us
    ppermute x3, waiting for transfers between devices, exchange(): r_b = lax.ppermute(b, AXES, pairs_b)  2.94 us
  transfers between devices with their start and end apart: 6, of which 2 were waited for; matrix products, arithmetic and copies ran while one was open for 0% of the time, Pallas kernels for 12%

commit v1 on v0

--- a/solution.py
+++ b/solution.py
@@ -60,27 +60,29 @@
     return jnp.dot(a, b, preferred_element_type=F32)
 
 
-def face_rows(ref, h, v, f):
-    base = v * NODES
+def rows_at(lead, base, f, i=None):
     if f < 2:
-        return ref[h, base + 48 * f : base + 48 * f + 16, :]
-    if f < 4:
-        first = base + 12 * (f - 2)
-        return jnp.concatenate([ref[h, first + 16 * i : first + 16 * i + 4, :] for i in range(4)], 0)
-    return ref[h, pl.ds(base + 3 * (f - 4), 16, stride=4), :]
-
-
-def add_face_rows(ref, lead, base, f, val):
-    at = (lambda r: (lead, r)) if lead is not None else (lambda r: (r,))
-    if f < 2:
-        r = at(pl.ds(base + 48 * f, 16)) + (slice(None),)
-        ref[r] = ref[r] + val
+        rows = pl.ds(base + 48 * f, 16)
     elif f < 4:
+        rows = pl.ds(base + 12 * (f - 2) + 16 * i, 4)
+    else:
+        rows = pl.ds(base + 3 * (f - 4), 16, stride=4)
+    return (rows, slice(None)) if lead is None else (lead, rows, slice(None))
+
+
+def face_rows(ref, lead, v, f):
+    if f in (2, 3):
+        return jnp.concatenate([ref[rows_at(lead, v * NODES, f, i)] for i in range(4)], 0)
+    return ref[rows_at(lead, v * NODES, f)]
+
+
+def add_face_rows(ref, lead, v, f, val):
+    if f in (2, 3):
         for i in range(4):
-            r = at(pl.ds(base + 12 * (f - 2) + 16 * i, 4)) + (slice(None),)
+            r = rows_at(lead, v * NODES, f, i)
             ref[r] = ref[r] + val[4 * i : 4 * i + 4, :]
     else:
-        r = at(pl.ds(base + 3 * (f - 4), 16, stride=4)) + (slice(None),)
+        r = rows_at(lead, v * NODES, f)
         ref[r] = ref[r] + val
 
 
@@ -88,40 +90,52 @@
     return (lax.axis_index("gx") * sizes[1] + lax.axis_index("gy")) * sizes[2] + lax.axis_index("gz")
 
 
-def send_kernel(sizes, start, old, nb_ref, ori_ref, s_a, s_b, rows_ref, col_ref, mk):
+def places(mask):
+    count = mask.shape[0]
+    upper = jnp.where(iota((EL, EL), 0) <= iota((EL, EL), 1), 1.0, 0.0).astype(BF)
+    inclusive = mm(mask.astype(BF), upper)
+    total = jnp.broadcast_to(inclusive[:, EL - 1 : EL], (count, LANES)).astype(BF)
+    r, c = iota((count, count), 0), iota((count, count), 1)
+    lower = jnp.where((c < r) & ((c >> 3) == (r >> 3)), 1.0, 0.0).astype(BF)
+    offset = mm(lower, total)[:, 0:1]
+    return jnp.where(mask > 0.5, inclusive + offset - 1.0, -1.0)
+
+
+def listed(place, values):
+    slot = iota((REMOTE, EL), 0).astype(F32)
+    accs = [jnp.zeros((REMOTE, EL), F32) for _ in values]
+    for f in range(FACES):
+        hit = place[f : f + 1, :] == slot
+        accs = [jnp.where(hit, x[f : f + 1, :], acc) for x, acc in zip(values, accs)]
+    return [jnp.sum(acc, 1, keepdims=True) for acc in accs]
+
+
+def send_kernel(sizes, start_hbm, old, nb, ori, s_a, s_b, rows_ref, col_ref, old_v, nb_v, ori_v, mk, start, sem):
     n = sizes[0] * sizes[1] * sizes[2]
+    copies = [
+        pltpu.make_async_copy(nb, nb_v, sem.at[0]),
+        pltpu.make_async_copy(ori, ori_v, sem.at[1]),
+        pltpu.make_async_copy(start_hbm, start, sem.at[2]),
+    ] + [pltpu.make_async_copy(old.at[v], old_v.at[v], sem.at[3 + v]) for v in range(VARS)]
+    for copy in copies:
+        copy.start()
     d = rank_of(sizes)
     even = (d & 1) == 0
     up = jnp.where(d + 1 == n, 0, d + 1) * EL
     down = jnp.where(d == 0, n - 1, d - 1) * EL
-    base_a = jnp.where(even, up, down)
-    base_b = jnp.where(even, down, up)
-    nb = nb_ref[...]
-    rel = [nb - base_a, nb - base_b]
     mk[...] = jnp.zeros((16, EL), F32)
+    copies[0].wait()
+    nb = nb_v[...]
+    rel = [nb - jnp.where(even, up, down), nb - jnp.where(even, down, up)]
     for k in range(2):
         mk[8 * k : 8 * k + FACES, :] = jnp.where((rel[k] >= 0) & (rel[k] < EL), 1.0, 0.0)
-    mask = mk[...]
-    upper = jnp.where(iota((EL, EL), 0) <= iota((EL, EL), 1), 1.0, 0.0).astype(BF)
-    inclusive = mm(mask.astype(BF), upper)
-    total = jnp.broadcast_to(inclusive[:, EL - 1 : EL], (16, LANES)).astype(BF)
-    r, c = iota((16, 16), 0), iota((16, 16), 1)
-    lower = jnp.where((c < r) & ((c >> 3) == (r >> 3)), 1.0, 0.0).astype(BF)
-    offset = mm(lower, total)[:, 0:1]
-    place = jnp.where(mask > 0.5, inclusive + offset - 1.0, -1.0)
+    place = places(mk[...])
+    copies[1].wait()
     face = iota((FACES, EL), 0)
-    own = (face * EL + iota((FACES, EL), 1) + 2048 * ori_ref[...]).astype(F32)
-    slot = iota((REMOTE, EL), 0).astype(F32)
+    own = (face * EL + iota((FACES, EL), 1) + 2048 * ori_v[...]).astype(F32)
     lists = []
     for k in range(2):
-        req = ((face ^ 1) * EL + rel[k]).astype(F32)
-        acc_r = jnp.zeros((REMOTE, EL), F32)
-        acc_o = jnp.zeros((REMOTE, EL), F32)
-        for f in range(FACES):
-            hit = place[8 * k + f : 8 * k + f + 1, :] == slot
-            acc_r = jnp.where(hit, req[f : f + 1, :], acc_r)
-            acc_o = jnp.where(hit, own[f : f + 1, :], acc_o)
-        lists.append((jnp.sum(acc_r, 1, keepdims=True), jnp.sum(acc_o, 1, keepdims=True)))
+        lists.append(listed(place[8 * k : 8 * k + 8, :], [((face ^ 1) * EL + rel[k]).astype(F32), own]))
     col = jnp.concatenate([lists[0][0], lists[1][0], lists[0][1], lists[1][1]], 0)
     wide = jnp.broadcast_to(col, (LANES, LANES))
     row = jnp.transpose(wide)[0:8, :]
@@ -130,23 +144,27 @@
     rows_ref[0:8, :] = code
     rows_ref[8:16, :] = turn
     col_ref[...] = wide[64:128, :]
-
+    s_a[ROWS : ROWS + 8, :] = code
+    s_b[ROWS : ROWS + 8, :] = code
+
+    copies[2].wait()
     o = start[d] - d * EL
     first = EL - o
     q, rot = first >> 7, first & 127
-    lane = iota((NODES, LANES), 1)
-    keep = lane < LANES - rot
+    keep = iota((NODES, LANES), 1) < LANES - rot
     back = (LANES - rot) & 127
     t0 = pl.ds(pl.multiple_of(q * LANES, LANES), LANES)
     t1 = pl.ds(pl.multiple_of(jnp.minimum(q + 1, 3) * LANES, LANES), LANES)
+    for copy in copies[3:]:
+        copy.wait()
 
     def put(to_up, to_down):
         for v in range(VARS):
             rows = slice(v * NODES, v * NODES + NODES)
             to_up[rows, :] = jnp.where(
-                keep, pltpu.roll(old[v, :, t0], back, 1), pltpu.roll(old[v, :, t1], back, 1)
+                keep, pltpu.roll(old_v[v, :, t0], back, 1), pltpu.roll(old_v[v, :, t1], back, 1)
             )
-            to_down[rows, :] = pltpu.roll(old[v, :, 0:LANES], o & 127, 1)
+            to_down[rows, :] = pltpu.roll(old_v[v, :, 0:LANES], o & 127, 1)
 
     @pl.when(even)
     def _():
@@ -156,11 +174,14 @@
     def _():
         put(s_b, s_a)
 
-    s_a[ROWS : ROWS + 8, :] = code
-    s_b[ROWS : ROWS + 8, :] = code
-
-
-def own_kernel(sizes, start, old, col_ref, own, ohs):
+
+def own_kernel(sizes, start, old, col_ref, d_hbm, size_hbm, own, ohs, dd, coef, d_v, size_v, sem):
+    copies = [
+        pltpu.make_async_copy(d_hbm, d_v, sem.at[0]),
+        pltpu.make_async_copy(size_hbm, size_v, sem.at[1]),
+    ]
+    for copy in copies:
+        copy.start()
     d = rank_of(sizes)
     s = d * EL - start[d]
     q, rot = s >> 7, s & 127
@@ -182,48 +203,48 @@
         hit = jnp.where((code & 255) == lane + h * LANES, 1.0, 0.0).astype(BF)
         ohs[0:64, h * LANES : h * LANES + LANES] = hit
         ohs[64:128, h * LANES : h * LANES + LANES] = jnp.zeros((64, LANES), BF)
-
-
-def requested(fld, one_hot, g):
-    acc = None
-    for f in range(FACES):
-        t = jnp.concatenate(
-            [
-                jnp.concatenate([face_rows(fld, h, v, f) for v in range(VARS)], 0)
-                for h in range(2)
-            ],
-            1,
-        )
-        part = mm(jnp.concatenate(split(t), 0), one_hot(f))
-        acc = part if acc is None else acc + part
-    g[...] = acc[0:80, :] + acc[80:160, :]
-
-
-def join_kernel(sizes, start, own, r_a, r_b, rows_ref, fld, ohg, g):
+    for copy in copies:
+        copy.wait()
+    dd[...] = jnp.concatenate(split(d_v[...]), 0)
+    coef[...] = (TIME_STEP * 2.0) / size_v[...]
+
+
+def requested(fld, hot, face, gs, g):
+    both = jnp.concatenate([fld[0], fld[1]], 1)
+    out = mm(jnp.concatenate(split(both), 0), hot)
+    gs[...] = out[0:ROWS, :] + out[ROWS : 2 * ROWS, :]
+    for v in range(VARS):
+        acc = face_rows(gs, None, v, 0)
+        for f in range(1, FACES):
+            acc = jnp.where(face == f, face_rows(gs, None, v, f), acc)
+        g[16 * v : 16 * v + 16, :] = acc
+
+
+def join_kernel(sizes, start, own, r_a, r_b, rows_ref, fld, hot_ref, code_ref, g, gs):
+    n = sizes[0] * sizes[1] * sizes[2]
     d = rank_of(sizes)
     even = (d & 1) == 0
     o = start[d] - d * EL
     u = start[d + 1] - d * EL
+    lane8 = iota((8, LANES), 1)
+    code_ref[...] = jnp.where(
+        lane8 < 32,
+        r_a[ROWS : ROWS + 8, :],
+        jnp.where(lane8 < 64, r_b[ROWS : ROWS + 8, :], rows_ref[0:8, :]),
+    )
+
     lane = iota((NODES, LANES), 1)
     for v in range(VARS):
         rows = slice(v * NODES, v * NODES + NODES)
         a, b = r_a[rows, :], r_b[rows, :]
         fld[0, rows, :] = jnp.where(lane < o, jnp.where(even, b, a), own[0, rows, :])
         fld[1, rows, :] = jnp.where(lane + LANES >= u, jnp.where(even, a, b), own[1, rows, :])
-    lane8 = iota((8, LANES), 1)
-    code = jnp.where(
-        lane8 < 32,
-        r_a[ROWS : ROWS + 8, :],
-        jnp.where(lane8 < 64, r_b[ROWS : ROWS + 8, :], rows_ref[0:8, :]),
-    ).astype(I32)
-    line = jnp.broadcast_to(code[0:1, :], (EL, LANES)) - iota((EL, LANES), 0)
-
-    def one_hot(f):
-        hot = jnp.where(line == f * EL, 1.0, 0.0).astype(BF)
-        ohg[f * EL : f * EL + EL, :] = hot
-        return hot
-
-    requested(fld, one_hot, g)
+    code = code_ref[...].astype(I32)
+    spot = jnp.broadcast_to(code[0:1, :] & 255, (EL, LANES))
+    hot = jnp.where(spot == iota((EL, LANES), 0), 1.0, 0.0).astype(BF)
+    hot_ref[...] = hot
+    face = jnp.broadcast_to(code[0:1, :] >> 8, (16, LANES))
+    requested(fld, hot, face, gs, g)
 
 
 def fluxes(u, speeds, p):
@@ -262,14 +283,14 @@
     return [jnp.where(b0, x[4 * t + s], x[4 * s + t]) for s in range(4) for t in range(4)]
 
 
-def local_kernel(sizes, last, fld, nb_ref, ori_ref, size_ref, d_ref, *rest):
+def local_kernel(sizes, last, fld, nb_ref, ori_ref, coef_ref, dd_ref, *rest):
     if last:
         old_fld, part, acc, xs, xg, xq, xo, xc, it = rest
     else:
         part, acc, xs, xg, xq, xo, xc, it = rest
     d = rank_of(sizes)
-    dh, dl = split(d_ref[...])
-    dd = jnp.concatenate([dh, dl], 0)
+    dd = dd_ref[...]
+    dh = dd[0:NODES, :]
     pieces = [[[], []] for _ in range(VARS)]
     for h in range(2):
         u = [fld[h, v * NODES : v * NODES + NODES, :] for v in range(VARS)]
@@ -326,11 +347,10 @@
         for f in range(FACES):
             for h in range(2):
                 add_face_rows(
-                    acc, h, v * NODES, f, xc[pl.ds(v * 256 + 2 * f + h, 16, stride=16), :]
+                    acc, h, v, f, xc[pl.ds(v * 256 + 2 * f + h, 16, stride=16), :]
                 )
     for h in range(2):
-        size = size_ref[0:1, h * LANES : h * LANES + LANES]
-        coef = (TIME_STEP * 2.0) / size
+        coef = coef_ref[0:1, h * LANES : h * LANES + LANES]
         for v in range(VARS):
             rows = slice(v * NODES, v * NODES + NODES)
             new = fld[h, rows, :] - coef * acc[h, rows, :]
@@ -339,11 +359,11 @@
             part[h, rows, :] = new
 
 
-def finish_kernel(last, part, g, r_a, r_b, rows_ref, ohs, size_ref, *rest):
+def finish_kernel(last, part, g, r_a, r_b, rows_ref, ohs, coef_ref, *rest):
     if last:
         out, ro, y, e = rest
     else:
-        ohg, out, g_next, ro, y, e = rest
+        hot_ref, code_ref, out, g_next, ro, y, e = rest
     lane = iota((80, LANES), 1)
     ro[0:80, :] = jnp.where(lane < 32, r_a[...], r_b[...])
     ro[80:128, :] = jnp.zeros((48, LANES), F32)
@@ -363,12 +383,12 @@
     for v in range(VARS):
         for f in range(FACES):
             add_face_rows(
-                e, None, v * NODES, f, jnp.where(live & (face == f), cor[v], 0.0)
+                e, None, v, f, jnp.where(live & (face == f), cor[v], 0.0)
             )
     spread = mm(jnp.concatenate(split(e[...]), 0), ohs[...])
-    scale = (TIME_STEP * 2.0 * LIFT) * (0.5 if last else 1.0)
+    scale = LIFT * (0.5 if last else 1.0)
     for h in range(2):
-        coef = scale / size_ref[0:1, h * LANES : h * LANES + LANES]
+        coef = scale * coef_ref[0:1, h * LANES : h * LANES + LANES]
         lanes = slice(h * LANES, h * LANES + LANES)
         for v in range(VARS):
             rows = slice(v * NODES, v * NODES + NODES)
@@ -379,15 +399,20 @@
             else:
                 out[h, rows, :] = new
     if not last:
-        requested(out, lambda f: ohg[f * EL : f * EL + EL, :], g_next)
-
-
-def call(body, out_shape, scratch, cost, *args):
+        asked = jnp.broadcast_to(code_ref[0:1, :].astype(I32) >> 8, (16, LANES))
+        requested(out, hot_ref[...], asked, e, g_next)
+
+
+def call(body, out_shape, scratch, cost, args, hbm=(), spare=None):
     spec = pl.BlockSpec(memory_space=pltpu.VMEM)
-    specs = [
-        pl.BlockSpec(memory_space=pltpu.SMEM) if a.dtype == I32 and a.ndim == 1 else spec
-        for a in args
-    ]
+    specs = []
+    for i, a in enumerate(args):
+        if i in hbm:
+            specs.append(pl.BlockSpec(memory_space=pltpu.HBM))
+        elif a.dtype == I32 and a.ndim == 1:
+            specs.append(pl.BlockSpec(memory_space=pltpu.SMEM))
+        else:
+            specs.append(spec)
     return pl.pallas_call(
         body,
         out_shape=out_shape,
@@ -396,7 +421,7 @@
         scratch_shapes=scratch,
         cost_estimate=pl.CostEstimate(flops=cost, bytes_accessed=cost, transcendentals=0),
         compiler_params=pltpu.CompilerParams(vmem_limit_bytes=32 * 1024 * 1024),
-    )(*args)
+    )(*[pltpu.with_memory_space_constraint(a, pltpu.HBM) if i in hbm else a for i, a in enumerate(args)])
 
 
 def shape(*dims, dtype=F32):
@@ -408,90 +433,95 @@
     pairs_a = [(i, i ^ 1) for i in range(n)]
     pairs_b = [(i, (i + 1) % n if i % 2 else (i - 1) % n) for i in range(n)]
 
-    def exchange(a, b):
-        r_b = lax.ppermute(b, AXES, pairs_b)
-        r_a = lax.ppermute(a, AXES, pairs_a)
-        return r_a, r_b
-
     size = element_size.reshape(1, EL)
     deriv = jnp.asarray(node_derivatives())
-    s_a, s_b, rows, col = call(
+    s_a, s_b, rows, col, old_v, nb_v, ori_v = call(
         functools.partial(send_kernel, sizes),
-        (shape(ROWS + 8, LANES), shape(ROWS + 8, LANES), shape(16, LANES), shape(64, LANES)),
-        [pltpu.VMEM((16, EL), F32)],
+        (
+            shape(ROWS + 8, LANES),
+            shape(ROWS + 8, LANES),
+            shape(16, LANES),
+            shape(64, LANES),
+            shape(*old_state.shape),
+            shape(FACES, EL, dtype=I32),
+            shape(FACES, EL, dtype=I32),
+        ),
+        [
+            pltpu.VMEM((16, EL), F32),
+            pltpu.SMEM(old_start.shape, I32),
+            pltpu.SemaphoreType.DMA((3 + VARS,)),
+        ],
         10000,
-        old_start,
-        old_state,
-        neighbour,
-        orientation,
-    )
-    r_a, r_b = exchange(s_a, s_b)
-    own, ohs = call(
+        (old_start, old_state, neighbour, orientation),
+        hbm=(0, 1, 2, 3),
+    )
+    r_a = lax.ppermute(s_a, AXES, pairs_a)
+    r_b = lax.ppermute(s_b, AXES, pairs_b)
+    own, ohs, dd, coef = call(
         functools.partial(own_kernel, sizes),
-        (shape(2, ROWS, LANES), shape(LANES, EL, dtype=BF)),
-        [],
+        (
+            shape(2, ROWS, LANES),
+            shape(LANES, EL, dtype=BF),
+            shape(2 * NODES, 3 * NODES, dtype=BF),
+            shape(1, EL),
+        ),
+        [
+            pltpu.VMEM((NODES, 3 * NODES), F32),
+            pltpu.VMEM((1, EL), F32),
+            pltpu.SemaphoreType.DMA((2,)),
+        ],
         10000,
-        old_start,
-        old_state,
-        col,
-    )
-    fld, ohg, g = call(
+        (old_start, old_v, col, deriv, size),
+        hbm=(3, 4),
+    )
+    table = pltpu.VMEM((ROWS, LANES), F32)
+    fld, hot, code, g = call(
         functools.partial(join_kernel, sizes),
-        (shape(2, ROWS, LANES), shape(FACES * EL, LANES, dtype=BF), shape(80, LANES)),
-        [],
+        (
+            shape(2, ROWS, LANES),
+            shape(EL, LANES, dtype=BF),
+            shape(8, LANES),
+            shape(80, LANES),
+        ),
+        [table],
         10000,
-        old_start,
-        own,
-        r_a,
-        r_b,
-        rows,
-    )
+        (old_start, own, r_a, r_b, rows),
+    )
+
+    def exchange(x):
+        wrap_b = pairs_b
+        r_a = lax.ppermute(x, AXES, pairs_a)
+        r_b = lax.ppermute(x, AXES, wrap_b)
+        return r_a, r_b
 
     def local(last, *args):
-        table = pltpu.VMEM((VARS * 256, LANES), F32)
+        faces = pltpu.VMEM((VARS * 256, LANES), F32)
         return call(
             functools.partial(local_kernel, sizes, last),
             shape(2, ROWS, LANES),
-            [pltpu.VMEM((2, ROWS, LANES), F32)] + [table] * 5 + [pltpu.VMEM((32, LANES), I32)],
+            [pltpu.VMEM((2, ROWS, LANES), F32)] + [faces] * 5 + [pltpu.VMEM((32, LANES), I32)],
             20000,
-            *args,
+            args,
         )
 
-    scratch = [
-        pltpu.VMEM((LANES, LANES), F32),
-        pltpu.VMEM((LANES, LANES), F32),
-        pltpu.VMEM((ROWS, LANES), F32),
-    ]
-    r_a, r_b = exchange(g, g)
-    part = local(False, fld, neighbour, orientation, size, deriv)
+    scratch = [pltpu.VMEM((LANES, LANES), F32), pltpu.VMEM((LANES, LANES), F32), table]
+    r_a, r_b = exchange(g)
+    part = local(False, fld, nb_v, ori_v, coef, dd)
     first, g2 = call(
         functools.partial(finish_kernel, False),
         (shape(2, ROWS, LANES), shape(80, LANES)),
         scratch,
         10000,
-        part,
-        g,
-        r_a,
-        r_b,
-        rows,
-        ohs,
-        size,
-        ohg,
-    )
-    r_a, r_b = exchange(g2, g2)
-    part = local(True, first, neighbour, orientation, size, deriv, fld)
+        (part, g, r_a, r_b, rows, ohs, coef, hot, code),
+    )
+    r_a, r_b = exchange(g2)
+    part = local(True, first, nb_v, ori_v, coef, dd, fld)
     return call(
         functools.partial(finish_kernel, True),
         shape(VARS, NODES, EL),
         scratch,
         10000,
-        part,
-        g2,
-        r_a,
-        r_b,
-        rows,
-        ohs,
-        size,
+        (part, g2, r_a, r_b, rows, ohs, coef),
     )
 
 

time: 32.5 us -> 28.8 us (0.89)
  local copies, waits for them, and re-layouts: 3.81 us -> 0.65 us
  waiting for transfers between devices: 2.95 us -> 1.21 us
  Pallas kernels: 8.07 us -> 8.82 us
  starting transfers between devices: 17.3 us -> 17.9 us
    unnamed x16 -> x2, local copies, waits for them, and re-layouts: 3.81 us -> 0.65 us
    ppermute x6, waiting for transfers between devices: 2.95 us -> 1.21 us  [the longest x1 0.93 us: per_device(): r_b = lax.ppermute(s_b, AXES, pairs_b)]
    pallas_call x7, Pallas kernels: 8.07 us -> 8.82 us  [call(): pl.pallas_call(body, out_shape=out_shape, in_specs=specs, out_specs=jax.t...]
    ppermute x6, starting transfers between devices: 17.3 us -> 17.9 us  [the longest x2 10.8 us: exchange(): r_b = lax.ppermute(x, AXES, wrap_b)]
  transfers between devices with their start and end apart: 6 -> 6, of which waited for: 2 -> 3; matrix products, arithmetic and copies ran while one was open for 0% -> 0% of each run, Pallas kernels for 12% -> 16%
where the time goes in v1:
time: 28.8 us; the launch traced here: 28.6 us
  starting transfers between devices  17.9 us (62%)
  Pallas kernels  8.82 us (31%)
  waiting for transfers between devices  1.21 us (4%)
  local copies, waits for them, and re-layouts  0.65 us (2%)
    ppermute x2, starting transfers between devices, exchange(): r_b = lax.ppermute(x, AXES, wrap_b)  10.8 us
    pallas_call x7, Pallas kernels, call(): pl.pallas_call(body, out_shape=out_shape, in_specs=specs, out_specs=jax.t...  8.82 us
    ppermute x1, starting transfers between devices, per_device(): r_b = lax.ppermute(s_b, AXES, pairs_b)  6.59 us
    ppermute x1, waiting for transfers between devices, per_device(): r_b = lax.ppermute(s_b, AXES, pairs_b)  0.93 us
    unnamed x2, local copies, waits for them, and re-layouts  0.65 us
  transfers between devices with their start and end apart: 6, of which 3 were waited for; matrix products, arithmetic and copies ran while one was open for 0% of the time, Pallas kernels for 16%

profile of v1, /device:TPU:0, one launch (start us, length us, event | category | flops | bytes accessed | tf_op | source)
XLA Modules:
  0.0 28.6 jit_solution(13212713484486433661)
XLA Ops:
  0.0 1.7 %shard_map.64 = (f32[328,128]{1,0:T(8,128)S(1)}, f32[328,128]{1,0:T(8,128)S(1)}, f32[16,128]{1,0:T(8,128)S(1)}, f32[64,128]{1,0:T(8,128)S(1)}, f32[5,64,512]{2,1...) custom-call(s32[33]{0:T(128)} %start.3, f32[5,64,512]{2,1,0:T(8,128)} %old.1, s32[6,256]{1,0:T(8,128)} %nb.1, ...), custom_call_target="tpu_custom_call" | custom-call | flops 10000 | bytes 10000 | tf_op jit(solution)/shard_map/pallas_call | solution.py:416
  1.7 0.5 %collective-permute-start = (f32[328,128]{1,0:T(8,128)S(1)}, f32[328,128]{1,0:T(8,128)S(1)}, u32[]{:S(2)}, u32[]{:S(2)}) collective-permute-start(f32[328,128]{1,0:T(8,128)S(1)} %get-tuple-element.25), channel_id=1, source_target_pairs={{0,1},{1,0},{2,3},{3,2},{4,5},{5,4},{6,7},{7,6},{8,9},{9,8},{10,11... | collective-permute-start | bytes 503816 | tf_op jit(solution)/shard_map/ppermute | solution.py:458
  2.2 6.6 %collective-permute-start.1 = (f32[328,128]{1,0:T(8,128)S(1)}, f32[328,128]{1,0:T(8,128)S(1)}, u32[]{:S(2)}, u32[]{:S(2)}) collective-permute-start(f32[328,128]{1,0:T(8,128)S(1)} %get-tuple-element.26), channel_id=1, source_target_pairs={{0,31},{1,2},{2,1},{3,4},{4,3},{5,6},{6,5},{7,8},{8,7},{9,10},{10,... | collective-permute-start | bytes 503816 | tf_op jit(solution)/shard_map/ppermute | solution.py:459
  8.8 0.0 copy-start
  8.8 0.7 %copy-done = s32[33]{0:T(128)S(1)} copy-done((s32[33]{0:T(128)S(1)}, s32[33]{0:T(128)}, u32[]{:S(2)}) %copy-start) | copy-done | bytes 156
  9.4 1.4 %shard_map.65 = (f32[2,320,128]{2,1,0:T(8,128)S(1)}, bf16[128,256]{1,0:T(8,128)(2,1)S(1)}, bf16[128,192]{1,0:T(8,128)(2,1)S(1)}, f32[1,256]{1,0:T(1,128)S(1)}) custom-call(s32[33]{0:T(128)S(1)} %copy-done, f32[5,64,512]{2,1,0:T(8,128)S(1)} %get-tuple-element.22.old, f32[64,128]{1,0:T(8,128)S(1)} %get-tuple-element.23.col_ref, ...), custom_call_target="tpu_custom_call" | custom-call | flops 10000 | bytes 10000 | tf_op jit(solution)/shard_map/pallas_call | solution.py:416
  10.9 0.0 collective-permute-done.r_a
  10.9 0.9 %collective-permute-done.1.r_b = f32[328,128]{1,0:T(8,128)S(1)} collective-permute-done((f32[328,128]{1,0:T(8,128)S(1)}, f32[328,128]{1,0:T(8,128)S(1)}, u32[]{:S(2)}, u32[]{:S(2)}) %collective-permute-start.1) | collective-permute-done | bytes 167968 | tf_op jit(solution)/shard_map/ppermute | solution.py:459
  11.8 0.8 %shard_map.66 = (f32[2,320,128]{2,1,0:T(8,128)S(1)}, bf16[256,128]{1,0:T(8,128)(2,1)S(1)}, f32[8,128]{1,0:T(8,128)S(1)}, f32[80,128]{1,0:T(8,128)S(1)}) custom-call(s32[33]{0:T(128)S(1)} %copy-done, f32[2,320,128]{2,1,0:T(8,128)S(1)} %get-tuple-element.24.own, f32[328,128]{1,0:T(8,128)S(1)} %collective-permute-done.r_a, ...), custom_call_target="tpu_custom_call" | custom-call | flops 10000 | bytes 10000 | tf_op jit(solution)/shard_map/pallas_call | solution.py:416
  12.7 5.4 %collective-permute-start.3 = (f32[80,128]{1,0:T(8,128)S(1)}, f32[80,128]{1,0:T(8,128)S(1)}, u32[]{:S(2)}, u32[]{:S(2)}) collective-permute-start(f32[80,128]{1,0:T(8,128)S(1)} %get-tuple-element.33.g), channel_id=1, source_target_pairs={{0,31},{1,2},{2,1},{3,4},{4,3},{5,6},{6,5},{7,8},{8,7},{9,10},{10,... | collective-permute-start | bytes 122888 | tf_op jit(solution)/shard_map/ppermute | solution.py:494
  18.1 0.0 collective-permute-start.2
  18.1 1.5 %shard_map.67.part = f32[2,320,128]{2,1,0:T(8,128)S(1)} custom-call(f32[2,320,128]{2,1,0:T(8,128)S(1)} %get-tuple-element.28.fld.rest_0_, s32[6,256]{1,0:T(8,128)S(1)} %get-tuple-element.29.nb_ref, s32[6,256]{1,0:T(8,128)S(1)} %get-tuple-element.30.ori_ref, f32[1,256]{1,0:T(1,128)S(1)} %get-tuple-element.31.coef_ref, ...), custom_call_target="tpu_custom_call" | custom-call | flops 20000 | bytes 20000 | tf_op jit(solution)/shard_map/pallas_call | solution.py:416
  19.6 0.2 collective-permute-done.3.r_b
  19.8 0.0 collective-permute-done.2.r_a
  19.8 0.7 %shard_map.68 = (f32[2,320,128]{2,1,0:T(8,128)S(1)}, f32[80,128]{1,0:T(8,128)S(1)}) custom-call(f32[2,320,128]{2,1,0:T(8,128)S(1)} %shard_map.67.part, f32[80,128]{1,0:T(8,128)S(1)} %get-tuple-element.33.g, f32[80,128]{1,0:T(8,128)S(1)} %collective-permute-done.2.r_a, f32[80,128]{1,0:T(8,128)S(1)} %collective-permute-done.3.r_b, ...), custom_call_target="tpu_custom_call" | custom-call | flops 10000 | bytes 10000 | tf_op jit(solution)/shard_map/pallas_call | solution.py:416
  20.5 5.4 %collective-permute-start.5 = (f32[80,128]{1,0:T(8,128)S(1)}, f32[80,128]{1,0:T(8,128)S(1)}, u32[]{:S(2)}, u32[]{:S(2)}) collective-permute-start(f32[80,128]{1,0:T(8,128)S(1)} %get-tuple-element.38.g), channel_id=1, source_target_pairs={{0,31},{1,2},{2,1},{3,4},{4,3},{5,6},{6,5},{7,8},{8,7},{9,10},{10,... | collective-permute-start | bytes 122888 | tf_op jit(solution)/shard_map/ppermute | solution.py:494
  25.8 0.0 collective-permute-start.4
  25.8 1.6 %shard_map.69.part = f32[2,320,128]{2,1,0:T(8,128)S(1)} custom-call(f32[2,320,128]{2,1,0:T(8,128)S(1)} %get-tuple-element.37.fld, s32[6,256]{1,0:T(8,128)S(1)} %get-tuple-element.29.nb_ref, s32[6,256]{1,0:T(8,128)S(1)} %get-tuple-element.30.ori_ref, f32[1,256]{1,0:T(1,128)S(1)} %get-tuple-element.31.coef_ref, bf16[128,192]{1,0:T(8,128)(2,1)S(1)} %get-tuple-element.32.dd_ref, ...), custom_call_target="tpu_custom_call" | custom-call | flops 20000 | bytes 20000 | tf_op jit(solution)/shard_map/pallas_call | solution.py:416
  27.4 0.1 collective-permute-done.5.r_b
  27.5 0.0 collective-permute-done.4.r_a
  27.6 1.1 %shard_map.70 = f32[5,64,256]{2,1,0:T(8,128)} custom-call(f32[2,320,128]{2,1,0:T(8,128)S(1)} %shard_map.69.part, f32[80,128]{1,0:T(8,128)S(1)} %get-tuple-element.38.g, f32[80,128]{1,0:T(8,128)S(1)} %collective-permute-done.4.r_a, f32[80,128]{1,0:T(8,128)S(1)} %collective-permute-done.5.r_b, f32[16,128]{1,0:T(8,128)S(1)} %get-tuple-element.27.rows_ref, ...), custom_call_target="tpu_custom_call" | custom-call | flops 10000 | bytes 10000 | tf_op jit(solution)/shard_map/pallas_call | solution.py:416
Async XLA Ops:
  1.7 9.2 %collective-permute-start = (f32[328,128]{1,0:T(8,128)S(1)}, f32[328,128]{1,0:T(8,128)S(1)}, u32[]{:S(2)}, u32[]{:S(2)}) collective-permute-start(f32[328,128]{1,0:T(8,128)S(1)} %get-tuple-element.25), channel_id=1, source_target_pairs={{0,1},{1,0},{2,3},{3,2},{4,5},{5,4},{6,7},{7,6},{8,9},{9,8},{10,11... | collective-permute-start | bytes 503816 | tf_op jit(solution)/shard_map/ppermute | solution.py:458
  2.2 9.6 %collective-permute-start.1 = (f32[328,128]{1,0:T(8,128)S(1)}, f32[328,128]{1,0:T(8,128)S(1)}, u32[]{:S(2)}, u32[]{:S(2)}) collective-permute-start(f32[328,128]{1,0:T(8,128)S(1)} %get-tuple-element.26), channel_id=1, source_target_pairs={{0,31},{1,2},{2,1},{3,4},{4,3},{5,6},{6,5},{7,8},{8,7},{9,10},{10,... | collective-permute-start | bytes 503816 | tf_op jit(solution)/shard_map/ppermute | solution.py:459
  8.8 0.7 %copy-start = (s32[33]{0:T(128)S(1)}, s32[33]{0:T(128)}, u32[]{:S(2)}) copy-start(s32[33]{0:T(128)} %start.3) | copy-start | bytes 400
  12.7 7.1 %collective-permute-start.3 = (f32[80,128]{1,0:T(8,128)S(1)}, f32[80,128]{1,0:T(8,128)S(1)}, u32[]{:S(2)}, u32[]{:S(2)}) collective-permute-start(f32[80,128]{1,0:T(8,128)S(1)} %get-tuple-element.33.g), channel_id=1, source_target_pairs={{0,31},{1,2},{2,1},{3,4},{4,3},{5,6},{6,5},{7,8},{8,7},{9,10},{10,... | collective-permute-start | bytes 122888 | tf_op jit(solution)/shard_map/ppermute | solution.py:494
  18.1 1.7 %collective-permute-start.2 = (f32[80,128]{1,0:T(8,128)S(1)}, f32[80,128]{1,0:T(8,128)S(1)}, u32[]{:S(2)}, u32[]{:S(2)}) collective-permute-start(f32[80,128]{1,0:T(8,128)S(1)} %get-tuple-element.33.g), channel_id=1, source_target_pairs={{0,1},{1,0},{2,3},{3,2},{4,5},{5,4},{6,7},{7,6},{8,9},{9,8},{10,11... | collective-permute-start | bytes 122888 | tf_op jit(solution)/shard_map/ppermute | solution.py:493
  20.5 7.1 %collective-permute-start.5 = (f32[80,128]{1,0:T(8,128)S(1)}, f32[80,128]{1,0:T(8,128)S(1)}, u32[]{:S(2)}, u32[]{:S(2)}) collective-permute-start(f32[80,128]{1,0:T(8,128)S(1)} %get-tuple-element.38.g), channel_id=1, source_target_pairs={{0,31},{1,2},{2,1},{3,4},{4,3},{5,6},{6,5},{7,8},{8,7},{9,10},{10,... | collective-permute-start | bytes 122888 | tf_op jit(solution)/shard_map/ppermute | solution.py:494
  25.8 1.7 %collective-permute-start.4 = (f32[80,128]{1,0:T(8,128)S(1)}, f32[80,128]{1,0:T(8,128)S(1)}, u32[]{:S(2)}, u32[]{:S(2)}) collective-permute-start(f32[80,128]{1,0:T(8,128)S(1)} %get-tuple-element.38.g), channel_id=1, source_target_pairs={{0,1},{1,0},{2,3},{3,2},{4,5},{5,4},{6,7},{7,6},{8,9},{9,8},{10,11... | collective-permute-start | bytes 122888 | tf_op jit(solution)/shard_map/ppermute | solution.py:493

commit v2 on v1

--- a/solution.py
+++ b/solution.py
@@ -110,7 +110,7 @@
     return [jnp.sum(acc, 1, keepdims=True) for acc in accs]
 
 
-def send_kernel(sizes, start_hbm, old, nb, ori, s_a, s_b, rows_ref, col_ref, old_v, nb_v, ori_v, mk, start, sem):
+def send_kernel(sizes, start_hbm, old, nb, ori, s_a, s_b, rows_ref, col_ref, old_v, nb_v, ori_v, edge, mk, start, sem):
     n = sizes[0] * sizes[1] * sizes[2]
     copies = [
         pltpu.make_async_copy(nb, nb_v, sem.at[0]),
@@ -144,11 +144,14 @@
     rows_ref[0:8, :] = code
     rows_ref[8:16, :] = turn
     col_ref[...] = wide[64:128, :]
-    s_a[ROWS : ROWS + 8, :] = code
-    s_b[ROWS : ROWS + 8, :] = code
+    for out in (s_a, s_b):
+        out[ROWS : ROWS + 8, :] = code
+        out[ROWS + 8 : ROWS + 16, :] = turn
 
     copies[2].wait()
     o = start[d] - d * EL
+    edge[0:4, :] = jnp.broadcast_to(o, (4, LANES))
+    edge[4:8, :] = jnp.broadcast_to(start[d + 1] - d * EL, (4, LANES))
     first = EL - o
     q, rot = first >> 7, first & 127
     keep = iota((NODES, LANES), 1) < LANES - rot
@@ -175,14 +178,18 @@
         put(s_b, s_a)
 
 
-def own_kernel(sizes, start, old, col_ref, d_hbm, size_hbm, own, ohs, dd, coef, d_v, size_v, sem):
+def own_kernel(
+    sizes, start_hbm, old, col_ref, d_hbm, size_hbm, own, ohs, dd, coef, d_v, size_v, start, sem
+):
     copies = [
+        pltpu.make_async_copy(start_hbm, start, sem.at[2]),
         pltpu.make_async_copy(d_hbm, d_v, sem.at[0]),
         pltpu.make_async_copy(size_hbm, size_v, sem.at[1]),
     ]
     for copy in copies:
         copy.start()
     d = rank_of(sizes)
+    copies[0].wait()
     s = d * EL - start[d]
     q, rot = s >> 7, s & 127
     keep = iota((NODES, LANES), 1) < LANES - rot
@@ -203,10 +210,17 @@
         hit = jnp.where((code & 255) == lane + h * LANES, 1.0, 0.0).astype(BF)
         ohs[0:64, h * LANES : h * LANES + LANES] = hit
         ohs[64:128, h * LANES : h * LANES + LANES] = jnp.zeros((64, LANES), BF)
-    for copy in copies:
+    for copy in copies[1:]:
         copy.wait()
     dd[...] = jnp.concatenate(split(d_v[...]), 0)
     coef[...] = (TIME_STEP * 2.0) / size_v[...]
+
+
+def chosen(gs, face, v):
+    acc = face_rows(gs, None, v, 0)
+    for f in range(1, FACES):
+        acc = jnp.where(face == f, face_rows(gs, None, v, f), acc)
+    return acc
 
 
 def requested(fld, hot, face, gs, g):
@@ -214,32 +228,30 @@
     out = mm(jnp.concatenate(split(both), 0), hot)
     gs[...] = out[0:ROWS, :] + out[ROWS : 2 * ROWS, :]
     for v in range(VARS):
-        acc = face_rows(gs, None, v, 0)
-        for f in range(1, FACES):
-            acc = jnp.where(face == f, face_rows(gs, None, v, f), acc)
-        g[16 * v : 16 * v + 16, :] = acc
-
-
-def join_kernel(sizes, start, own, r_a, r_b, rows_ref, fld, hot_ref, code_ref, g, gs):
-    n = sizes[0] * sizes[1] * sizes[2]
-    d = rank_of(sizes)
-    even = (d & 1) == 0
-    o = start[d] - d * EL
-    u = start[d + 1] - d * EL
+        g[16 * v : 16 * v + 16, :] = chosen(gs, face, v)
+
+
+def join_kernel(sizes, own, r_a, r_b, rows_ref, edge, fld, hot_ref, code_ref, info, g, gs):
+    even = (rank_of(sizes) & 1) == 0
+    lane = iota((NODES, LANES), 1)
+    below = lane < edge[0:1, :]
+    above = lane + LANES >= edge[4:5, :]
+    for v in range(VARS):
+        rows = slice(v * NODES, v * NODES + NODES)
+        a, b = r_a[rows, :], r_b[rows, :]
+        fld[0, rows, :] = jnp.where(below, jnp.where(even, b, a), own[0, rows, :])
+        fld[1, rows, :] = jnp.where(above, jnp.where(even, a, b), own[1, rows, :])
     lane8 = iota((8, LANES), 1)
-    code_ref[...] = jnp.where(
+    code = jnp.where(
         lane8 < 32,
         r_a[ROWS : ROWS + 8, :],
         jnp.where(lane8 < 64, r_b[ROWS : ROWS + 8, :], rows_ref[0:8, :]),
-    )
-
-    lane = iota((NODES, LANES), 1)
-    for v in range(VARS):
-        rows = slice(v * NODES, v * NODES + NODES)
-        a, b = r_a[rows, :], r_b[rows, :]
-        fld[0, rows, :] = jnp.where(lane < o, jnp.where(even, b, a), own[0, rows, :])
-        fld[1, rows, :] = jnp.where(lane + LANES >= u, jnp.where(even, a, b), own[1, rows, :])
-    code = code_ref[...].astype(I32)
+    ).astype(I32)
+    code_ref[...] = code
+    lane16 = iota((16, LANES), 1)
+    info[...] = jnp.where(
+        lane16 < 96, pltpu.roll(rows_ref[...], 64, 1), r_b[ROWS : ROWS + 16, :]
+    ).astype(I32)
     spot = jnp.broadcast_to(code[0:1, :] & 255, (EL, LANES))
     hot = jnp.where(spot == iota((EL, LANES), 0), 1.0, 0.0).astype(BF)
     hot_ref[...] = hot
@@ -359,48 +371,100 @@
             part[h, rows, :] = new
 
 
-def finish_kernel(last, part, g, r_a, r_b, rows_ref, ohs, coef_ref, *rest):
-    if last:
-        out, ro, y, e = rest
-    else:
-        hot_ref, code_ref, out, g_next, ro, y, e = rest
-    lane = iota((80, LANES), 1)
-    ro[0:80, :] = jnp.where(lane < 32, r_a[...], r_b[...])
+def face_terms(inner, outer, info, live, ro, y, e):
+    ro[0:80, :] = outer
     ro[80:128, :] = jnp.zeros((48, LANES), F32)
-    code = pltpu.roll(rows_ref[0:8, :], 64, 1).astype(I32)
-    turn = pltpu.roll(rows_ref[8:16, :], 64, 1).astype(I32)
+    turn = info[8:16, :]
     x = [ro[pl.ds(m, 8, stride=16), :] for m in range(16)]
     for m, val in enumerate(turned(x, (turn & 1) != 0, (turn & 2) != 0, (turn & 4) != 0)):
         y[8 * m : 8 * m + 8, :] = val
-    live = iota((16, LANES), 1) < 64
-    face = jnp.where(live, jnp.broadcast_to(code[0:1, :], (16, LANES)) >> 8, 0)
+    face = jnp.where(live, jnp.broadcast_to(info[0:1, :], (16, LANES)) >> 8, -1)
     axis_is = (face < 2, (face >= 2) & (face < 4))
     half_sign = jnp.where((face & 1) != 0, 0.5, -0.5)
-    inner = [pltpu.roll(g[16 * v : 16 * v + 16, :], 64, 1) for v in range(VARS)]
-    outer = [y[pl.ds(v, 16, stride=8), :] for v in range(VARS)]
-    cor = correction(inner, outer, axis_is, half_sign)
+    behind = [y[pl.ds(v, 16, stride=8), :] for v in range(VARS)]
+    here = [inner[16 * v : 16 * v + 16, :] for v in range(VARS)]
+    cor = correction(here, behind, axis_is, half_sign)
     e[...] = jnp.zeros((ROWS, LANES), F32)
     for v in range(VARS):
         for f in range(FACES):
-            add_face_rows(
-                e, None, v, f, jnp.where(live & (face == f), cor[v], 0.0)
-            )
-    spread = mm(jnp.concatenate(split(e[...]), 0), ohs[...])
-    scale = LIFT * (0.5 if last else 1.0)
+            add_face_rows(e, None, v, f, jnp.where(face == f, cor[v], 0.0))
+
+
+def added(part, spread, coef_ref, scale, put):
     for h in range(2):
-        coef = scale * coef_ref[0:1, h * LANES : h * LANES + LANES]
         lanes = slice(h * LANES, h * LANES + LANES)
+        coef = scale * coef_ref[0:1, lanes]
         for v in range(VARS):
             rows = slice(v * NODES, v * NODES + NODES)
             low = slice(ROWS + v * NODES, ROWS + v * NODES + NODES)
-            new = part[h, rows, :] - coef * (spread[rows, lanes] + spread[low, lanes])
-            if last:
-                out[v, :, lanes] = new
-            else:
-                out[h, rows, :] = new
-    if not last:
-        asked = jnp.broadcast_to(code_ref[0:1, :].astype(I32) >> 8, (16, LANES))
-        requested(out, hot_ref[...], asked, e, g_next)
+            put(h, v, part[h, rows, :] - coef * (spread[rows, lanes] + spread[low, lanes]))
+
+
+def near_kernel(part, g, r_a, info, ohs, coef_ref, hot_ref, code_ref, fp, pb, ro, y, e, g1):
+    lane = iota((16, LANES), 1)
+    face_terms(pltpu.roll(g[...], 64, 1), r_a[...], info, lane < 32, ro, y, e)
+    spread = mm(jnp.concatenate(split(e[...]), 0), ohs[...])
+
+    def put(h, v, new):
+        fp[h, v * NODES : v * NODES + NODES, :] = new
+
+    added(part, spread, coef_ref, LIFT, put)
+    hot = hot_ref[...]
+    asked = jnp.broadcast_to(code_ref[0:1, :] >> 8, (16, LANES))
+    requested(fp, hot, asked, e, g1)
+    lane = iota((80, LANES), 1)
+    pb[0:80, :] = jnp.where(lane < 32, pltpu.roll(g1[...], 96, 1), g[...])
+    ch, cl = split(jnp.broadcast_to(LIFT * coef_ref[0:1, :], (16, EL)))
+    pb[80:96, :] = mm(ch, hot) + mm(cl, hot)
+
+
+def pair_kernel(info, rows_ref, after, pairs):
+    theirs = jnp.transpose(jnp.broadcast_to(info[0:1, :].astype(F32), (LANES, LANES))).astype(I32)
+    mine = jnp.broadcast_to(rows_ref[0:1, :].astype(I32), (LANES, LANES))
+    row, lane = iota((LANES, LANES), 0), iota((LANES, LANES), 1)
+    on = ((theirs & 255) == (mine & 255)) & (row >= 96) & (lane >= 32) & (lane < 64)
+    pairs[...] = jnp.where(on, 1.0, 0.0).astype(BF)
+
+
+def far_kernel(
+    fp, g, r_b, info, rows_ref, ohs, pairs, coef_ref, hot_ref, code_ref, first, g1, o1, ro, y, e
+):
+    lane = iota((80, LANES), 1)
+    mine = pltpu.roll(g[...], 64, 1)
+    got = r_b[0:80, :]
+    lane16 = iota((16, LANES), 1)
+    live = ((lane16 >= 32) & (lane16 < 64)) | (lane16 >= 96)
+    face_terms(
+        jnp.where(lane < 64, mine, got), jnp.where(lane < 64, got, mine), info, live, ro, y, e
+    )
+    parts = jnp.concatenate(split(e[...]), 0)
+    spread = mm(parts, ohs[...])
+
+    def put(h, v, new):
+        first[h, v * NODES : v * NODES + NODES, :] = new
+
+    added(fp, spread, coef_ref, LIFT, put)
+    theirs = mm(parts, pairs[...])
+    e[...] = theirs[0:ROWS, :] + theirs[ROWS : 2 * ROWS, :]
+    face = jnp.broadcast_to(rows_ref[0:1, :].astype(I32) >> 8, (16, LANES))
+    coef = r_b[80:81, :]
+    for v in range(VARS):
+        rows = slice(16 * v, 16 * v + 16)
+        o1[rows, :] = pltpu.roll(r_b[rows, :], 32, 1) - coef * chosen(e, face, v)
+    asked = jnp.broadcast_to(code_ref[0:1, :] >> 8, (16, LANES))
+    requested(first, hot_ref[...], asked, e, g1)
+
+
+def last_kernel(part, g1, r_a, o1, info, ohs, coef_ref, out, ro, y, e):
+    lane = iota((80, LANES), 1)
+    outer = jnp.where(lane < 32, r_a[...], o1[...])
+    face_terms(pltpu.roll(g1[...], 64, 1), outer, info, iota((16, LANES), 1) < 64, ro, y, e)
+    spread = mm(jnp.concatenate(split(e[...]), 0), ohs[...])
+
+    def put(h, v, new):
+        out[v, :, h * LANES : h * LANES + LANES] = new
+
+    added(part, spread, coef_ref, 0.5 * LIFT, put)
 
 
 def call(body, out_shape, scratch, cost, args, hbm=(), spare=None):
@@ -435,16 +499,17 @@
 
     size = element_size.reshape(1, EL)
     deriv = jnp.asarray(node_derivatives())
-    s_a, s_b, rows, col, old_v, nb_v, ori_v = call(
+    s_a, s_b, rows, col, old_v, nb_v, ori_v, edge = call(
         functools.partial(send_kernel, sizes),
         (
-            shape(ROWS + 8, LANES),
-            shape(ROWS + 8, LANES),
+            shape(ROWS + 16, LANES),
+            shape(ROWS + 16, LANES),
             shape(16, LANES),
             shape(64, LANES),
             shape(*old_state.shape),
             shape(FACES, EL, dtype=I32),
             shape(FACES, EL, dtype=I32),
+            shape(8, LANES, dtype=I32),
         ),
         [
             pltpu.VMEM((16, EL), F32),
@@ -468,60 +533,67 @@
         [
             pltpu.VMEM((NODES, 3 * NODES), F32),
             pltpu.VMEM((1, EL), F32),
-            pltpu.SemaphoreType.DMA((2,)),
+            pltpu.SMEM(old_start.shape, I32),
+            pltpu.SemaphoreType.DMA((3,)),
         ],
         10000,
         (old_start, old_v, col, deriv, size),
-        hbm=(3, 4),
+        hbm=(0, 3, 4),
     )
     table = pltpu.VMEM((ROWS, LANES), F32)
-    fld, hot, code, g = call(
+    square = pltpu.VMEM((LANES, LANES), F32)
+    traces = shape(80, LANES)
+    state = shape(2, ROWS, LANES)
+    fld, hot, code, info, g = call(
         functools.partial(join_kernel, sizes),
         (
-            shape(2, ROWS, LANES),
+            state,
             shape(EL, LANES, dtype=BF),
-            shape(8, LANES),
-            shape(80, LANES),
+            shape(8, LANES, dtype=I32),
+            shape(16, LANES, dtype=I32),
+            traces,
         ),
         [table],
         10000,
-        (old_start, own, r_a, r_b, rows),
-    )
-
-    def exchange(x):
-        wrap_b = pairs_b
-        r_a = lax.ppermute(x, AXES, pairs_a)
-        r_b = lax.ppermute(x, AXES, wrap_b)
-        return r_a, r_b
+        (own, r_a, r_b, rows, edge),
+    )
 
     def local(last, *args):
         faces = pltpu.VMEM((VARS * 256, LANES), F32)
         return call(
             functools.partial(local_kernel, sizes, last),
-            shape(2, ROWS, LANES),
+            state,
             [pltpu.VMEM((2, ROWS, LANES), F32)] + [faces] * 5 + [pltpu.VMEM((32, LANES), I32)],
             20000,
             args,
         )
 
-    scratch = [pltpu.VMEM((LANES, LANES), F32), pltpu.VMEM((LANES, LANES), F32), table]
-    r_a, r_b = exchange(g)
+    r_a = lax.ppermute(g, AXES, pairs_a)
     part = local(False, fld, nb_v, ori_v, coef, dd)
-    first, g2 = call(
-        functools.partial(finish_kernel, False),
-        (shape(2, ROWS, LANES), shape(80, LANES)),
-        scratch,
+    fp, pb = call(
+        near_kernel,
+        (state, shape(96, LANES)),
+        [square, square, table, pltpu.VMEM((80, LANES), F32)],
         10000,
-        (part, g, r_a, r_b, rows, ohs, coef, hot, code),
-    )
-    r_a, r_b = exchange(g2)
+        (part, g, r_a, info, ohs, coef, hot, code),
+    )
+    r_b = lax.ppermute(pb, AXES, pairs_b)
+    pairs = call(pair_kernel, shape(LANES, LANES, dtype=BF), [], 10000, (info, rows, fp))
+    first, g1, o1 = call(
+        far_kernel,
+        (state, traces, traces),
+        [square, square, table],
+        10000,
+        (fp, g, r_b, info, rows, ohs, pairs, coef, hot, code),
+    )
+    r_a = lax.ppermute(g1, AXES, pairs_a)
     part = local(True, first, nb_v, ori_v, coef, dd, fld)
     return call(
-        functools.partial(finish_kernel, True),
+        last_kernel,
         shape(VARS, NODES, EL),
-        scratch,
+        [square, square, table],
         10000,
-        (part, g2, r_a, r_b, rows, ohs, coef),
+        (part, g1, r_a, o1, info, ohs, coef),
     )
 
 

time: 28.8 us -> 25.4 us (0.88)
  starting transfers between devices: 17.9 us -> 12.6 us
  waiting for transfers between devices: 1.21 us -> 3.84 us
  local copies, waits for them, and re-layouts: 0.65 us -> 0 us
    ppermute x4 -> x3, starting transfers between devices: 10.8 us -> 5.5 us  [the longest x1 5.36 us: per_device(): r_b = lax.ppermute(pb, AXES, pairs_b)]
    ppermute x4 -> x3, waiting for transfers between devices: 0.27 us -> 1.67 us  [the longest x1 1.67 us: per_device(): r_b = lax.ppermute(pb, AXES, pairs_b)]
    ppermute x1, waiting for transfers between devices: 0.93 us -> 2.16 us  [per_device(): r_b = lax.ppermute(s_b, AXES, pairs_b)]
    unnamed x2 -> x0, local copies, waits for them, and re-layouts: 0.65 us -> none
    pallas_call x7 -> x9, Pallas kernels: 8.82 us -> 8.63 us  [call(): pl.pallas_call(body, out_shape=out_shape, in_specs=specs, out_specs=jax.t...]
  transfers between devices with their start and end apart: 6 -> 5, of which waited for: 3 -> 2; matrix products, arithmetic and copies ran while one was open for 0% -> 0% of each run, Pallas kernels for 16% -> 16%
where the time goes in v2:
time: 25.4 us; the launch traced here: 25.2 us
  starting transfers between devices  12.6 us (50%)
  Pallas kernels  8.63 us (34%)
  waiting for transfers between devices  3.84 us (15%)
    pallas_call x9, Pallas kernels, call(): pl.pallas_call(body, out_shape=out_shape, in_specs=specs, out_specs=jax.t...  8.63 us
    ppermute x1, starting transfers between devices, per_device(): r_b = lax.ppermute(s_b, AXES, pairs_b)  6.59 us
    ppermute x1, starting transfers between devices, per_device(): r_b = lax.ppermute(pb, AXES, pairs_b)  5.36 us
    ppermute x1, waiting for transfers between devices, per_device(): r_b = lax.ppermute(s_b, AXES, pairs_b)  2.16 us
    ppermute x1, waiting for transfers between devices, per_device(): r_b = lax.ppermute(pb, AXES, pairs_b)  1.67 us
    ppermute x1, starting transfers between devices, per_device(): r_a = lax.ppermute(s_a, AXES, pairs_a)  0.52 us
  transfers between devices with their start and end apart: 5, of which 2 were waited for; matrix products, arithmetic and copies ran while one was open for 0% of the time, Pallas kernels for 16%

profile of v2, /device:TPU:0, one launch (start us, length us, event | category | flops | bytes accessed | tf_op | source)
XLA Modules:
  0.0 25.2 jit_solution(17554465029438664720)
XLA Ops:
  0.0 1.7 %shard_map.64 = (f32[336,128]{1,0:T(8,128)S(1)}, f32[336,128]{1,0:T(8,128)S(1)}, f32[16,128]{1,0:T(8,128)S(1)}, f32[64,128]{1,0:T(8,128)S(1)}, f32[5,64,512]{2,1...) custom-call(s32[33]{0:T(128)} %start_hbm.3, f32[5,64,512]{2,1,0:T(8,128)} %old.1, ...), custom_call_target="tpu_custom_call" | custom-call | flops 10000 | bytes 10000 | tf_op jit(solution)/shard_map/pallas_call | solution.py:480
  1.7 0.5 %collective-permute-start = (f32[336,128]{1,0:T(8,128)S(1)}, f32[336,128]{1,0:T(8,128)S(1)}, u32[]{:S(2)}, u32[]{:S(2)}) collective-permute-start(f32[336,128]{1,0:T(8,128)S(1)} %get-tuple-element.30), channel_id=1, source_target_pairs={{0,1},{1,0},{2,3},{3,2},{4,5},{5,4},{6,7},{7,6},{8,9},{9,8},{10,11... | collective-permute-start | bytes 516104 | tf_op jit(solution)/shard_map/ppermute | solution.py:523
  2.2 6.6 %collective-permute-start.1 = (f32[336,128]{1,0:T(8,128)S(1)}, f32[336,128]{1,0:T(8,128)S(1)}, u32[]{:S(2)}, u32[]{:S(2)}) collective-permute-start(f32[336,128]{1,0:T(8,128)S(1)} %get-tuple-element.31), channel_id=1, source_target_pairs={{0,31},{1,2},{2,1},{3,4},{4,3},{5,6},{6,5},{7,8},{8,7},{9,10},{10,... | collective-permute-start | bytes 516104 | tf_op jit(solution)/shard_map/ppermute | solution.py:524
  8.8 0.9 %shard_map.65 = (f32[2,320,128]{2,1,0:T(8,128)S(1)}, bf16[128,256]{1,0:T(8,128)(2,1)S(1)}, bf16[128,192]{1,0:T(8,128)(2,1)S(1)}, f32[1,256]{1,0:T(1,128)S(1)}) custom-call(s32[33]{0:T(128)} %start_hbm.3, f32[5,64,512]{2,1,0:T(8,128)S(1)} %get-tuple-element.27.old, f32[64,128]{1,0:T(8,128)S(1)} %get-tuple-element.28.col_ref, f32[64,192]{1,0:T(8,128)} %constant.2.clone.d_hbm, ...), custom_call_target="tpu_custom_call" | custom-call | flops 10000 | bytes 10000 | tf_op jit(solution)/shard_map/pallas_call | solution.py:480
  9.7 0.0 collective-permute-done.r_a
  9.7 2.2 %collective-permute-done.1.r_b = f32[336,128]{1,0:T(8,128)S(1)} collective-permute-done((f32[336,128]{1,0:T(8,128)S(1)}, f32[336,128]{1,0:T(8,128)S(1)}, u32[]{:S(2)}, u32[]{:S(2)}) %collective-permute-start.1) | collective-permute-done | bytes 172064 | tf_op jit(solution)/shard_map/ppermute | solution.py:524
  11.9 0.3 %shard_map.66 = (f32[2,320,128]{2,1,0:T(8,128)S(1)}, bf16[256,128]{1,0:T(8,128)(2,1)S(1)}, s32[8,128]{1,0:T(8,128)S(1)}, s32[16,128]{1,0:T(8,128)S(1)}, f32[80,128]{1,0:T(8,128)S(1)}) custom-call(f32[2,320,128]{2,1,0:T(8,128)S(1)} %get-tuple-element.29.own, f32[336,128]{1,0:T(8,128)S(1)} %collective-permute-done.r_a, ...), custom_call_target="tpu_custom_call" | custom-call | flops 10000 | bytes 10000 | tf_op jit(solution)/shard_map/pallas_call | solution.py:480
  12.2 0.1 collective-permute-start.2
  12.2 1.5 %shard_map.67.part = f32[2,320,128]{2,1,0:T(8,128)S(1)} custom-call(f32[2,320,128]{2,1,0:T(8,128)S(1)} %get-tuple-element.34.fld.rest_0_, s32[6,256]{1,0:T(8,128)S(1)} %get-tuple-element.35.nb_ref, s32[6,256]{1,0:T(8,128)S(1)} %get-tuple-element.36.ori_ref, f32[1,256]{1,0:T(1,128)S(1)} %get-tuple-element.37.coef_ref, ...), custom_call_target="tpu_custom_call" | custom-call | flops 20000 | bytes 20000 | tf_op jit(solution)/shard_map/pallas_call | solution.py:480
  13.8 0.0 collective-permute-done.2.r_a
  13.8 0.7 %shard_map.68 = (f32[2,320,128]{2,1,0:T(8,128)S(1)}, f32[96,128]{1,0:T(8,128)S(1)}) custom-call(f32[2,320,128]{2,1,0:T(8,128)S(1)} %shard_map.67.part, f32[80,128]{1,0:T(8,128)S(1)} %get-tuple-element.39.g, f32[80,128]{1,0:T(8,128)S(1)} %collective-permute-done.2.r_a, s32[16,128]{1,0:T(8,128)S(1)} %get-tuple-element.40.info, ...), custom_call_target="tpu_custom_call" | custom-call | flops 10000 | bytes 10000 | tf_op jit(solution)/shard_map/pallas_call | solution.py:480
  14.5 5.4 %collective-permute-start.3 = (f32[96,128]{1,0:T(8,128)S(1)}, f32[96,128]{1,0:T(8,128)S(1)}, u32[]{:S(2)}, u32[]{:S(2)}) collective-permute-start(f32[96,128]{1,0:T(8,128)S(1)} %get-tuple-element.45), channel_id=1, source_target_pairs={{0,31},{1,2},{2,1},{3,4},{4,3},{5,6},{6,5},{7,8},{8,7},{9,10},{10,... | collective-permute-start | bytes 147464 | tf_op jit(solution)/shard_map/ppermute | solution.py:580
  19.9 0.1 shard_map.69.pairs
  20.0 1.7 %collective-permute-done.3.r_b = f32[96,128]{1,0:T(8,128)S(1)} collective-permute-done((f32[96,128]{1,0:T(8,128)S(1)}, f32[96,128]{1,0:T(8,128)S(1)}, u32[]{:S(2)}, u32[]{:S(2)}) %collective-permute-start.3) | collective-permute-done | bytes 49184 | tf_op jit(solution)/shard_map/ppermute | solution.py:580
  21.7 0.7 %shard_map.70 = (f32[2,320,128]{2,1,0:T(8,128)S(1)}, f32[80,128]{1,0:T(8,128)S(1)}, f32[80,128]{1,0:T(8,128)S(1)}) custom-call(f32[2,320,128]{2,1,0:T(8,128)S(1)} %get-tuple-element.44.after.fp, f32[80,128]{1,0:T(8,128)S(1)} %get-tuple-element.39.g, f32[96,128]{1,0:T(8,128)S(1)} %collective-permute-done.3.r_b, s32[16,128]{1,0:T(8,128)S(1)} %get-tuple-element.40.info, ...), custom_call_target="tpu_custom_call" | custom-call | flops 10000 | bytes 10000 | tf_op jit(solution)/shard_map/pallas_call | solution.py:480
  22.4 0.1 collective-permute-start.4
  22.5 1.6 %shard_map.71.part = f32[2,320,128]{2,1,0:T(8,128)S(1)} custom-call(f32[2,320,128]{2,1,0:T(8,128)S(1)} %get-tuple-element.46.fld, s32[6,256]{1,0:T(8,128)S(1)} %get-tuple-element.35.nb_ref, s32[6,256]{1,0:T(8,128)S(1)} %get-tuple-element.36.ori_ref, f32[1,256]{1,0:T(1,128)S(1)} %get-tuple-element.37.coef_ref, bf16[128,192]{1,0:T(8,128)(2,1)S(1)} %get-tuple-element.38.dd_ref, ...), custom_call_target="tpu_custom_call" | custom-call | flops 20000 | bytes 20000 | tf_op jit(solution)/shard_map/pallas_call | solution.py:480
  24.1 0.0 collective-permute-done.4.r_a
  24.1 1.1 %shard_map.72 = f32[5,64,256]{2,1,0:T(8,128)} custom-call(f32[2,320,128]{2,1,0:T(8,128)S(1)} %shard_map.71.part, f32[80,128]{1,0:T(8,128)S(1)} %get-tuple-element.47.g1, f32[80,128]{1,0:T(8,128)S(1)} %collective-permute-done.4.r_a, f32[80,128]{1,0:T(8,128)S(1)} %get-tuple-element.48.o1, s32[16,128]{1,0:T(8,128)S(1)} %get-tuple-element.40.info, ...), custom_call_target="tpu_custom_call" | custom-call | flops 10000 | bytes 10000 | tf_op jit(solution)/shard_map/pallas_call | solution.py:480
Async XLA Ops:
  1.7 8.0 %collective-permute-start = (f32[336,128]{1,0:T(8,128)S(1)}, f32[336,128]{1,0:T(8,128)S(1)}, u32[]{:S(2)}, u32[]{:S(2)}) collective-permute-start(f32[336,128]{1,0:T(8,128)S(1)} %get-tuple-element.30), channel_id=1, source_target_pairs={{0,1},{1,0},{2,3},{3,2},{4,5},{5,4},{6,7},{7,6},{8,9},{9,8},{10,11... | collective-permute-start | bytes 516104 | tf_op jit(solution)/shard_map/ppermute | solution.py:523
  2.2 9.7 %collective-permute-start.1 = (f32[336,128]{1,0:T(8,128)S(1)}, f32[336,128]{1,0:T(8,128)S(1)}, u32[]{:S(2)}, u32[]{:S(2)}) collective-permute-start(f32[336,128]{1,0:T(8,128)S(1)} %get-tuple-element.31), channel_id=1, source_target_pairs={{0,31},{1,2},{2,1},{3,4},{4,3},{5,6},{6,5},{7,8},{8,7},{9,10},{10,... | collective-permute-start | bytes 516104 | tf_op jit(solution)/shard_map/ppermute | solution.py:524
  12.2 1.6 %collective-permute-start.2 = (f32[80,128]{1,0:T(8,128)S(1)}, f32[80,128]{1,0:T(8,128)S(1)}, u32[]{:S(2)}, u32[]{:S(2)}) collective-permute-start(f32[80,128]{1,0:T(8,128)S(1)} %get-tuple-element.39.g), channel_id=1, source_target_pairs={{0,1},{1,0},{2,3},{3,2},{4,5},{5,4},{6,7},{7,6},{8,9},{9,8},{10,11... | collective-permute-start | bytes 122888 | tf_op jit(solution)/shard_map/ppermute | solution.py:571
  14.5 7.1 %collective-permute-start.3 = (f32[96,128]{1,0:T(8,128)S(1)}, f32[96,128]{1,0:T(8,128)S(1)}, u32[]{:S(2)}, u32[]{:S(2)}) collective-permute-start(f32[96,128]{1,0:T(8,128)S(1)} %get-tuple-element.45), channel_id=1, source_target_pairs={{0,31},{1,2},{2,1},{3,4},{4,3},{5,6},{6,5},{7,8},{8,7},{9,10},{10,... | collective-permute-start | bytes 147464 | tf_op jit(solution)/shard_map/ppermute | solution.py:580
  22.4 1.7 %collective-permute-start.4 = (f32[80,128]{1,0:T(8,128)S(1)}, f32[80,128]{1,0:T(8,128)S(1)}, u32[]{:S(2)}, u32[]{:S(2)}) collective-permute-start(f32[80,128]{1,0:T(8,128)S(1)} %get-tuple-element.47.g1), channel_id=1, source_target_pairs={{0,1},{1,0},{2,3},{3,2},{4,5},{5,4},{6,7},{7,6},{8,9},{9,8},{10,11... | collective-permute-start | bytes 122888 | tf_op jit(solution)/shard_map/ppermute | solution.py:589

commit v3 on v2

--- a/solution.py
+++ b/solution.py
@@ -144,9 +144,8 @@
     rows_ref[0:8, :] = code
     rows_ref[8:16, :] = turn
     col_ref[...] = wide[64:128, :]
-    for out in (s_a, s_b):
-        out[ROWS : ROWS + 8, :] = code
-        out[ROWS + 8 : ROWS + 16, :] = turn
+    s_a[ROWS : ROWS + 8, :] = code
+    s_a[ROWS + 8 : ROWS + 16, :] = turn
 
     copies[2].wait()
     o = start[d] - d * EL
@@ -231,7 +230,7 @@
         g[16 * v : 16 * v + 16, :] = chosen(gs, face, v)
 
 
-def join_kernel(sizes, own, r_a, r_b, rows_ref, edge, fld, hot_ref, code_ref, info, g, gs):
+def join_kernel(sizes, own, r_a, r_b, c_b, rows_ref, edge, fld, hot_ref, code_ref, info, g, gs):
     even = (rank_of(sizes) & 1) == 0
     lane = iota((NODES, LANES), 1)
     below = lane < edge[0:1, :]
@@ -245,12 +244,12 @@
     code = jnp.where(
         lane8 < 32,
         r_a[ROWS : ROWS + 8, :],
-        jnp.where(lane8 < 64, r_b[ROWS : ROWS + 8, :], rows_ref[0:8, :]),
+        jnp.where(lane8 < 64, c_b[0:8, :], rows_ref[0:8, :]),
     ).astype(I32)
     code_ref[...] = code
     lane16 = iota((16, LANES), 1)
     info[...] = jnp.where(
-        lane16 < 96, pltpu.roll(rows_ref[...], 64, 1), r_b[ROWS : ROWS + 16, :]
+        lane16 < 96, pltpu.roll(rows_ref[...], 64, 1), c_b[...]
     ).astype(I32)
     spot = jnp.broadcast_to(code[0:1, :] & 255, (EL, LANES))
     hot = jnp.where(spot == iota((EL, LANES), 0), 1.0, 0.0).astype(BF)
@@ -503,7 +502,7 @@
         functools.partial(send_kernel, sizes),
         (
             shape(ROWS + 16, LANES),
-            shape(ROWS + 16, LANES),
+            shape(ROWS, LANES),
             shape(16, LANES),
             shape(64, LANES),
             shape(*old_state.shape),
@@ -521,7 +520,8 @@
         hbm=(0, 1, 2, 3),
     )
     r_a = lax.ppermute(s_a, AXES, pairs_a)
-    r_b = lax.ppermute(s_b, AXES, pairs_b)
+    c_b = lax.ppermute(rows, AXES, pairs_b)
+    r_b = lax.ppermute(s_b, AXES, pairs_b[1:-1])
     own, ohs, dd, coef = call(
         functools.partial(own_kernel, sizes),
         (
@@ -555,7 +555,7 @@
         ),
         [table],
         10000,
-        (own, r_a, r_b, rows, edge),
+        (own, r_a, r_b, c_b, rows, edge),
     )
 
     def local(last, *args):

time: 25.4 us -> 25 us (0.984)
  waiting for transfers between devices: 3.84 us -> 2.21 us
  starting transfers between devices: 12.6 us -> 13.8 us
    ppermute x1 -> x2, waiting for transfers between devices: 2.16 us -> 0.53 us  [the longest x1 0.53 us: per_device(): c_b = lax.ppermute(rows, AXES, pairs_b)]
    ppermute x1 -> x2, starting transfers between devices: 6.59 us -> 7.32 us  [the longest x1 6.66 us: per_device(): c_b = lax.ppermute(rows, AXES, pairs_b)]
    ppermute x1, starting transfers between devices: 5.36 us -> 5.86 us  [per_device(): r_b = lax.ppermute(pb, AXES, pairs_b)]
  transfers between devices with their start and end apart: 5 -> 6, of which waited for: 2 -> 2; matrix products, arithmetic and copies ran while one was open for 0% -> 0% of each run, Pallas kernels for 16% -> 17%
where the time goes in v3:
time: 25 us; the launch traced here: 24.8 us
  starting transfers between devices  13.8 us (55%)
  Pallas kernels  8.62 us (34%)
  waiting for transfers between devices  2.21 us (9%)
    pallas_call x9, Pallas kernels, call(): pl.pallas_call(body, out_shape=out_shape, in_specs=specs, out_specs=jax.t...  8.62 us
    ppermute x1, starting transfers between devices, per_device(): c_b = lax.ppermute(rows, AXES, pairs_b)  6.66 us
    ppermute x1, starting transfers between devices, per_device(): r_b = lax.ppermute(pb, AXES, pairs_b)  5.86 us
    ppermute x1, waiting for transfers between devices, per_device(): r_b = lax.ppermute(pb, AXES, pairs_b)  1.67 us
    ppermute x1, starting transfers between devices, per_device(): r_b = lax.ppermute(s_b, AXES, pairs_b[1:-1])  0.66 us
    ppermute x1, waiting for transfers between devices, per_device(): c_b = lax.ppermute(rows, AXES, pairs_b)  0.53 us
    ppermute x1, starting transfers between devices, per_device(): r_a = lax.ppermute(s_a, AXES, pairs_a)  0.52 us
  transfers between devices with their start and end apart: 6, of which 2 were waited for; matrix products, arithmetic and copies ran while one was open for 0% of the time, Pallas kernels for 17%

profile of v3, /device:TPU:0, one launch (start us, length us, event | category | flops | bytes accessed | tf_op | source)
XLA Modules:
  0.0 24.8 jit_solution(16044183982911739201)
XLA Ops:
  0.0 1.7 %shard_map.64 = (f32[336,128]{1,0:T(8,128)S(1)}, f32[320,128]{1,0:T(8,128)S(1)}, f32[16,128]{1,0:T(8,128)S(1)}, f32[64,128]{1,0:T(8,128)S(1)}, f32[5,64,512]{2,1...) custom-call(s32[33]{0:T(128)} %start_hbm.3, f32[5,64,512]{2,1,0:T(8,128)} %old.1, ...), custom_call_target="tpu_custom_call" | custom-call | flops 10000 | bytes 10000 | tf_op jit(solution)/shard_map/pallas_call | solution.py:479
  1.7 0.5 %collective-permute-start = (f32[336,128]{1,0:T(8,128)S(1)}, f32[336,128]{1,0:T(8,128)S(1)}, u32[]{:S(2)}, u32[]{:S(2)}) collective-permute-start(f32[336,128]{1,0:T(8,128)S(1)} %get-tuple-element.30), channel_id=1, source_target_pairs={{0,1},{1,0},{2,3},{3,2},{4,5},{5,4},{6,7},{7,6},{8,9},{9,8},{10,11... | collective-permute-start | bytes 516104 | tf_op jit(solution)/shard_map/ppermute | solution.py:522
  2.2 0.7 %collective-permute-start.1 = (f32[320,128]{1,0:T(8,128)S(1)}, f32[320,128]{1,0:T(8,128)S(1)}, u32[]{:S(2)}, u32[]{:S(2)}) collective-permute-start(f32[320,128]{1,0:T(8,128)S(1)} %get-tuple-element.31), channel_id=1, source_target_pairs={{1,2},{2,1},{3,4},{4,3},{5,6},{6,5},{7,8},{8,7},{9,10},{10,9},{11,... | collective-permute-start | bytes 491528 | tf_op jit(solution)/shard_map/ppermute | solution.py:524
  2.9 6.7 %collective-permute-start.2 = (f32[16,128]{1,0:T(8,128)S(1)}, f32[16,128]{1,0:T(8,128)S(1)}, u32[]{:S(2)}, u32[]{:S(2)}) collective-permute-start(f32[16,128]{1,0:T(8,128)S(1)} %get-tuple-element.32.rows_ref), channel_id=1, source_target_pairs={{0,31},{1,2},{2,1},{3,4},{4,3},{5,6},{6,5},{7,8},{8,7},{9,10},{10,... | collective-permute-start | bytes 24584 | tf_op jit(solution)/shard_map/ppermute | solution.py:523
  9.5 0.9 %shard_map.65 = (f32[2,320,128]{2,1,0:T(8,128)S(1)}, bf16[128,256]{1,0:T(8,128)(2,1)S(1)}, bf16[128,192]{1,0:T(8,128)(2,1)S(1)}, f32[1,256]{1,0:T(1,128)S(1)}) custom-call(s32[33]{0:T(128)} %start_hbm.3, f32[5,64,512]{2,1,0:T(8,128)S(1)} %get-tuple-element.27.old, f32[64,128]{1,0:T(8,128)S(1)} %get-tuple-element.28.col_ref, f32[64,192]{1,0:T(8,128)} %constant.2.clone.d_hbm, ...), custom_call_target="tpu_custom_call" | custom-call | flops 10000 | bytes 10000 | tf_op jit(solution)/shard_map/pallas_call | solution.py:479
  10.4 0.5 %collective-permute-done.2.c_b = f32[16,128]{1,0:T(8,128)S(1)} collective-permute-done((f32[16,128]{1,0:T(8,128)S(1)}, f32[16,128]{1,0:T(8,128)S(1)}, u32[]{:S(2)}, u32[]{:S(2)}) %collective-permute-start.2) | collective-permute-done | bytes 8224 | tf_op jit(solution)/shard_map/ppermute | solution.py:523
  11.0 0.0 collective-permute-done.1.r_b
  11.0 0.0 collective-permute-done.r_a
  11.0 0.3 %shard_map.66 = (f32[2,320,128]{2,1,0:T(8,128)S(1)}, bf16[256,128]{1,0:T(8,128)(2,1)S(1)}, s32[8,128]{1,0:T(8,128)S(1)}, s32[16,128]{1,0:T(8,128)S(1)}, f32[80,128]{1,0:T(8,128)S(1)}) custom-call(f32[2,320,128]{2,1,0:T(8,128)S(1)} %get-tuple-element.29.own, f32[336,128]{1,0:T(8,128)S(1)} %collective-permute-done.r_a, ...), custom_call_target="tpu_custom_call" | custom-call | flops 10000 | bytes 10000 | tf_op jit(solution)/shard_map/pallas_call | solution.py:479
  11.3 0.1 collective-permute-start.3
  11.3 1.5 %shard_map.67.part = f32[2,320,128]{2,1,0:T(8,128)S(1)} custom-call(f32[2,320,128]{2,1,0:T(8,128)S(1)} %get-tuple-element.34.fld.rest_0_, s32[6,256]{1,0:T(8,128)S(1)} %get-tuple-element.35.nb_ref, s32[6,256]{1,0:T(8,128)S(1)} %get-tuple-element.36.ori_ref, f32[1,256]{1,0:T(1,128)S(1)} %get-tuple-element.37.coef_ref, ...), custom_call_target="tpu_custom_call" | custom-call | flops 20000 | bytes 20000 | tf_op jit(solution)/shard_map/pallas_call | solution.py:479
  12.9 0.0 collective-permute-done.3.r_a
  12.9 0.7 %shard_map.68 = (f32[2,320,128]{2,1,0:T(8,128)S(1)}, f32[96,128]{1,0:T(8,128)S(1)}) custom-call(f32[2,320,128]{2,1,0:T(8,128)S(1)} %shard_map.67.part, f32[80,128]{1,0:T(8,128)S(1)} %get-tuple-element.39.g, f32[80,128]{1,0:T(8,128)S(1)} %collective-permute-done.3.r_a, s32[16,128]{1,0:T(8,128)S(1)} %get-tuple-element.40.info, ...), custom_call_target="tpu_custom_call" | custom-call | flops 10000 | bytes 10000 | tf_op jit(solution)/shard_map/pallas_call | solution.py:479
  13.6 5.9 %collective-permute-start.4 = (f32[96,128]{1,0:T(8,128)S(1)}, f32[96,128]{1,0:T(8,128)S(1)}, u32[]{:S(2)}, u32[]{:S(2)}) collective-permute-start(f32[96,128]{1,0:T(8,128)S(1)} %get-tuple-element.45), channel_id=1, source_target_pairs={{0,31},{1,2},{2,1},{3,4},{4,3},{5,6},{6,5},{7,8},{8,7},{9,10},{10,... | collective-permute-start | bytes 147464 | tf_op jit(solution)/shard_map/ppermute | solution.py:580
  19.5 0.1 shard_map.69.pairs
  19.6 1.7 %collective-permute-done.4.r_b = f32[96,128]{1,0:T(8,128)S(1)} collective-permute-done((f32[96,128]{1,0:T(8,128)S(1)}, f32[96,128]{1,0:T(8,128)S(1)}, u32[]{:S(2)}, u32[]{:S(2)}) %collective-permute-start.4) | collective-permute-done | bytes 49184 | tf_op jit(solution)/shard_map/ppermute | solution.py:580
  21.3 0.7 %shard_map.70 = (f32[2,320,128]{2,1,0:T(8,128)S(1)}, f32[80,128]{1,0:T(8,128)S(1)}, f32[80,128]{1,0:T(8,128)S(1)}) custom-call(f32[2,320,128]{2,1,0:T(8,128)S(1)} %get-tuple-element.44.after.fp, f32[80,128]{1,0:T(8,128)S(1)} %get-tuple-element.39.g, f32[96,128]{1,0:T(8,128)S(1)} %collective-permute-done.4.r_b, s32[16,128]{1,0:T(8,128)S(1)} %get-tuple-element.40.info, ...), custom_call_target="tpu_custom_call" | custom-call | flops 10000 | bytes 10000 | tf_op jit(solution)/shard_map/pallas_call | solution.py:479
  22.0 0.1 collective-permute-start.5
  22.1 1.6 %shard_map.71.part = f32[2,320,128]{2,1,0:T(8,128)S(1)} custom-call(f32[2,320,128]{2,1,0:T(8,128)S(1)} %get-tuple-element.46.fld, s32[6,256]{1,0:T(8,128)S(1)} %get-tuple-element.35.nb_ref, s32[6,256]{1,0:T(8,128)S(1)} %get-tuple-element.36.ori_ref, f32[1,256]{1,0:T(1,128)S(1)} %get-tuple-element.37.coef_ref, bf16[128,192]{1,0:T(8,128)(2,1)S(1)} %get-tuple-element.38.dd_ref, ...), custom_call_target="tpu_custom_call" | custom-call | flops 20000 | bytes 20000 | tf_op jit(solution)/shard_map/pallas_call | solution.py:479
  23.7 0.0 collective-permute-done.5.r_a
  23.7 1.1 %shard_map.72 = f32[5,64,256]{2,1,0:T(8,128)} custom-call(f32[2,320,128]{2,1,0:T(8,128)S(1)} %shard_map.71.part, f32[80,128]{1,0:T(8,128)S(1)} %get-tuple-element.47.g1, f32[80,128]{1,0:T(8,128)S(1)} %collective-permute-done.5.r_a, f32[80,128]{1,0:T(8,128)S(1)} %get-tuple-element.48.o1, s32[16,128]{1,0:T(8,128)S(1)} %get-tuple-element.40.info, ...), custom_call_target="tpu_custom_call" | custom-call | flops 10000 | bytes 10000 | tf_op jit(solution)/shard_map/pallas_call | solution.py:479
Async XLA Ops:
  1.7 9.3 %collective-permute-start = (f32[336,128]{1,0:T(8,128)S(1)}, f32[336,128]{1,0:T(8,128)S(1)}, u32[]{:S(2)}, u32[]{:S(2)}) collective-permute-start(f32[336,128]{1,0:T(8,128)S(1)} %get-tuple-element.30), channel_id=1, source_target_pairs={{0,1},{1,0},{2,3},{3,2},{4,5},{5,4},{6,7},{7,6},{8,9},{9,8},{10,11... | collective-permute-start | bytes 516104 | tf_op jit(solution)/shard_map/ppermute | solution.py:522
  2.2 8.8 %collective-permute-start.1 = (f32[320,128]{1,0:T(8,128)S(1)}, f32[320,128]{1,0:T(8,128)S(1)}, u32[]{:S(2)}, u32[]{:S(2)}) collective-permute-start(f32[320,128]{1,0:T(8,128)S(1)} %get-tuple-element.31), channel_id=1, source_target_pairs={{1,2},{2,1},{3,4},{4,3},{5,6},{6,5},{7,8},{8,7},{9,10},{10,9},{11,... | collective-permute-start | bytes 491528 | tf_op jit(solution)/shard_map/ppermute | solution.py:524
  2.9 8.1 %collective-permute-start.2 = (f32[16,128]{1,0:T(8,128)S(1)}, f32[16,128]{1,0:T(8,128)S(1)}, u32[]{:S(2)}, u32[]{:S(2)}) collective-permute-start(f32[16,128]{1,0:T(8,128)S(1)} %get-tuple-element.32.rows_ref), channel_id=1, source_target_pairs={{0,31},{1,2},{2,1},{3,4},{4,3},{5,6},{6,5},{7,8},{8,7},{9,10},{10,... | collective-permute-start | bytes 24584 | tf_op jit(solution)/shard_map/ppermute | solution.py:523
  11.3 1.6 %collective-permute-start.3 = (f32[80,128]{1,0:T(8,128)S(1)}, f32[80,128]{1,0:T(8,128)S(1)}, u32[]{:S(2)}, u32[]{:S(2)}) collective-permute-start(f32[80,128]{1,0:T(8,128)S(1)} %get-tuple-element.39.g), channel_id=1, source_target_pairs={{0,1},{1,0},{2,3},{3,2},{4,5},{5,4},{6,7},{7,6},{8,9},{9,8},{10,11... | collective-permute-start | bytes 122888 | tf_op jit(solution)/shard_map/ppermute | solution.py:571
  13.6 7.6 %collective-permute-start.4 = (f32[96,128]{1,0:T(8,128)S(1)}, f32[96,128]{1,0:T(8,128)S(1)}, u32[]{:S(2)}, u32[]{:S(2)}) collective-permute-start(f32[96,128]{1,0:T(8,128)S(1)} %get-tuple-element.45), channel_id=1, source_target_pairs={{0,31},{1,2},{2,1},{3,4},{4,3},{5,6},{6,5},{7,8},{8,7},{9,10},{10,... | collective-permute-start | bytes 147464 | tf_op jit(solution)/shard_map/ppermute | solution.py:580
  22.0 1.7 %collective-permute-start.5 = (f32[80,128]{1,0:T(8,128)S(1)}, f32[80,128]{1,0:T(8,128)S(1)}, u32[]{:S(2)}, u32[]{:S(2)}) collective-permute-start(f32[80,128]{1,0:T(8,128)S(1)} %get-tuple-element.47.g1), channel_id=1, source_target_pairs={{0,1},{1,0},{2,3},{3,2},{4,5},{5,4},{6,7},{7,6},{8,9},{9,8},{10,11... | collective-permute-start | bytes 122888 | tf_op jit(solution)/shard_map/ppermute | solution.py:589

commit v4 on v3

--- a/solution.py
+++ b/solution.py
@@ -15,6 +15,8 @@
 NODES = 64
 EL = 256
 LANES = 128
+PITCH = 12
+TABLE = 16 * PITCH
 REMOTE = 32
 FACES = 6
 ROWS = VARS * NODES
@@ -76,14 +78,13 @@
     return ref[rows_at(lead, v * NODES, f)]
 
 
-def add_face_rows(ref, lead, v, f, val):
+def put_face_rows(across, lead, v, f, val):
+    ref = across[f // 2]
     if f in (2, 3):
         for i in range(4):
-            r = rows_at(lead, v * NODES, f, i)
-            ref[r] = ref[r] + val[4 * i : 4 * i + 4, :]
+            ref[rows_at(lead, v * NODES, f, i)] = val[4 * i : 4 * i + 4, :]
     else:
-        r = rows_at(lead, v * NODES, f)
-        ref[r] = ref[r] + val
+        ref[rows_at(lead, v * NODES, f)] = val
 
 
 def rank_of(sizes):
@@ -296,9 +297,11 @@
 
 def local_kernel(sizes, last, fld, nb_ref, ori_ref, coef_ref, dd_ref, *rest):
     if last:
-        old_fld, part, acc, xs, xg, xq, xo, xc, it = rest
+        old_fld, part, acc, ax, ay, az, xs, xg, xq, xo, xc, it = rest
     else:
-        part, acc, xs, xg, xq, xo, xc, it = rest
+        part, acc, ax, ay, az, xs, xg, xq, xo, xc, it = rest
+    for ref in (ax, ay, az):
+        ref[...] = jnp.zeros((2, ROWS, LANES), F32)
     d = rank_of(sizes)
     dd = dd_ref[...]
     dh = dd[0:NODES, :]
@@ -323,10 +326,10 @@
         for f in range(FACES):
             for h in range(2):
                 t = face_rows(fld, h, v, f)
-                b = v * 256
-                xs[pl.ds(b + 2 * f + h, 16, stride=16), :] = t
-                xg[pl.ds(b + 2 * (f ^ 1) + h, 16, stride=16), :] = t
-                xq[pl.ds(b + 2 * (f ^ 1) + 1 - h, 16, stride=16), :] = t
+                b = v * TABLE
+                xs[pl.ds(b + 2 * f + h, 16, stride=PITCH), :] = t
+                xg[pl.ds(b + 2 * (f ^ 1) + h, 16, stride=PITCH), :] = t
+                xq[pl.ds(b + 2 * (f ^ 1) + 1 - h, 16, stride=PITCH), :] = t
     it[...] = jnp.zeros((32, LANES), I32)
     for h in range(2):
         it[pl.ds(h, FACES, stride=2), :] = nb_ref[:, h * LANES : h * LANES + LANES]
@@ -341,52 +344,56 @@
     for v in range(VARS):
         got = []
         for m in range(16):
-            rows = slice(v * 256 + m * 16, v * 256 + m * 16 + 16)
+            rows = pl.ds(v * TABLE + m * PITCH, 16)
             ga = jnp.take_along_axis(xg[rows, :], idx, axis=1)
             gb = jnp.take_along_axis(xq[rows, :], idx, axis=1)
             got.append(jnp.where(same, ga, gb))
         for m, x in enumerate(turned(got, b0, b1, b2)):
-            xo[v * 256 + m * 16 : v * 256 + m * 16 + 16, :] = x
+            xo[pl.ds(v * TABLE + m * PITCH, 12), :] = x[0:12, :]
     axis_is = (row < 4, (row >= 4) & (row < 8))
     half_sign = jnp.where((row & 2) != 0, 0.5, -0.5)
     for m in range(16):
-        rows = [slice(v * 256 + m * 16, v * 256 + m * 16 + 16) for v in range(VARS)]
+        rows = [pl.ds(v * TABLE + m * PITCH, 16) for v in range(VARS)]
         cor = correction([xs[r, :] for r in rows], [xo[r, :] for r in rows], axis_is, half_sign)
         for v in range(VARS):
-            xc[rows[v], :] = jnp.where(local, LIFT * cor[v], 0.0)
+            val = jnp.where(local, LIFT * cor[v], 0.0)
+            xc[pl.ds(v * TABLE + m * PITCH, 12), :] = val[0:12, :]
     for v in range(VARS):
         for f in range(FACES):
             for h in range(2):
-                add_face_rows(
-                    acc, h, v, f, xc[pl.ds(v * 256 + 2 * f + h, 16, stride=16), :]
+                put_face_rows(
+                    (ax, ay, az), h, v, f, xc[pl.ds(v * TABLE + 2 * f + h, 16, stride=PITCH), :]
                 )
     for h in range(2):
         coef = coef_ref[0:1, h * LANES : h * LANES + LANES]
         for v in range(VARS):
             rows = slice(v * NODES, v * NODES + NODES)
-            new = fld[h, rows, :] - coef * acc[h, rows, :]
+            rate = acc[h, rows, :] + ax[h, rows, :] + ay[h, rows, :] + az[h, rows, :]
+            new = fld[h, rows, :] - coef * rate
             if last:
                 new = 0.5 * old_fld[h, rows, :] + 0.5 * new
             part[h, rows, :] = new
 
 
-def face_terms(inner, outer, info, live, ro, y, e):
-    ro[0:80, :] = outer
-    ro[80:128, :] = jnp.zeros((48, LANES), F32)
+def face_terms(inner, outer, info, live, ro, y, ex, ey, ez):
+    for v in range(VARS):
+        ro[17 * v : 17 * v + 16, :] = outer[16 * v : 16 * v + 16, :]
     turn = info[8:16, :]
-    x = [ro[pl.ds(m, 8, stride=16), :] for m in range(16)]
+    x = [ro[pl.ds(m, 8, stride=17), :] for m in range(16)]
     for m, val in enumerate(turned(x, (turn & 1) != 0, (turn & 2) != 0, (turn & 4) != 0)):
-        y[8 * m : 8 * m + 8, :] = val
+        y[9 * m : 9 * m + 8, :] = val
     face = jnp.where(live, jnp.broadcast_to(info[0:1, :], (16, LANES)) >> 8, -1)
     axis_is = (face < 2, (face >= 2) & (face < 4))
     half_sign = jnp.where((face & 1) != 0, 0.5, -0.5)
-    behind = [y[pl.ds(v, 16, stride=8), :] for v in range(VARS)]
+    behind = [y[pl.ds(v, 16, stride=9), :] for v in range(VARS)]
     here = [inner[16 * v : 16 * v + 16, :] for v in range(VARS)]
     cor = correction(here, behind, axis_is, half_sign)
-    e[...] = jnp.zeros((ROWS, LANES), F32)
+    for ref in (ex, ey, ez):
+        ref[...] = jnp.zeros((ROWS, LANES), F32)
     for v in range(VARS):
         for f in range(FACES):
-            add_face_rows(e, None, v, f, jnp.where(face == f, cor[v], 0.0))
+            put_face_rows((ex, ey, ez), None, v, f, jnp.where(face == f, cor[v], 0.0))
+    return jnp.concatenate(split(ex[...] + ey[...] + ez[...]), 0)
 
 
 def added(part, spread, coef_ref, scale, put):
@@ -399,10 +406,10 @@
             put(h, v, part[h, rows, :] - coef * (spread[rows, lanes] + spread[low, lanes]))
 
 
-def near_kernel(part, g, r_a, info, ohs, coef_ref, hot_ref, code_ref, fp, pb, ro, y, e, g1):
+def near_kernel(part, g, r_a, info, ohs, coef_ref, hot_ref, code_ref, fp, pb, ro, y, ex, ey, ez, g1):
     lane = iota((16, LANES), 1)
-    face_terms(pltpu.roll(g[...], 64, 1), r_a[...], info, lane < 32, ro, y, e)
-    spread = mm(jnp.concatenate(split(e[...]), 0), ohs[...])
+    parts = face_terms(pltpu.roll(g[...], 64, 1), r_a[...], info, lane < 32, ro, y, ex, ey, ez)
+    spread = mm(parts, ohs[...])
 
     def put(h, v, new):
         fp[h, v * NODES : v * NODES + NODES, :] = new
@@ -410,7 +417,7 @@
     added(part, spread, coef_ref, LIFT, put)
     hot = hot_ref[...]
     asked = jnp.broadcast_to(code_ref[0:1, :] >> 8, (16, LANES))
-    requested(fp, hot, asked, e, g1)
+    requested(fp, hot, asked, ex, g1)
     lane = iota((80, LANES), 1)
     pb[0:80, :] = jnp.where(lane < 32, pltpu.roll(g1[...], 96, 1), g[...])
     ch, cl = split(jnp.broadcast_to(LIFT * coef_ref[0:1, :], (16, EL)))
@@ -426,17 +433,15 @@
 
 
 def far_kernel(
-    fp, g, r_b, info, rows_ref, ohs, pairs, coef_ref, hot_ref, code_ref, first, g1, o1, ro, y, e
+    fp, g, r_b, info, rows_ref, ohs, pairs, coef_ref, hot_ref, code_ref, first, g1, o1, ro, y, ex, ey, ez
 ):
     lane = iota((80, LANES), 1)
     mine = pltpu.roll(g[...], 64, 1)
     got = r_b[0:80, :]
     lane16 = iota((16, LANES), 1)
     live = ((lane16 >= 32) & (lane16 < 64)) | (lane16 >= 96)
-    face_terms(
-        jnp.where(lane < 64, mine, got), jnp.where(lane < 64, got, mine), info, live, ro, y, e
-    )
-    parts = jnp.concatenate(split(e[...]), 0)
+    inner, outer = jnp.where(lane < 64, mine, got), jnp.where(lane < 64, got, mine)
+    parts = face_terms(inner, outer, info, live, ro, y, ex, ey, ez)
     spread = mm(parts, ohs[...])
 
     def put(h, v, new):
@@ -444,21 +449,22 @@
 
     added(fp, spread, coef_ref, LIFT, put)
     theirs = mm(parts, pairs[...])
-    e[...] = theirs[0:ROWS, :] + theirs[ROWS : 2 * ROWS, :]
+    ey[...] = theirs[0:ROWS, :] + theirs[ROWS : 2 * ROWS, :]
     face = jnp.broadcast_to(rows_ref[0:1, :].astype(I32) >> 8, (16, LANES))
     coef = r_b[80:81, :]
     for v in range(VARS):
         rows = slice(16 * v, 16 * v + 16)
-        o1[rows, :] = pltpu.roll(r_b[rows, :], 32, 1) - coef * chosen(e, face, v)
+        o1[rows, :] = pltpu.roll(r_b[rows, :], 32, 1) - coef * chosen(ey, face, v)
     asked = jnp.broadcast_to(code_ref[0:1, :] >> 8, (16, LANES))
-    requested(first, hot_ref[...], asked, e, g1)
-
-
-def last_kernel(part, g1, r_a, o1, info, ohs, coef_ref, out, ro, y, e):
+    requested(first, hot_ref[...], asked, ex, g1)
+
+
+def last_kernel(part, g1, r_a, o1, info, ohs, coef_ref, out, ro, y, ex, ey, ez):
     lane = iota((80, LANES), 1)
     outer = jnp.where(lane < 32, r_a[...], o1[...])
-    face_terms(pltpu.roll(g1[...], 64, 1), outer, info, iota((16, LANES), 1) < 64, ro, y, e)
-    spread = mm(jnp.concatenate(split(e[...]), 0), ohs[...])
+    live = iota((16, LANES), 1) < 64
+    parts = face_terms(pltpu.roll(g1[...], 64, 1), outer, info, live, ro, y, ex, ey, ez)
+    spread = mm(parts, ohs[...])
 
     def put(h, v, new):
         out[v, :, h * LANES : h * LANES + LANES] = new
@@ -541,7 +547,7 @@
         hbm=(0, 3, 4),
     )
     table = pltpu.VMEM((ROWS, LANES), F32)
-    square = pltpu.VMEM((LANES, LANES), F32)
+    square = pltpu.VMEM((LANES + 24, LANES), F32)
     traces = shape(80, LANES)
     state = shape(2, ROWS, LANES)
     fld, hot, code, info, g = call(
@@ -559,11 +565,11 @@
     )
 
     def local(last, *args):
-        faces = pltpu.VMEM((VARS * 256, LANES), F32)
+        faces = pltpu.VMEM((VARS * TABLE + 8, LANES), F32)
         return call(
             functools.partial(local_kernel, sizes, last),
             state,
-            [pltpu.VMEM((2, ROWS, LANES), F32)] + [faces] * 5 + [pltpu.VMEM((32, LANES), I32)],
+            [pltpu.VMEM((2, ROWS, LANES), F32)] * 4 + [faces] * 5 + [pltpu.VMEM((32, LANES), I32)],
             20000,
             args,
         )
@@ -573,7 +579,7 @@
     fp, pb = call(
         near_kernel,
         (state, shape(96, LANES)),
-        [square, square, table, pltpu.VMEM((80, LANES), F32)],
+        [square, square, table, table, table, pltpu.VMEM((80, LANES), F32)],
         10000,
         (part, g, r_a, info, ohs, coef, hot, code),
     )
@@ -582,7 +588,7 @@
     first, g1, o1 = call(
         far_kernel,
         (state, traces, traces),
-        [square, square, table],
+        [square, square, table, table, table],
         10000,
         (fp, g, r_b, info, rows, ohs, pairs, coef, hot, code),
     )
@@ -591,7 +597,7 @@
     return call(
         last_kernel,
         shape(VARS, NODES, EL),
-        [square, square, table],
+        [square, square, table, table, table],
         10000,
         (part, g1, r_a, o1, info, ohs, coef),
     )

time: 25 us -> 24.2 us (0.968)
  Pallas kernels: 8.62 us -> 7.79 us
    pallas_call x9, Pallas kernels: 8.62 us -> 7.79 us  [call(): pl.pallas_call(body, out_shape=out_shape, in_specs=specs, out_specs=jax.t...]
  transfers between devices with their start and end apart: 6 -> 6, of which waited for: 2 -> 2; matrix products, arithmetic and copies ran while one was open for 0% -> 0% of each run, Pallas kernels for 17% -> 14%
where the time goes in v4:
time: 24.2 us; the launch traced here: 23.9 us
  starting transfers between devices  13.8 us (57%)
  Pallas kernels  7.79 us (32%)
  waiting for transfers between devices  2.23 us (9%)
    pallas_call x9, Pallas kernels, call(): pl.pallas_call(body, out_shape=out_shape, in_specs=specs, out_specs=jax.t...  7.79 us
    ppermute x1, starting transfers between devices, per_device(): c_b = lax.ppermute(rows, AXES, pairs_b)  6.66 us
    ppermute x1, starting transfers between devices, per_device(): r_b = lax.ppermute(pb, AXES, pairs_b)  5.84 us
    ppermute x1, waiting for transfers between devices, per_device(): r_b = lax.ppermute(pb, AXES, pairs_b)  1.67 us
    ppermute x1, starting transfers between devices, per_device(): r_b = lax.ppermute(s_b, AXES, pairs_b[1:-1])  0.66 us
    ppermute x1, waiting for transfers between devices, per_device(): c_b = lax.ppermute(rows, AXES, pairs_b)  0.53 us
    ppermute x1, starting transfers between devices, per_device(): r_a = lax.ppermute(s_a, AXES, pairs_a)  0.52 us
  transfers between devices with their start and end apart: 6, of which 2 were waited for; matrix products, arithmetic and copies ran while one was open for 0% of the time, Pallas kernels for 14%

profile of v4, /device:TPU:0, one launch (start us, length us, event | category | flops | bytes accessed | tf_op | source)
XLA Modules:
  0.0 23.9 jit_solution(2293692594530695845)
XLA Ops:
  0.0 1.7 %shard_map.64 = (f32[336,128]{1,0:T(8,128)S(1)}, f32[320,128]{1,0:T(8,128)S(1)}, f32[16,128]{1,0:T(8,128)S(1)}, f32[64,128]{1,0:T(8,128)S(1)}, f32[5,64,512]{2,1...) custom-call(s32[33]{0:T(128)} %start_hbm.3, f32[5,64,512]{2,1,0:T(8,128)} %old.1, ...), custom_call_target="tpu_custom_call" | custom-call | flops 10000 | bytes 10000 | tf_op jit(solution)/shard_map/pallas_call | solution.py:485
  1.7 0.5 %collective-permute-start = (f32[336,128]{1,0:T(8,128)S(1)}, f32[336,128]{1,0:T(8,128)S(1)}, u32[]{:S(2)}, u32[]{:S(2)}) collective-permute-start(f32[336,128]{1,0:T(8,128)S(1)} %get-tuple-element.30), channel_id=1, source_target_pairs={{0,1},{1,0},{2,3},{3,2},{4,5},{5,4},{6,7},{7,6},{8,9},{9,8},{10,11... | collective-permute-start | bytes 516104 | tf_op jit(solution)/shard_map/ppermute | solution.py:528
  2.2 0.7 %collective-permute-start.1 = (f32[320,128]{1,0:T(8,128)S(1)}, f32[320,128]{1,0:T(8,128)S(1)}, u32[]{:S(2)}, u32[]{:S(2)}) collective-permute-start(f32[320,128]{1,0:T(8,128)S(1)} %get-tuple-element.31), channel_id=1, source_target_pairs={{1,2},{2,1},{3,4},{4,3},{5,6},{6,5},{7,8},{8,7},{9,10},{10,9},{11,... | collective-permute-start | bytes 491528 | tf_op jit(solution)/shard_map/ppermute | solution.py:530
  2.9 6.7 %collective-permute-start.2 = (f32[16,128]{1,0:T(8,128)S(1)}, f32[16,128]{1,0:T(8,128)S(1)}, u32[]{:S(2)}, u32[]{:S(2)}) collective-permute-start(f32[16,128]{1,0:T(8,128)S(1)} %get-tuple-element.32.rows_ref), channel_id=1, source_target_pairs={{0,31},{1,2},{2,1},{3,4},{4,3},{5,6},{6,5},{7,8},{8,7},{9,10},{10,... | collective-permute-start | bytes 24584 | tf_op jit(solution)/shard_map/ppermute | solution.py:529
  9.5 0.9 %shard_map.65 = (f32[2,320,128]{2,1,0:T(8,128)S(1)}, bf16[128,256]{1,0:T(8,128)(2,1)S(1)}, bf16[128,192]{1,0:T(8,128)(2,1)S(1)}, f32[1,256]{1,0:T(1,128)S(1)}) custom-call(s32[33]{0:T(128)} %start_hbm.3, f32[5,64,512]{2,1,0:T(8,128)S(1)} %get-tuple-element.27.old, f32[64,128]{1,0:T(8,128)S(1)} %get-tuple-element.28.col_ref, f32[64,192]{1,0:T(8,128)} %constant.2.clone.d_hbm, ...), custom_call_target="tpu_custom_call" | custom-call | flops 10000 | bytes 10000 | tf_op jit(solution)/shard_map/pallas_call | solution.py:485
  10.4 0.5 %collective-permute-done.2.c_b = f32[16,128]{1,0:T(8,128)S(1)} collective-permute-done((f32[16,128]{1,0:T(8,128)S(1)}, f32[16,128]{1,0:T(8,128)S(1)}, u32[]{:S(2)}, u32[]{:S(2)}) %collective-permute-start.2) | collective-permute-done | bytes 8224 | tf_op jit(solution)/shard_map/ppermute | solution.py:529
  11.0 0.0 collective-permute-done.1.r_b
  11.0 0.0 collective-permute-done.r_a
  11.0 0.3 %shard_map.66 = (f32[2,320,128]{2,1,0:T(8,128)S(1)}, bf16[256,128]{1,0:T(8,128)(2,1)S(1)}, s32[8,128]{1,0:T(8,128)S(1)}, s32[16,128]{1,0:T(8,128)S(1)}, f32[80,128]{1,0:T(8,128)S(1)}) custom-call(f32[2,320,128]{2,1,0:T(8,128)S(1)} %get-tuple-element.29.own, f32[336,128]{1,0:T(8,128)S(1)} %collective-permute-done.r_a, ...), custom_call_target="tpu_custom_call" | custom-call | flops 10000 | bytes 10000 | tf_op jit(solution)/shard_map/pallas_call | solution.py:485
  11.3 0.1 collective-permute-start.3
  11.3 1.2 %shard_map.67.part = f32[2,320,128]{2,1,0:T(8,128)S(1)} custom-call(f32[2,320,128]{2,1,0:T(8,128)S(1)} %get-tuple-element.34.fld.rest_0_, s32[6,256]{1,0:T(8,128)S(1)} %get-tuple-element.35.nb_ref, s32[6,256]{1,0:T(8,128)S(1)} %get-tuple-element.36.ori_ref, f32[1,256]{1,0:T(1,128)S(1)} %get-tuple-element.37.coef_ref, ...), custom_call_target="tpu_custom_call" | custom-call | flops 20000 | bytes 20000 | tf_op jit(solution)/shard_map/pallas_call | solution.py:485
  12.5 0.0 collective-permute-done.3.r_a
  12.5 0.7 %shard_map.68 = (f32[2,320,128]{2,1,0:T(8,128)S(1)}, f32[96,128]{1,0:T(8,128)S(1)}) custom-call(f32[2,320,128]{2,1,0:T(8,128)S(1)} %shard_map.67.part, f32[80,128]{1,0:T(8,128)S(1)} %get-tuple-element.39.g, f32[80,128]{1,0:T(8,128)S(1)} %collective-permute-done.3.r_a, s32[16,128]{1,0:T(8,128)S(1)} %get-tuple-element.40.info, ...), custom_call_target="tpu_custom_call" | custom-call | flops 10000 | bytes 10000 | tf_op jit(solution)/shard_map/pallas_call | solution.py:485
  13.3 5.8 %collective-permute-start.4 = (f32[96,128]{1,0:T(8,128)S(1)}, f32[96,128]{1,0:T(8,128)S(1)}, u32[]{:S(2)}, u32[]{:S(2)}) collective-permute-start(f32[96,128]{1,0:T(8,128)S(1)} %get-tuple-element.45), channel_id=1, source_target_pairs={{0,31},{1,2},{2,1},{3,4},{4,3},{5,6},{6,5},{7,8},{8,7},{9,10},{10,... | collective-permute-start | bytes 147464 | tf_op jit(solution)/shard_map/ppermute | solution.py:586
  19.1 0.1 shard_map.69.pairs
  19.2 1.7 %collective-permute-done.4.r_b = f32[96,128]{1,0:T(8,128)S(1)} collective-permute-done((f32[96,128]{1,0:T(8,128)S(1)}, f32[96,128]{1,0:T(8,128)S(1)}, u32[]{:S(2)}, u32[]{:S(2)}) %collective-permute-start.4) | collective-permute-done | bytes 49184 | tf_op jit(solution)/shard_map/ppermute | solution.py:586
  20.9 0.7 %shard_map.70 = (f32[2,320,128]{2,1,0:T(8,128)S(1)}, f32[80,128]{1,0:T(8,128)S(1)}, f32[80,128]{1,0:T(8,128)S(1)}) custom-call(f32[2,320,128]{2,1,0:T(8,128)S(1)} %get-tuple-element.44.after.fp, f32[80,128]{1,0:T(8,128)S(1)} %get-tuple-element.39.g, f32[96,128]{1,0:T(8,128)S(1)} %collective-permute-done.4.r_b, s32[16,128]{1,0:T(8,128)S(1)} %get-tuple-element.40.info, ...), custom_call_target="tpu_custom_call" | custom-call | flops 10000 | bytes 10000 | tf_op jit(solution)/shard_map/pallas_call | solution.py:485
  21.6 0.1 collective-permute-start.5
  21.6 1.2 %shard_map.71.part = f32[2,320,128]{2,1,0:T(8,128)S(1)} custom-call(f32[2,320,128]{2,1,0:T(8,128)S(1)} %get-tuple-element.46.fld, s32[6,256]{1,0:T(8,128)S(1)} %get-tuple-element.35.nb_ref, s32[6,256]{1,0:T(8,128)S(1)} %get-tuple-element.36.ori_ref, f32[1,256]{1,0:T(1,128)S(1)} %get-tuple-element.37.coef_ref, bf16[128,192]{1,0:T(8,128)(2,1)S(1)} %get-tuple-element.38.dd_ref, ...), custom_call_target="tpu_custom_call" | custom-call | flops 20000 | bytes 20000 | tf_op jit(solution)/shard_map/pallas_call | solution.py:485
  22.9 0.0 collective-permute-done.5.r_a
  22.9 1.1 %shard_map.72 = f32[5,64,256]{2,1,0:T(8,128)} custom-call(f32[2,320,128]{2,1,0:T(8,128)S(1)} %shard_map.71.part, f32[80,128]{1,0:T(8,128)S(1)} %get-tuple-element.47.g1, f32[80,128]{1,0:T(8,128)S(1)} %collective-permute-done.5.r_a, f32[80,128]{1,0:T(8,128)S(1)} %get-tuple-element.48.o1, s32[16,128]{1,0:T(8,128)S(1)} %get-tuple-element.40.info, ...), custom_call_target="tpu_custom_call" | custom-call | flops 10000 | bytes 10000 | tf_op jit(solution)/shard_map/pallas_call | solution.py:485
Async XLA Ops:
  1.7 9.3 %collective-permute-start = (f32[336,128]{1,0:T(8,128)S(1)}, f32[336,128]{1,0:T(8,128)S(1)}, u32[]{:S(2)}, u32[]{:S(2)}) collective-permute-start(f32[336,128]{1,0:T(8,128)S(1)} %get-tuple-element.30), channel_id=1, source_target_pairs={{0,1},{1,0},{2,3},{3,2},{4,5},{5,4},{6,7},{7,6},{8,9},{9,8},{10,11... | collective-permute-start | bytes 516104 | tf_op jit(solution)/shard_map/ppermute | solution.py:528
  2.2 8.8 %collective-permute-start.1 = (f32[320,128]{1,0:T(8,128)S(1)}, f32[320,128]{1,0:T(8,128)S(1)}, u32[]{:S(2)}, u32[]{:S(2)}) collective-permute-start(f32[320,128]{1,0:T(8,128)S(1)} %get-tuple-element.31), channel_id=1, source_target_pairs={{1,2},{2,1},{3,4},{4,3},{5,6},{6,5},{7,8},{8,7},{9,10},{10,9},{11,... | collective-permute-start | bytes 491528 | tf_op jit(solution)/shard_map/ppermute | solution.py:530
  2.9 8.1 %collective-permute-start.2 = (f32[16,128]{1,0:T(8,128)S(1)}, f32[16,128]{1,0:T(8,128)S(1)}, u32[]{:S(2)}, u32[]{:S(2)}) collective-permute-start(f32[16,128]{1,0:T(8,128)S(1)} %get-tuple-element.32.rows_ref), channel_id=1, source_target_pairs={{0,31},{1,2},{2,1},{3,4},{4,3},{5,6},{6,5},{7,8},{8,7},{9,10},{10,... | collective-permute-start | bytes 24584 | tf_op jit(solution)/shard_map/ppermute | solution.py:529
  11.3 1.3 %collective-permute-start.3 = (f32[80,128]{1,0:T(8,128)S(1)}, f32[80,128]{1,0:T(8,128)S(1)}, u32[]{:S(2)}, u32[]{:S(2)}) collective-permute-start(f32[80,128]{1,0:T(8,128)S(1)} %get-tuple-element.39.g), channel_id=1, source_target_pairs={{0,1},{1,0},{2,3},{3,2},{4,5},{5,4},{6,7},{7,6},{8,9},{9,8},{10,11... | collective-permute-start | bytes 122888 | tf_op jit(solution)/shard_map/ppermute | solution.py:577
  13.3 7.6 %collective-permute-start.4 = (f32[96,128]{1,0:T(8,128)S(1)}, f32[96,128]{1,0:T(8,128)S(1)}, u32[]{:S(2)}, u32[]{:S(2)}) collective-permute-start(f32[96,128]{1,0:T(8,128)S(1)} %get-tuple-element.45), channel_id=1, source_target_pairs={{0,31},{1,2},{2,1},{3,4},{4,3},{5,6},{6,5},{7,8},{8,7},{9,10},{10,... | collective-permute-start | bytes 147464 | tf_op jit(solution)/shard_map/ppermute | solution.py:586
  21.6 1.3 %collective-permute-start.5 = (f32[80,128]{1,0:T(8,128)S(1)}, f32[80,128]{1,0:T(8,128)S(1)}, u32[]{:S(2)}, u32[]{:S(2)}) collective-permute-start(f32[80,128]{1,0:T(8,128)S(1)} %get-tuple-element.47.g1), channel_id=1, source_target_pairs={{0,1},{1,0},{2,3},{3,2},{4,5},{5,4},{6,7},{7,6},{8,9},{9,8},{10,11... | collective-permute-start | bytes 122888 | tf_op jit(solution)/shard_map/ppermute | solution.py:595

commit v5 on v4

--- a/solution.py
+++ b/solution.py
@@ -231,7 +231,9 @@
         g[16 * v : 16 * v + 16, :] = chosen(gs, face, v)
 
 
-def join_kernel(sizes, own, r_a, r_b, c_b, rows_ref, edge, fld, hot_ref, code_ref, info, g, gs):
+def join_kernel(
+    sizes, own, r_a, r_b, c_b, rows_ref, edge, col_ref, fld, hot_ref, code_ref, info, meet, g, gs
+):
     even = (rank_of(sizes) & 1) == 0
     lane = iota((NODES, LANES), 1)
     below = lane < edge[0:1, :]
@@ -257,6 +259,9 @@
     hot_ref[...] = hot
     face = jnp.broadcast_to(code[0:1, :] >> 8, (16, LANES))
     requested(fld, hot, face, gs, g)
+    same = (col_ref[...].astype(I32) & 255) == jnp.broadcast_to(code[0:1, :] & 255, (64, LANES))
+    meet[0:64, :] = jnp.where(same, 1.0, 0.0).astype(BF)
+    meet[64:128, :] = jnp.zeros((64, LANES), BF)
 
 
 def fluxes(u, speeds, p):
@@ -297,7 +302,13 @@
 
 def local_kernel(sizes, last, fld, nb_ref, ori_ref, coef_ref, dd_ref, *rest):
     if last:
-        old_fld, part, acc, ax, ay, az, xs, xg, xq, xo, xc, it = rest
+        old_fld, e, ohs, part, acc, ax, ay, az, xs, xg, xq, xo, xc, it, first = rest
+
+        def put(h, v, new):
+            first[h, v * NODES : v * NODES + NODES, :] = new
+
+        added(fld, mm(e[...], ohs[...]), coef_ref, LIFT, put)
+        fld = first
     else:
         part, acc, ax, ay, az, xs, xg, xq, xo, xc, it = rest
     for ref in (ax, ay, az):
@@ -406,64 +417,62 @@
             put(h, v, part[h, rows, :] - coef * (spread[rows, lanes] + spread[low, lanes]))
 
 
-def near_kernel(part, g, r_a, info, ohs, coef_ref, hot_ref, code_ref, fp, pb, ro, y, ex, ey, ez, g1):
-    lane = iota((16, LANES), 1)
-    parts = face_terms(pltpu.roll(g[...], 64, 1), r_a[...], info, lane < 32, ro, y, ex, ey, ez)
-    spread = mm(parts, ohs[...])
-
-    def put(h, v, new):
-        fp[h, v * NODES : v * NODES + NODES, :] = new
-
-    added(part, spread, coef_ref, LIFT, put)
+def near_kernel(
+    part, g, r_a, info, meet, coef_ref, hot_ref, code_ref, parts, q, pb, ro, y, ex, ey, ez, gs, g1
+):
     hot = hot_ref[...]
     asked = jnp.broadcast_to(code_ref[0:1, :] >> 8, (16, LANES))
-    requested(fp, hot, asked, ex, g1)
-    lane = iota((80, LANES), 1)
-    pb[0:80, :] = jnp.where(lane < 32, pltpu.roll(g1[...], 96, 1), g[...])
+    requested(part, hot, asked, gs, g1)
     ch, cl = split(jnp.broadcast_to(LIFT * coef_ref[0:1, :], (16, EL)))
-    pb[80:96, :] = mm(ch, hot) + mm(cl, hot)
-
-
-def pair_kernel(info, rows_ref, after, pairs):
+    coef = mm(ch, hot) + mm(cl, hot)
+    lane = iota((16, LANES), 1)
+    terms = face_terms(pltpu.roll(g[...], 64, 1), r_a[...], info, lane < 32, ro, y, ex, ey, ez)
+    parts[...] = terms
+    change = mm(terms, meet[...])
+    ex[...] = change[0:ROWS, :] + change[ROWS : 2 * ROWS, :]
+    for v in range(VARS):
+        rows = slice(16 * v, 16 * v + 16)
+        new = g1[rows, :] - coef * chosen(ex, asked, v)
+        q[rows, :] = new
+        pb[rows, :] = jnp.where(lane < 32, pltpu.roll(new, 96, 1), g[rows, :])
+    pb[80:96, :] = coef
+
+
+def pair_kernel(info, rows_ref, meet, after, pairs):
     theirs = jnp.transpose(jnp.broadcast_to(info[0:1, :].astype(F32), (LANES, LANES))).astype(I32)
     mine = jnp.broadcast_to(rows_ref[0:1, :].astype(I32), (LANES, LANES))
     row, lane = iota((LANES, LANES), 0), iota((LANES, LANES), 1)
-    on = ((theirs & 255) == (mine & 255)) & (row >= 96) & (lane >= 32) & (lane < 64)
-    pairs[...] = jnp.where(on, 1.0, 0.0).astype(BF)
-
-
-def far_kernel(
-    fp, g, r_b, info, rows_ref, ohs, pairs, coef_ref, hot_ref, code_ref, first, g1, o1, ro, y, ex, ey, ez
-):
+    to_b = (lane >= 32) & (lane < 64)
+    on = ((theirs & 255) == (mine & 255)) & (row >= 96) & to_b
+    kept = jnp.where(to_b, 0.0, meet[...].astype(F32))
+    pairs[...] = jnp.where(on, 1.0, kept).astype(BF)
+
+
+def far_kernel(g, q1, pb, r_b, info, rows_ref, code_ref, pairs, e1, q, e, ro, y, ex, ey, ez):
     lane = iota((80, LANES), 1)
     mine = pltpu.roll(g[...], 64, 1)
     got = r_b[0:80, :]
     lane16 = iota((16, LANES), 1)
-    live = ((lane16 >= 32) & (lane16 < 64)) | (lane16 >= 96)
+    to_b = (lane16 >= 32) & (lane16 < 64)
     inner, outer = jnp.where(lane < 64, mine, got), jnp.where(lane < 64, got, mine)
-    parts = face_terms(inner, outer, info, live, ro, y, ex, ey, ez)
-    spread = mm(parts, ohs[...])
-
-    def put(h, v, new):
-        first[h, v * NODES : v * NODES + NODES, :] = new
-
-    added(fp, spread, coef_ref, LIFT, put)
-    theirs = mm(parts, pairs[...])
-    ey[...] = theirs[0:ROWS, :] + theirs[ROWS : 2 * ROWS, :]
-    face = jnp.broadcast_to(rows_ref[0:1, :].astype(I32) >> 8, (16, LANES))
-    coef = r_b[80:81, :]
+    terms = face_terms(inner, outer, info, to_b | (lane16 >= 96), ro, y, ex, ey, ez)
+    e[...] = e1[...] + terms
+    change = mm(terms, pairs[...])
+    ex[...] = change[0:ROWS, :] + change[ROWS : 2 * ROWS, :]
+    code = jnp.where(to_b[0:1, :], rows_ref[0:1, :].astype(I32), code_ref[0:1, :])
+    face = jnp.broadcast_to(code >> 8, (16, LANES))
+    coef = jnp.where(to_b, r_b[80:96, :], pb[80:96, :])
     for v in range(VARS):
         rows = slice(16 * v, 16 * v + 16)
-        o1[rows, :] = pltpu.roll(r_b[rows, :], 32, 1) - coef * chosen(ey, face, v)
-    asked = jnp.broadcast_to(code_ref[0:1, :] >> 8, (16, LANES))
-    requested(first, hot_ref[...], asked, ex, g1)
-
-
-def last_kernel(part, g1, r_a, o1, info, ohs, coef_ref, out, ro, y, ex, ey, ez):
+        base = jnp.where(to_b, pltpu.roll(r_b[rows, :], 32, 1), q1[rows, :])
+        q[rows, :] = base - coef * chosen(ex, face, v)
+
+
+def last_kernel(part, q, r_a, info, ohs, coef_ref, out, ro, y, ex, ey, ez):
     lane = iota((80, LANES), 1)
-    outer = jnp.where(lane < 32, r_a[...], o1[...])
+    outer = jnp.where(lane < 32, r_a[...], q[...])
     live = iota((16, LANES), 1) < 64
-    parts = face_terms(pltpu.roll(g1[...], 64, 1), outer, info, live, ro, y, ex, ey, ez)
+    parts = face_terms(pltpu.roll(q[...], 64, 1), outer, info, live, ro, y, ex, ey, ez)
     spread = mm(parts, ohs[...])
 
     def put(h, v, new):
@@ -550,56 +559,62 @@
     square = pltpu.VMEM((LANES + 24, LANES), F32)
     traces = shape(80, LANES)
     state = shape(2, ROWS, LANES)
-    fld, hot, code, info, g = call(
+    fld, hot, code, info, meet, g = call(
         functools.partial(join_kernel, sizes),
         (
             state,
             shape(EL, LANES, dtype=BF),
             shape(8, LANES, dtype=I32),
             shape(16, LANES, dtype=I32),
+            shape(LANES, LANES, dtype=BF),
             traces,
         ),
         [table],
         10000,
-        (own, r_a, r_b, c_b, rows, edge),
+        (own, r_a, r_b, c_b, rows, edge, col),
     )
 
     def local(last, *args):
         faces = pltpu.VMEM((VARS * TABLE + 8, LANES), F32)
+        both = pltpu.VMEM((2, ROWS, LANES), F32)
         return call(
             functools.partial(local_kernel, sizes, last),
             state,
-            [pltpu.VMEM((2, ROWS, LANES), F32)] * 4 + [faces] * 5 + [pltpu.VMEM((32, LANES), I32)],
+            [both] * 4 + [faces] * 5 + [pltpu.VMEM((32, LANES), I32)] + ([both] if last else []),
             20000,
             args,
         )
 
     r_a = lax.ppermute(g, AXES, pairs_a)
     part = local(False, fld, nb_v, ori_v, coef, dd)
-    fp, pb = call(
+    terms = shape(2 * ROWS, LANES, dtype=BF)
+    scratch = [square, square, table, table, table]
+    e1, q1, pb = call(
         near_kernel,
-        (state, shape(96, LANES)),
-        [square, square, table, table, table, pltpu.VMEM((80, LANES), F32)],
+        (terms, traces, shape(96, LANES)),
+        scratch + [table, pltpu.VMEM((80, LANES), F32)],
         10000,
-        (part, g, r_a, info, ohs, coef, hot, code),
+        (part, g, r_a, info, meet, coef, hot, code),
     )
     r_b = lax.ppermute(pb, AXES, pairs_b)
-    pairs = call(pair_kernel, shape(LANES, LANES, dtype=BF), [], 10000, (info, rows, fp))
-    first, g1, o1 = call(
+    pairs = call(
+        pair_kernel, shape(LANES, LANES, dtype=BF), [], 10000, (info, rows, meet, q1)
+    )
+    q, e = call(
         far_kernel,
-        (state, traces, traces),
-        [square, square, table, table, table],
+        (traces, terms),
+        scratch,
         10000,
-        (fp, g, r_b, info, rows, ohs, pairs, coef, hot, code),
-    )
-    r_a = lax.ppermute(g1, AXES, pairs_a)
-    part = local(True, first, nb_v, ori_v, coef, dd, fld)
+        (g, q1, pb, r_b, info, rows, code, pairs, e1),
+    )
+    r_a = lax.ppermute(q, AXES, pairs_a)
+    part = local(True, part, nb_v, ori_v, coef, dd, fld, e, ohs)
     return call(
         last_kernel,
         shape(VARS, NODES, EL),
-        [square, square, table, table, table],
+        scratch,
         10000,
-        (part, g1, r_a, o1, info, ohs, coef),
+        (part, q, r_a, info, ohs, coef),
     )
 
 

time: 24.2 us -> 23.8 us (0.983)
  Pallas kernels: 7.79 us -> 7.4 us
    pallas_call x9, Pallas kernels: 7.79 us -> 7.4 us  [call(): pl.pallas_call(body, out_shape=out_shape, in_specs=specs, out_specs=jax.t...]
  transfers between devices with their start and end apart: 6 -> 6, of which waited for: 2 -> 2; matrix products, arithmetic and copies ran while one was open for 0% -> 0% of each run, Pallas kernels for 14% -> 15%
where the time goes in v5:
time: 23.8 us; the launch traced here: 23.6 us
  starting transfers between devices  13.9 us (58%)
  Pallas kernels  7.4 us (31%)
  waiting for transfers between devices  2.21 us (9%)
    pallas_call x9, Pallas kernels, call(): pl.pallas_call(body, out_shape=out_shape, in_specs=specs, out_specs=jax.t...  7.4 us
    ppermute x1, starting transfers between devices, per_device(): c_b = lax.ppermute(rows, AXES, pairs_b)  6.66 us
    ppermute x1, starting transfers between devices, per_device(): r_b = lax.ppermute(pb, AXES, pairs_b)  5.89 us
    ppermute x1, waiting for transfers between devices, per_device(): r_b = lax.ppermute(pb, AXES, pairs_b)  1.67 us
    ppermute x1, starting transfers between devices, per_device(): r_b = lax.ppermute(s_b, AXES, pairs_b[1:-1])  0.66 us
    ppermute x1, waiting for transfers between devices, per_device(): c_b = lax.ppermute(rows, AXES, pairs_b)  0.53 us
    ppermute x1, starting transfers between devices, per_device(): r_a = lax.ppermute(s_a, AXES, pairs_a)  0.52 us
  transfers between devices with their start and end apart: 6, of which 2 were waited for; matrix products, arithmetic and copies ran while one was open for 0% of the time, Pallas kernels for 15%

profile of v5, /device:TPU:0, one launch (start us, length us, event | category | flops | bytes accessed | tf_op | source)
XLA Modules:
  0.0 23.6 jit_solution(3715854830518993255)
XLA Ops:
  0.0 1.7 %shard_map.64 = (f32[336,128]{1,0:T(8,128)S(1)}, f32[320,128]{1,0:T(8,128)S(1)}, f32[16,128]{1,0:T(8,128)S(1)}, f32[64,128]{1,0:T(8,128)S(1)}, f32[5,64,512]{2,1...) custom-call(s32[33]{0:T(128)} %start_hbm.3, f32[5,64,512]{2,1,0:T(8,128)} %old.1, ...), custom_call_target="tpu_custom_call" | custom-call | flops 10000 | bytes 10000 | tf_op jit(solution)/shard_map/pallas_call | solution.py:494
  1.7 0.5 %collective-permute-start = (f32[336,128]{1,0:T(8,128)S(1)}, f32[336,128]{1,0:T(8,128)S(1)}, u32[]{:S(2)}, u32[]{:S(2)}) collective-permute-start(f32[336,128]{1,0:T(8,128)S(1)} %get-tuple-element.31), channel_id=1, source_target_pairs={{0,1},{1,0},{2,3},{3,2},{4,5},{5,4},{6,7},{7,6},{8,9},{9,8},{10,11... | collective-permute-start | bytes 516104 | tf_op jit(solution)/shard_map/ppermute | solution.py:537
  2.2 0.7 %collective-permute-start.1 = (f32[320,128]{1,0:T(8,128)S(1)}, f32[320,128]{1,0:T(8,128)S(1)}, u32[]{:S(2)}, u32[]{:S(2)}) collective-permute-start(f32[320,128]{1,0:T(8,128)S(1)} %get-tuple-element.32), channel_id=1, source_target_pairs={{1,2},{2,1},{3,4},{4,3},{5,6},{6,5},{7,8},{8,7},{9,10},{10,9},{11,... | collective-permute-start | bytes 491528 | tf_op jit(solution)/shard_map/ppermute | solution.py:539
  2.9 6.7 %collective-permute-start.2 = (f32[16,128]{1,0:T(8,128)S(1)}, f32[16,128]{1,0:T(8,128)S(1)}, u32[]{:S(2)}, u32[]{:S(2)}) collective-permute-start(f32[16,128]{1,0:T(8,128)S(1)} %get-tuple-element.33.rows_ref), channel_id=1, source_target_pairs={{0,31},{1,2},{2,1},{3,4},{4,3},{5,6},{6,5},{7,8},{8,7},{9,10},{10,... | collective-permute-start | bytes 24584 | tf_op jit(solution)/shard_map/ppermute | solution.py:538
  9.5 0.9 %shard_map.65 = (f32[2,320,128]{2,1,0:T(8,128)S(1)}, bf16[128,256]{1,0:T(8,128)(2,1)S(1)}, bf16[128,192]{1,0:T(8,128)(2,1)S(1)}, f32[1,256]{1,0:T(1,128)S(1)}) custom-call(s32[33]{0:T(128)} %start_hbm.3, f32[5,64,512]{2,1,0:T(8,128)S(1)} %get-tuple-element.28.old, f32[64,128]{1,0:T(8,128)S(1)} %get-tuple-element.29.col_ref, f32[64,192]{1,0:T(8,128)} %constant.2.clone.d_hbm, ...), custom_call_target="tpu_custom_call" | custom-call | flops 10000 | bytes 10000 | tf_op jit(solution)/shard_map/pallas_call | solution.py:494
  10.4 0.5 %collective-permute-done.2.c_b = f32[16,128]{1,0:T(8,128)S(1)} collective-permute-done((f32[16,128]{1,0:T(8,128)S(1)}, f32[16,128]{1,0:T(8,128)S(1)}, u32[]{:S(2)}, u32[]{:S(2)}) %collective-permute-start.2) | collective-permute-done | bytes 8224 | tf_op jit(solution)/shard_map/ppermute | solution.py:538
  11.0 0.0 collective-permute-done.1.r_b
  11.0 0.0 collective-permute-done.r_a
  11.0 0.3 %shard_map.66 = (f32[2,320,128]{2,1,0:T(8,128)S(1)}, bf16[256,128]{1,0:T(8,128)(2,1)S(1)}, s32[8,128]{1,0:T(8,128)S(1)}, s32[16,128]{1,0:T(8,128)S(1)}, bf16[128...) custom-call(f32[2,320,128]{2,1,0:T(8,128)S(1)} %get-tuple-element.30.own, f32[336,128]{1,0:T(8,128)S(1)} %collective-permute-done.r_a, ...), custom_call_target="tpu_custom_call" | custom-call | flops 10000 | bytes 10000 | tf_op jit(solution)/shard_map/pallas_call | solution.py:494
  11.3 0.1 collective-permute-start.3
  11.3 1.2 %shard_map.67.part.fld = f32[2,320,128]{2,1,0:T(8,128)S(1)} custom-call(f32[2,320,128]{2,1,0:T(8,128)S(1)} %get-tuple-element.35.fld.rest_0_, s32[6,256]{1,0:T(8,128)S(1)} %get-tuple-element.36.nb_ref, s32[6,256]{1,0:T(8,128)S(1)} %get-tuple-element.37.ori_ref, f32[1,256]{1,0:T(1,128)S(1)} %get-tuple-element.38.coef_ref, ...), custom_call_target="tpu_custom_call" | custom-call | flops 20000 | bytes 20000 | tf_op jit(solution)/shard_map/pallas_call | solution.py:494
  12.5 0.0 collective-permute-done.3.r_a
  12.6 0.4 %shard_map.68 = (bf16[640,128]{1,0:T(8,128)(2,1)S(1)}, f32[80,128]{1,0:T(8,128)S(1)}, f32[96,128]{1,0:T(8,128)S(1)}) custom-call(f32[2,320,128]{2,1,0:T(8,128)S(1)} %shard_map.67.part.fld, f32[80,128]{1,0:T(8,128)S(1)} %get-tuple-element.40.g, f32[80,128]{1,0:T(8,128)S(1)} %collective-permute-done.3.r_a, s32[16,128]{1,0:T(8,128)S(1)} %get-tuple-element.41.info, ...), custom_call_target="tpu_custom_call" | custom-call | flops 10000 | bytes 10000 | tf_op jit(solution)/shard_map/pallas_call | solution.py:494
  13.0 5.9 %collective-permute-start.4 = (f32[96,128]{1,0:T(8,128)S(1)}, f32[96,128]{1,0:T(8,128)S(1)}, u32[]{:S(2)}, u32[]{:S(2)}) collective-permute-start(f32[96,128]{1,0:T(8,128)S(1)} %get-tuple-element.46.pb), channel_id=1, source_target_pairs={{0,31},{1,2},{2,1},{3,4},{4,3},{5,6},{6,5},{7,8},{8,7},{9,10},{10,... | collective-permute-start | bytes 147464 | tf_op jit(solution)/shard_map/ppermute | solution.py:599
  18.9 0.1 shard_map.69.pairs
  19.0 1.7 %collective-permute-done.4.r_b = f32[96,128]{1,0:T(8,128)S(1)} collective-permute-done((f32[96,128]{1,0:T(8,128)S(1)}, f32[96,128]{1,0:T(8,128)S(1)}, u32[]{:S(2)}, u32[]{:S(2)}) %collective-permute-start.4) | collective-permute-done | bytes 49184 | tf_op jit(solution)/shard_map/ppermute | solution.py:599
  20.7 0.3 %shard_map.70 = (f32[80,128]{1,0:T(8,128)S(1)}, bf16[640,128]{1,0:T(8,128)(2,1)S(1)}) custom-call(f32[80,128]{1,0:T(8,128)S(1)} %get-tuple-element.40.g, f32[80,128]{1,0:T(8,128)S(1)} %get-tuple-element.45.after.q1, f32[96,128]{1,0:T(8,128)S(1)} %get-tuple-element.46.pb, f32[96,128]{1,0:T(8,128)S(1)} %collective-permute-done.4.r_b, ...), custom_call_target="tpu_custom_call" | custom-call | flops 10000 | bytes 10000 | tf_op jit(solution)/shard_map/pallas_call | solution.py:494
  21.0 0.1 collective-permute-start.5
  21.1 1.4 %shard_map.71.part = f32[2,320,128]{2,1,0:T(8,128)S(1)} custom-call(f32[2,320,128]{2,1,0:T(8,128)S(1)} %shard_map.67.part.fld, s32[6,256]{1,0:T(8,128)S(1)} %get-tuple-element.36.nb_ref, s32[6,256]{1,0:T(8,128)S(1)} %get-tuple-element.37.ori_ref, f32[1,256]{1,0:T(1,128)S(1)} %get-tuple-element.38.coef_ref, bf16[128,192]{1,0:T(8,128)(2,1)S(1)} %get-tuple-element.39.dd_ref, ...), custom_call_target="tpu_custom_call" | custom-call | flops 20000 | bytes 20000 | tf_op jit(solution)/shard_map/pallas_call | solution.py:494
  22.5 0.0 collective-permute-done.5.r_a
  22.5 1.1 %shard_map.72 = f32[5,64,256]{2,1,0:T(8,128)} custom-call(f32[2,320,128]{2,1,0:T(8,128)S(1)} %shard_map.71.part, f32[80,128]{1,0:T(8,128)S(1)} %get-tuple-element.50.q, f32[80,128]{1,0:T(8,128)S(1)} %collective-permute-done.5.r_a, s32[16,128]{1,0:T(8,128)S(1)} %get-tuple-element.41.info, bf16[128,256]{1,0:T(8,128)(2,1)S(1)} %get-tuple-element.49.rest_2_.ohs, ...), custom_call_target="tpu_custom_call" | custom-call | flops 10000 | bytes 10000 | tf_op jit(solution)/shard_map/pallas_call | solution.py:494
Async XLA Ops:
  1.7 9.3 %collective-permute-start = (f32[336,128]{1,0:T(8,128)S(1)}, f32[336,128]{1,0:T(8,128)S(1)}, u32[]{:S(2)}, u32[]{:S(2)}) collective-permute-start(f32[336,128]{1,0:T(8,128)S(1)} %get-tuple-element.31), channel_id=1, source_target_pairs={{0,1},{1,0},{2,3},{3,2},{4,5},{5,4},{6,7},{7,6},{8,9},{9,8},{10,11... | collective-permute-start | bytes 516104 | tf_op jit(solution)/shard_map/ppermute | solution.py:537
  2.2 8.8 %collective-permute-start.1 = (f32[320,128]{1,0:T(8,128)S(1)}, f32[320,128]{1,0:T(8,128)S(1)}, u32[]{:S(2)}, u32[]{:S(2)}) collective-permute-start(f32[320,128]{1,0:T(8,128)S(1)} %get-tuple-element.32), channel_id=1, source_target_pairs={{1,2},{2,1},{3,4},{4,3},{5,6},{6,5},{7,8},{8,7},{9,10},{10,9},{11,... | collective-permute-start | bytes 491528 | tf_op jit(solution)/shard_map/ppermute | solution.py:539
  2.9 8.1 %collective-permute-start.2 = (f32[16,128]{1,0:T(8,128)S(1)}, f32[16,128]{1,0:T(8,128)S(1)}, u32[]{:S(2)}, u32[]{:S(2)}) collective-permute-start(f32[16,128]{1,0:T(8,128)S(1)} %get-tuple-element.33.rows_ref), channel_id=1, source_target_pairs={{0,31},{1,2},{2,1},{3,4},{4,3},{5,6},{6,5},{7,8},{8,7},{9,10},{10,... | collective-permute-start | bytes 24584 | tf_op jit(solution)/shard_map/ppermute | solution.py:538
  11.3 1.3 %collective-permute-start.3 = (f32[80,128]{1,0:T(8,128)S(1)}, f32[80,128]{1,0:T(8,128)S(1)}, u32[]{:S(2)}, u32[]{:S(2)}) collective-permute-start(f32[80,128]{1,0:T(8,128)S(1)} %get-tuple-element.40.g), channel_id=1, source_target_pairs={{0,1},{1,0},{2,3},{3,2},{4,5},{5,4},{6,7},{7,6},{8,9},{9,8},{10,11... | collective-permute-start | bytes 122888 | tf_op jit(solution)/shard_map/ppermute | solution.py:588
  13.0 7.7 %collective-permute-start.4 = (f32[96,128]{1,0:T(8,128)S(1)}, f32[96,128]{1,0:T(8,128)S(1)}, u32[]{:S(2)}, u32[]{:S(2)}) collective-permute-start(f32[96,128]{1,0:T(8,128)S(1)} %get-tuple-element.46.pb), channel_id=1, source_target_pairs={{0,31},{1,2},{2,1},{3,4},{4,3},{5,6},{6,5},{7,8},{8,7},{9,10},{10,... | collective-permute-start | bytes 147464 | tf_op jit(solution)/shard_map/ppermute | solution.py:599
  21.0 1.5 %collective-permute-start.5 = (f32[80,128]{1,0:T(8,128)S(1)}, f32[80,128]{1,0:T(8,128)S(1)}, u32[]{:S(2)}, u32[]{:S(2)}) collective-permute-start(f32[80,128]{1,0:T(8,128)S(1)} %get-tuple-element.50.q), channel_id=1, source_target_pairs={{0,1},{1,0},{2,3},{3,2},{4,5},{5,4},{6,7},{7,6},{8,9},{9,8},{10,11... | collective-permute-start | bytes 122888 | tf_op jit(solution)/shard_map/ppermute | solution.py:610

commit v6 on v5

--- a/solution.py
+++ b/solution.py
@@ -117,7 +117,8 @@
         pltpu.make_async_copy(nb, nb_v, sem.at[0]),
         pltpu.make_async_copy(ori, ori_v, sem.at[1]),
         pltpu.make_async_copy(start_hbm, start, sem.at[2]),
-    ] + [pltpu.make_async_copy(old.at[v], old_v.at[v], sem.at[3 + v]) for v in range(VARS)]
+        pltpu.make_async_copy(old, old_v, sem.at[3]),
+    ]
     for copy in copies:
         copy.start()
     d = rank_of(sizes)
@@ -275,23 +276,25 @@
 
 
 def directed(u, axis_is):
-    inv = 1.0 / u[0]
-    p = 0.4 * (u[4] - 0.5 * ((u[1] * u[1] + u[2] * u[2] + u[3] * u[3]) * inv))
+    inv = pl.reciprocal(u[0])
+    p = 0.4 * u[4] - 0.2 * ((u[1] * u[1] + u[2] * u[2] + u[3] * u[3]) * inv)
     mom = jnp.where(axis_is[0], u[1], jnp.where(axis_is[1], u[2], u[3]))
     s = mom * inv
-    flux = [u[0] * s] + [u[i] * s for i in range(1, 4)] + [(u[4] + p) * s]
-    zero = jnp.zeros_like(p)
-    flux[1] = flux[1] + jnp.where(axis_is[0], p, zero)
-    flux[2] = flux[2] + jnp.where(axis_is[1], p, zero)
-    flux[3] = flux[3] + jnp.where(axis_is[0] | axis_is[1], zero, p)
-    return flux, jnp.abs(s) + jnp.sqrt(1.4 * p * inv)
-
-
-def correction(inner, outer, axis_is, half_sign):
-    fi, si = directed(inner, axis_is)
-    fo, so = directed(outer, axis_is)
-    lam = 0.5 * jnp.maximum(si, so)
-    return [half_sign * (fo[v] - fi[v]) - lam * (outer[v] - inner[v]) for v in range(VARS)]
+    return p, mom, s, jnp.abs(s) + jnp.sqrt(1.4 * (p * inv))
+
+
+def correction(inner, outer, axis_is, sign_scale, scale):
+    pi, mi, si, ci = directed(inner, axis_is)
+    po, mo, so, co = directed(outer, axis_is)
+    lam = scale * jnp.maximum(ci, co)
+    dp = po - pi
+    along = (axis_is[0], axis_is[1], jnp.logical_not(axis_is[0] | axis_is[1]))
+    flux = [mo - mi]
+    flux += [
+        (outer[i] * so - inner[i] * si) + jnp.where(along[i - 1], dp, 0.0) for i in range(1, 4)
+    ]
+    flux += [(outer[4] + po) * so - (inner[4] + pi) * si]
+    return [sign_scale * flux[v] - lam * (outer[v] - inner[v]) for v in range(VARS)]
 
 
 def turned(x, b0, b1, b2):
@@ -362,12 +365,13 @@
         for m, x in enumerate(turned(got, b0, b1, b2)):
             xo[pl.ds(v * TABLE + m * PITCH, 12), :] = x[0:12, :]
     axis_is = (row < 4, (row >= 4) & (row < 8))
-    half_sign = jnp.where((row & 2) != 0, 0.5, -0.5)
+    sign_scale = jnp.where((row & 2) != 0, 0.5 * LIFT, -0.5 * LIFT)
     for m in range(16):
         rows = [pl.ds(v * TABLE + m * PITCH, 16) for v in range(VARS)]
-        cor = correction([xs[r, :] for r in rows], [xo[r, :] for r in rows], axis_is, half_sign)
+        inner, outer = [xs[r, :] for r in rows], [xo[r, :] for r in rows]
+        cor = correction(inner, outer, axis_is, sign_scale, 0.5 * LIFT)
         for v in range(VARS):
-            val = jnp.where(local, LIFT * cor[v], 0.0)
+            val = jnp.where(local, cor[v], 0.0)
             xc[pl.ds(v * TABLE + m * PITCH, 12), :] = val[0:12, :]
     for v in range(VARS):
         for f in range(FACES):
@@ -398,7 +402,7 @@
     half_sign = jnp.where((face & 1) != 0, 0.5, -0.5)
     behind = [y[pl.ds(v, 16, stride=9), :] for v in range(VARS)]
     here = [inner[16 * v : 16 * v + 16, :] for v in range(VARS)]
-    cor = correction(here, behind, axis_is, half_sign)
+    cor = correction(here, behind, axis_is, half_sign, 0.5)
     for ref in (ex, ey, ez):
         ref[...] = jnp.zeros((ROWS, LANES), F32)
     for v in range(VARS):
@@ -418,7 +422,7 @@
 
 
 def near_kernel(
-    part, g, r_a, info, meet, coef_ref, hot_ref, code_ref, parts, q, pb, ro, y, ex, ey, ez, gs, g1
+    part, g, r_a, info, meet, coef_ref, hot_ref, code_ref, parts, q, pb, unit, ro, y, ex, ey, ez, gs, g1
 ):
     hot = hot_ref[...]
     asked = jnp.broadcast_to(code_ref[0:1, :] >> 8, (16, LANES))
@@ -434,8 +438,9 @@
         rows = slice(16 * v, 16 * v + 16)
         new = g1[rows, :] - coef * chosen(ex, asked, v)
         q[rows, :] = new
-        pb[rows, :] = jnp.where(lane < 32, pltpu.roll(new, 96, 1), g[rows, :])
-    pb[80:96, :] = coef
+        sent = jnp.where((lane >= 64) & (lane < 96), pltpu.roll(coef, 32, 1), g[rows, :])
+        pb[rows, :] = jnp.where(lane < 32, pltpu.roll(new, 96, 1), sent)
+    unit[...] = coef
 
 
 def pair_kernel(info, rows_ref, meet, after, pairs):
@@ -448,10 +453,10 @@
     pairs[...] = jnp.where(on, 1.0, kept).astype(BF)
 
 
-def far_kernel(g, q1, pb, r_b, info, rows_ref, code_ref, pairs, e1, q, e, ro, y, ex, ey, ez):
+def far_kernel(g, q1, unit, r_b, info, rows_ref, code_ref, pairs, e1, q, e, ro, y, ex, ey, ez):
     lane = iota((80, LANES), 1)
     mine = pltpu.roll(g[...], 64, 1)
-    got = r_b[0:80, :]
+    got = r_b[...]
     lane16 = iota((16, LANES), 1)
     to_b = (lane16 >= 32) & (lane16 < 64)
     inner, outer = jnp.where(lane < 64, mine, got), jnp.where(lane < 64, got, mine)
@@ -461,27 +466,34 @@
     ex[...] = change[0:ROWS, :] + change[ROWS : 2 * ROWS, :]
     code = jnp.where(to_b[0:1, :], rows_ref[0:1, :].astype(I32), code_ref[0:1, :])
     face = jnp.broadcast_to(code >> 8, (16, LANES))
-    coef = jnp.where(to_b, r_b[80:96, :], pb[80:96, :])
+    coef = jnp.where(to_b, pltpu.roll(r_b[0:16, :], 96, 1), unit[...])
     for v in range(VARS):
         rows = slice(16 * v, 16 * v + 16)
         base = jnp.where(to_b, pltpu.roll(r_b[rows, :], 32, 1), q1[rows, :])
         q[rows, :] = base - coef * chosen(ex, face, v)
 
 
-def last_kernel(part, q, r_a, info, ohs, coef_ref, out, ro, y, ex, ey, ez):
+def last_kernel(part, q, r_a, info, ohs, coef_ref, out_hbm, ro, y, ex, ey, ez, out, sem):
     lane = iota((80, LANES), 1)
     outer = jnp.where(lane < 32, r_a[...], q[...])
     live = iota((16, LANES), 1) < 64
     parts = face_terms(pltpu.roll(q[...], 64, 1), outer, info, live, ro, y, ex, ey, ez)
     spread = mm(parts, ohs[...])
-
-    def put(h, v, new):
-        out[v, :, h * LANES : h * LANES + LANES] = new
-
-    added(part, spread, coef_ref, 0.5 * LIFT, put)
-
-
-def call(body, out_shape, scratch, cost, args, hbm=(), spare=None):
+    copies = []
+    for v in range(VARS):
+        for h in range(2):
+            lanes = slice(h * LANES, h * LANES + LANES)
+            rows = slice(v * NODES, v * NODES + NODES)
+            low = slice(ROWS + v * NODES, ROWS + v * NODES + NODES)
+            coef = (0.5 * LIFT) * coef_ref[0:1, lanes]
+            out[v, :, lanes] = part[h, rows, :] - coef * (spread[rows, lanes] + spread[low, lanes])
+        copies.append(pltpu.make_async_copy(out.at[v], out_hbm.at[v], sem.at[v]))
+        copies[v].start()
+    for copy in copies:
+        copy.wait()
+
+
+def call(body, out_shape, scratch, cost, args, hbm=(), out_hbm=False):
     spec = pl.BlockSpec(memory_space=pltpu.VMEM)
     specs = []
     for i, a in enumerate(args):
@@ -495,7 +507,9 @@
         body,
         out_shape=out_shape,
         in_specs=specs,
-        out_specs=jax.tree.map(lambda _: spec, out_shape),
+        out_specs=pl.BlockSpec(memory_space=pltpu.HBM)
+        if out_hbm
+        else jax.tree.map(lambda _: spec, out_shape),
         scratch_shapes=scratch,
         cost_estimate=pl.CostEstimate(flops=cost, bytes_accessed=cost, transcendentals=0),
         compiler_params=pltpu.CompilerParams(vmem_limit_bytes=32 * 1024 * 1024),
@@ -528,7 +542,7 @@
         [
             pltpu.VMEM((16, EL), F32),
             pltpu.SMEM(old_start.shape, I32),
-            pltpu.SemaphoreType.DMA((3 + VARS,)),
+            pltpu.SemaphoreType.DMA((4,)),
         ],
         10000,
         (old_start, old_state, neighbour, orientation),
@@ -589,9 +603,9 @@
     part = local(False, fld, nb_v, ori_v, coef, dd)
     terms = shape(2 * ROWS, LANES, dtype=BF)
     scratch = [square, square, table, table, table]
-    e1, q1, pb = call(
+    e1, q1, pb, unit = call(
         near_kernel,
-        (terms, traces, shape(96, LANES)),
+        (terms, traces, traces, shape(16, LANES)),
         scratch + [table, pltpu.VMEM((80, LANES), F32)],
         10000,
         (part, g, r_a, info, meet, coef, hot, code),
@@ -605,16 +619,17 @@
         (traces, terms),
         scratch,
         10000,
-        (g, q1, pb, r_b, info, rows, code, pairs, e1),
+        (g, q1, unit, r_b, info, rows, code, pairs, e1),
     )
     r_a = lax.ppermute(q, AXES, pairs_a)
     part = local(True, part, nb_v, ori_v, coef, dd, fld, e, ohs)
     return call(
         last_kernel,
         shape(VARS, NODES, EL),
-        scratch,
+        scratch + [pltpu.VMEM((VARS, NODES, EL), F32), pltpu.SemaphoreType.DMA((VARS,))],
         10000,
         (part, q, r_a, info, ohs, coef),
+        out_hbm=True,
     )
 
 

time: 23.8 us -> 23.6 us (level)
  no operation moved by 1% of the time
where the time goes in v6:
time: 23.6 us; the launch traced here: 23.4 us
  starting transfers between devices  13.8 us (58%)
  Pallas kernels  7.27 us (31%)
  waiting for transfers between devices  2.15 us (9%)
    pallas_call x9, Pallas kernels, call(): pl.pallas_call(body, out_shape=out_shape, in_specs=specs, out_specs=pl.Bl...  7.27 us
    ppermute x1, starting transfers between devices, per_device(): c_b = lax.ppermute(rows, AXES, pairs_b)  6.66 us
    ppermute x1, starting transfers between devices, per_device(): r_b = lax.ppermute(pb, AXES, pairs_b)  5.86 us
    ppermute x1, waiting for transfers between devices, per_device(): r_b = lax.ppermute(pb, AXES, pairs_b)  1.58 us
    ppermute x1, starting transfers between devices, per_device(): r_b = lax.ppermute(s_b, AXES, pairs_b[1:-1])  0.66 us
    ppermute x1, waiting for transfers between devices, per_device(): c_b = lax.ppermute(rows, AXES, pairs_b)  0.53 us
    ppermute x1, starting transfers between devices, per_device(): r_a = lax.ppermute(s_a, AXES, pairs_a)  0.52 us
  transfers between devices with their start and end apart: 6, of which 2 were waited for; matrix products, arithmetic and copies ran while one was open for 0% of the time, Pallas kernels for 15%

profile of v6, /device:TPU:0, one launch (start us, length us, event | category | flops | bytes accessed | tf_op | source)
XLA Modules:
  0.0 23.4 jit_solution(206777228612316611)
XLA Ops:
  0.0 1.6 %shard_map.64 = (f32[336,128]{1,0:T(8,128)S(1)}, f32[320,128]{1,0:T(8,128)S(1)}, f32[16,128]{1,0:T(8,128)S(1)}, f32[64,128]{1,0:T(8,128)S(1)}, f32[5,64,512]{2,1...) custom-call(s32[33]{0:T(128)} %start_hbm.3, f32[5,64,512]{2,1,0:T(8,128)} %old.1, ...), custom_call_target="tpu_custom_call" | custom-call | flops 10000 | bytes 10000 | tf_op jit(solution)/shard_map/pallas_call | solution.py:506
  1.6 0.5 %collective-permute-start = (f32[336,128]{1,0:T(8,128)S(1)}, f32[336,128]{1,0:T(8,128)S(1)}, u32[]{:S(2)}, u32[]{:S(2)}) collective-permute-start(f32[336,128]{1,0:T(8,128)S(1)} %get-tuple-element.32), channel_id=1, source_target_pairs={{0,1},{1,0},{2,3},{3,2},{4,5},{5,4},{6,7},{7,6},{8,9},{9,8},{10,11... | collective-permute-start | bytes 516104 | tf_op jit(solution)/shard_map/ppermute | solution.py:551
  2.1 0.7 %collective-permute-start.1 = (f32[320,128]{1,0:T(8,128)S(1)}, f32[320,128]{1,0:T(8,128)S(1)}, u32[]{:S(2)}, u32[]{:S(2)}) collective-permute-start(f32[320,128]{1,0:T(8,128)S(1)} %get-tuple-element.33), channel_id=1, source_target_pairs={{1,2},{2,1},{3,4},{4,3},{5,6},{6,5},{7,8},{8,7},{9,10},{10,9},{11,... | collective-permute-start | bytes 491528 | tf_op jit(solution)/shard_map/ppermute | solution.py:553
  2.8 6.7 %collective-permute-start.2 = (f32[16,128]{1,0:T(8,128)S(1)}, f32[16,128]{1,0:T(8,128)S(1)}, u32[]{:S(2)}, u32[]{:S(2)}) collective-permute-start(f32[16,128]{1,0:T(8,128)S(1)} %get-tuple-element.34.rows_ref), channel_id=1, source_target_pairs={{0,31},{1,2},{2,1},{3,4},{4,3},{5,6},{6,5},{7,8},{8,7},{9,10},{10,... | collective-permute-start | bytes 24584 | tf_op jit(solution)/shard_map/ppermute | solution.py:552
  9.5 0.9 %shard_map.65 = (f32[2,320,128]{2,1,0:T(8,128)S(1)}, bf16[128,256]{1,0:T(8,128)(2,1)S(1)}, bf16[128,192]{1,0:T(8,128)(2,1)S(1)}, f32[1,256]{1,0:T(1,128)S(1)}) custom-call(s32[33]{0:T(128)} %start_hbm.3, f32[5,64,512]{2,1,0:T(8,128)S(1)} %get-tuple-element.29.old, f32[64,128]{1,0:T(8,128)S(1)} %get-tuple-element.30.col_ref, f32[64,192]{1,0:T(8,128)} %constant.2.clone.d_hbm, ...), custom_call_target="tpu_custom_call" | custom-call | flops 10000 | bytes 10000 | tf_op jit(solution)/shard_map/pallas_call | solution.py:506
  10.4 0.5 %collective-permute-done.2.c_b = f32[16,128]{1,0:T(8,128)S(1)} collective-permute-done((f32[16,128]{1,0:T(8,128)S(1)}, f32[16,128]{1,0:T(8,128)S(1)}, u32[]{:S(2)}, u32[]{:S(2)}) %collective-permute-start.2) | collective-permute-done | bytes 8224 | tf_op jit(solution)/shard_map/ppermute | solution.py:552
  10.9 0.0 collective-permute-done.1.r_b
  10.9 0.0 collective-permute-done.r_a
  10.9 0.3 %shard_map.66 = (f32[2,320,128]{2,1,0:T(8,128)S(1)}, bf16[256,128]{1,0:T(8,128)(2,1)S(1)}, s32[8,128]{1,0:T(8,128)S(1)}, s32[16,128]{1,0:T(8,128)S(1)}, bf16[128...) custom-call(f32[2,320,128]{2,1,0:T(8,128)S(1)} %get-tuple-element.31.own, f32[336,128]{1,0:T(8,128)S(1)} %collective-permute-done.r_a, ...), custom_call_target="tpu_custom_call" | custom-call | flops 10000 | bytes 10000 | tf_op jit(solution)/shard_map/pallas_call | solution.py:506
  11.2 0.1 collective-permute-start.3
  11.3 1.2 %shard_map.67.part.fld = f32[2,320,128]{2,1,0:T(8,128)S(1)} custom-call(f32[2,320,128]{2,1,0:T(8,128)S(1)} %get-tuple-element.36.fld.rest_0_, s32[6,256]{1,0:T(8,128)S(1)} %get-tuple-element.37.nb_ref, s32[6,256]{1,0:T(8,128)S(1)} %get-tuple-element.38.ori_ref, f32[1,256]{1,0:T(1,128)S(1)} %get-tuple-element.39.coef_ref, ...), custom_call_target="tpu_custom_call" | custom-call | flops 20000 | bytes 20000 | tf_op jit(solution)/shard_map/pallas_call | solution.py:506
  12.5 0.0 collective-permute-done.3.r_a
  12.5 0.4 %shard_map.68 = (bf16[640,128]{1,0:T(8,128)(2,1)S(1)}, f32[80,128]{1,0:T(8,128)S(1)}, f32[80,128]{1,0:T(8,128)S(1)}, f32[16,128]{1,0:T(8,128)S(1)}) custom-call(f32[2,320,128]{2,1,0:T(8,128)S(1)} %shard_map.67.part.fld, f32[80,128]{1,0:T(8,128)S(1)} %get-tuple-element.41.g, f32[80,128]{1,0:T(8,128)S(1)} %collective-permute-done.3.r_a, ...), custom_call_target="tpu_custom_call" | custom-call | flops 10000 | bytes 10000 | tf_op jit(solution)/shard_map/pallas_call | solution.py:506
  12.9 5.9 %collective-permute-start.4 = (f32[80,128]{1,0:T(8,128)S(1)}, f32[80,128]{1,0:T(8,128)S(1)}, u32[]{:S(2)}, u32[]{:S(2)}) collective-permute-start(f32[80,128]{1,0:T(8,128)S(1)} %get-tuple-element.48), channel_id=1, source_target_pairs={{0,31},{1,2},{2,1},{3,4},{4,3},{5,6},{6,5},{7,8},{8,7},{9,10},{10,... | collective-permute-start | bytes 122888 | tf_op jit(solution)/shard_map/ppermute | solution.py:613
  18.8 0.1 shard_map.69.pairs
  18.9 1.6 %collective-permute-done.4.r_b = f32[80,128]{1,0:T(8,128)S(1)} collective-permute-done((f32[80,128]{1,0:T(8,128)S(1)}, f32[80,128]{1,0:T(8,128)S(1)}, u32[]{:S(2)}, u32[]{:S(2)}) %collective-permute-start.4) | collective-permute-done | bytes 40992 | tf_op jit(solution)/shard_map/ppermute | solution.py:613
  20.5 0.3 %shard_map.70 = (f32[80,128]{1,0:T(8,128)S(1)}, bf16[640,128]{1,0:T(8,128)(2,1)S(1)}) custom-call(f32[80,128]{1,0:T(8,128)S(1)} %get-tuple-element.41.g, f32[80,128]{1,0:T(8,128)S(1)} %get-tuple-element.46.after.q1, f32[16,128]{1,0:T(8,128)S(1)} %get-tuple-element.47.unit, f32[80,128]{1,0:T(8,128)S(1)} %collective-permute-done.4.r_b, ...), custom_call_target="tpu_custom_call" | custom-call | flops 10000 | bytes 10000 | tf_op jit(solution)/shard_map/pallas_call | solution.py:506
  20.8 0.1 collective-permute-start.5
  20.9 1.4 %shard_map.71.part = f32[2,320,128]{2,1,0:T(8,128)S(1)} custom-call(f32[2,320,128]{2,1,0:T(8,128)S(1)} %shard_map.67.part.fld, s32[6,256]{1,0:T(8,128)S(1)} %get-tuple-element.37.nb_ref, s32[6,256]{1,0:T(8,128)S(1)} %get-tuple-element.38.ori_ref, f32[1,256]{1,0:T(1,128)S(1)} %get-tuple-element.39.coef_ref, bf16[128,192]{1,0:T(8,128)(2,1)S(1)} %get-tuple-element.40.dd_ref, ...), custom_call_target="tpu_custom_call" | custom-call | flops 20000 | bytes 20000 | tf_op jit(solution)/shard_map/pallas_call | solution.py:506
  22.3 0.0 collective-permute-done.5.r_a
  22.3 1.0 %shard_map.72 = f32[5,64,256]{2,1,0:T(8,128)} custom-call(f32[2,320,128]{2,1,0:T(8,128)S(1)} %shard_map.71.part, f32[80,128]{1,0:T(8,128)S(1)} %get-tuple-element.52.q, f32[80,128]{1,0:T(8,128)S(1)} %collective-permute-done.5.r_a, s32[16,128]{1,0:T(8,128)S(1)} %get-tuple-element.42.info, bf16[128,256]{1,0:T(8,128)(2,1)S(1)} %get-tuple-element.51.rest_2_.ohs, ...), custom_call_target="tpu_custom_call" | custom-call | flops 10000 | bytes 10000 | tf_op jit(solution)/shard_map/pallas_call | solution.py:506
Async XLA Ops:
  1.6 9.3 %collective-permute-start = (f32[336,128]{1,0:T(8,128)S(1)}, f32[336,128]{1,0:T(8,128)S(1)}, u32[]{:S(2)}, u32[]{:S(2)}) collective-permute-start(f32[336,128]{1,0:T(8,128)S(1)} %get-tuple-element.32), channel_id=1, source_target_pairs={{0,1},{1,0},{2,3},{3,2},{4,5},{5,4},{6,7},{7,6},{8,9},{9,8},{10,11... | collective-permute-start | bytes 516104 | tf_op jit(solution)/shard_map/ppermute | solution.py:551
  2.1 8.8 %collective-permute-start.1 = (f32[320,128]{1,0:T(8,128)S(1)}, f32[320,128]{1,0:T(8,128)S(1)}, u32[]{:S(2)}, u32[]{:S(2)}) collective-permute-start(f32[320,128]{1,0:T(8,128)S(1)} %get-tuple-element.33), channel_id=1, source_target_pairs={{1,2},{2,1},{3,4},{4,3},{5,6},{6,5},{7,8},{8,7},{9,10},{10,9},{11,... | collective-permute-start | bytes 491528 | tf_op jit(solution)/shard_map/ppermute | solution.py:553
  2.8 8.1 %collective-permute-start.2 = (f32[16,128]{1,0:T(8,128)S(1)}, f32[16,128]{1,0:T(8,128)S(1)}, u32[]{:S(2)}, u32[]{:S(2)}) collective-permute-start(f32[16,128]{1,0:T(8,128)S(1)} %get-tuple-element.34.rows_ref), channel_id=1, source_target_pairs={{0,31},{1,2},{2,1},{3,4},{4,3},{5,6},{6,5},{7,8},{8,7},{9,10},{10,... | collective-permute-start | bytes 24584 | tf_op jit(solution)/shard_map/ppermute | solution.py:552
  11.2 1.3 %collective-permute-start.3 = (f32[80,128]{1,0:T(8,128)S(1)}, f32[80,128]{1,0:T(8,128)S(1)}, u32[]{:S(2)}, u32[]{:S(2)}) collective-permute-start(f32[80,128]{1,0:T(8,128)S(1)} %get-tuple-element.41.g), channel_id=1, source_target_pairs={{0,1},{1,0},{2,3},{3,2},{4,5},{5,4},{6,7},{7,6},{8,9},{9,8},{10,11... | collective-permute-start | bytes 122888 | tf_op jit(solution)/shard_map/ppermute | solution.py:602
  12.9 7.5 %collective-permute-start.4 = (f32[80,128]{1,0:T(8,128)S(1)}, f32[80,128]{1,0:T(8,128)S(1)}, u32[]{:S(2)}, u32[]{:S(2)}) collective-permute-start(f32[80,128]{1,0:T(8,128)S(1)} %get-tuple-element.48), channel_id=1, source_target_pairs={{0,31},{1,2},{2,1},{3,4},{4,3},{5,6},{6,5},{7,8},{8,7},{9,10},{10,... | collective-permute-start | bytes 122888 | tf_op jit(solution)/shard_map/ppermute | solution.py:613
  20.8 1.5 %collective-permute-start.5 = (f32[80,128]{1,0:T(8,128)S(1)}, f32[80,128]{1,0:T(8,128)S(1)}, u32[]{:S(2)}, u32[]{:S(2)}) collective-permute-start(f32[80,128]{1,0:T(8,128)S(1)} %get-tuple-element.52.q), channel_id=1, source_target_pairs={{0,1},{1,0},{2,3},{3,2},{4,5},{5,4},{6,7},{7,6},{8,9},{9,8},{10,11... | collective-permute-start | bytes 122888 | tf_op jit(solution)/shard_map/ppermute | solution.py:624

commit v7 on v6

--- a/solution.py
+++ b/solution.py
@@ -265,13 +265,19 @@
     meet[64:128, :] = jnp.zeros((64, LANES), BF)
 
 
-def fluxes(u, speeds, p):
-    out = []
+def flux_parts(u):
+    inv = pl.reciprocal(u[0])
+    speeds = [u[i] * inv for i in range(1, 4)]
+    p = 0.4 * (u[4] - 0.5 * (u[1] * speeds[0] + u[2] * speeds[1] + u[3] * speeds[2]))
+    enthalpy = u[4] + p
+    stress = {}
     for a in range(3):
-        s = speeds[a]
-        row = [u[0] * s, u[1] * s, u[2] * s, u[3] * s, (u[4] + p) * s]
-        row[1 + a] = row[1 + a] + p
-        out.append(row)
+        for b in range(a, 3):
+            t = u[1 + a] * speeds[b]
+            stress[a, b] = stress[b, a] = split(t + p if a == b else t)
+    out = [[split(u[1 + a]) for a in range(3)]]
+    out += [[stress[a, b] for a in range(3)] for b in range(3)]
+    out.append([split(enthalpy * speeds[a]) for a in range(3)])
     return out
 
 
@@ -280,7 +286,8 @@
     p = 0.4 * u[4] - 0.2 * ((u[1] * u[1] + u[2] * u[2] + u[3] * u[3]) * inv)
     mom = jnp.where(axis_is[0], u[1], jnp.where(axis_is[1], u[2], u[3]))
     s = mom * inv
-    return p, mom, s, jnp.abs(s) + jnp.sqrt(1.4 * (p * inv))
+    t = 1.4 * (p * inv)
+    return p, mom, s, jnp.abs(s) + t * lax.rsqrt(jnp.maximum(t, 1.2e-38))
 
 
 def correction(inner, outer, axis_is, sign_scale, scale):
@@ -322,12 +329,9 @@
     pieces = [[[], []] for _ in range(VARS)]
     for h in range(2):
         u = [fld[h, v * NODES : v * NODES + NODES, :] for v in range(VARS)]
-        inv = 1.0 / u[0]
-        speeds = [u[i] * inv for i in range(1, 4)]
-        p = 0.4 * (u[4] - 0.5 * (u[1] * speeds[0] + u[2] * speeds[1] + u[3] * speeds[2]))
-        fl = fluxes(u, speeds, p)
+        fl = flux_parts(u)
         for v in range(VARS):
-            hl = [split(fl[a][v]) for a in range(3)]
+            hl = fl[v]
             pieces[v][0].append(jnp.concatenate([x[0] for x in hl], 0))
             pieces[v][1].append(jnp.concatenate([x[1] for x in hl], 0))
     for v in range(VARS):

time: 23.6 us -> 23.4 us (level)
  transfers between devices with their start and end apart: 6 -> 6, of which waited for: 2 -> 3; matrix products, arithmetic and copies ran while one was open for 0% -> 0% of each run, Pallas kernels for 15% -> 15%
where the time goes in v7:
time: 23.4 us; the launch traced here: 23.2 us
  starting transfers between devices  13.7 us (59%)
  Pallas kernels  7.08 us (30%)
  waiting for transfers between devices  2.26 us (10%)
    pallas_call x9, Pallas kernels, call(): pl.pallas_call(body, out_shape=out_shape, in_specs=specs, out_specs=pl.Bl...  7.08 us
    ppermute x1, starting transfers between devices, per_device(): c_b = lax.ppermute(rows, AXES, pairs_b)  6.66 us
    ppermute x1, starting transfers between devices, per_device(): r_b = lax.ppermute(pb, AXES, pairs_b)  5.76 us
    ppermute x1, waiting for transfers between devices, per_device(): r_b = lax.ppermute(pb, AXES, pairs_b)  1.58 us
    ppermute x1, starting transfers between devices, per_device(): r_b = lax.ppermute(s_b, AXES, pairs_b[1:-1])  0.66 us
    ppermute x1, waiting for transfers between devices, per_device(): c_b = lax.ppermute(rows, AXES, pairs_b)  0.53 us
    ppermute x1, starting transfers between devices, per_device(): r_a = lax.ppermute(s_a, AXES, pairs_a)  0.52 us
  transfers between devices with their start and end apart: 6, of which 3 were waited for; matrix products, arithmetic and copies ran while one was open for 0% of the time, Pallas kernels for 15%

profile of v7, /device:TPU:0, one launch (start us, length us, event | category | flops | bytes accessed | tf_op | source)
XLA Modules:
  0.0 23.2 jit_solution(11862868315881007877)
XLA Ops:
  0.0 1.6 %shard_map.64 = (f32[336,128]{1,0:T(8,128)S(1)}, f32[320,128]{1,0:T(8,128)S(1)}, f32[16,128]{1,0:T(8,128)S(1)}, f32[64,128]{1,0:T(8,128)S(1)}, f32[5,64,512]{2,1...) custom-call(s32[33]{0:T(128)} %start_hbm.3, f32[5,64,512]{2,1,0:T(8,128)} %old.1, ...), custom_call_target="tpu_custom_call" | custom-call | flops 10000 | bytes 10000 | tf_op jit(solution)/shard_map/pallas_call | solution.py:510
  1.6 0.5 %collective-permute-start = (f32[336,128]{1,0:T(8,128)S(1)}, f32[336,128]{1,0:T(8,128)S(1)}, u32[]{:S(2)}, u32[]{:S(2)}) collective-permute-start(f32[336,128]{1,0:T(8,128)S(1)} %get-tuple-element.32), channel_id=1, source_target_pairs={{0,1},{1,0},{2,3},{3,2},{4,5},{5,4},{6,7},{7,6},{8,9},{9,8},{10,11... | collective-permute-start | bytes 516104 | tf_op jit(solution)/shard_map/ppermute | solution.py:555
  2.1 0.7 %collective-permute-start.1 = (f32[320,128]{1,0:T(8,128)S(1)}, f32[320,128]{1,0:T(8,128)S(1)}, u32[]{:S(2)}, u32[]{:S(2)}) collective-permute-start(f32[320,128]{1,0:T(8,128)S(1)} %get-tuple-element.33), channel_id=1, source_target_pairs={{1,2},{2,1},{3,4},{4,3},{5,6},{6,5},{7,8},{8,7},{9,10},{10,9},{11,... | collective-permute-start | bytes 491528 | tf_op jit(solution)/shard_map/ppermute | solution.py:557
  2.8 6.7 %collective-permute-start.2 = (f32[16,128]{1,0:T(8,128)S(1)}, f32[16,128]{1,0:T(8,128)S(1)}, u32[]{:S(2)}, u32[]{:S(2)}) collective-permute-start(f32[16,128]{1,0:T(8,128)S(1)} %get-tuple-element.34.rows_ref), channel_id=1, source_target_pairs={{0,31},{1,2},{2,1},{3,4},{4,3},{5,6},{6,5},{7,8},{8,7},{9,10},{10,... | collective-permute-start | bytes 24584 | tf_op jit(solution)/shard_map/ppermute | solution.py:556
  9.5 0.9 %shard_map.65 = (f32[2,320,128]{2,1,0:T(8,128)S(1)}, bf16[128,256]{1,0:T(8,128)(2,1)S(1)}, bf16[128,192]{1,0:T(8,128)(2,1)S(1)}, f32[1,256]{1,0:T(1,128)S(1)}) custom-call(s32[33]{0:T(128)} %start_hbm.3, f32[5,64,512]{2,1,0:T(8,128)S(1)} %get-tuple-element.29.old, f32[64,128]{1,0:T(8,128)S(1)} %get-tuple-element.30.col_ref, f32[64,192]{1,0:T(8,128)} %constant.2.clone.d_hbm, ...), custom_call_target="tpu_custom_call" | custom-call | flops 10000 | bytes 10000 | tf_op jit(solution)/shard_map/pallas_call | solution.py:510
  10.4 0.5 %collective-permute-done.2.c_b = f32[16,128]{1,0:T(8,128)S(1)} collective-permute-done((f32[16,128]{1,0:T(8,128)S(1)}, f32[16,128]{1,0:T(8,128)S(1)}, u32[]{:S(2)}, u32[]{:S(2)}) %collective-permute-start.2) | collective-permute-done | bytes 8224 | tf_op jit(solution)/shard_map/ppermute | solution.py:556
  10.9 0.0 collective-permute-done.1.r_b
  10.9 0.0 collective-permute-done.r_a
  10.9 0.3 %shard_map.66 = (f32[2,320,128]{2,1,0:T(8,128)S(1)}, bf16[256,128]{1,0:T(8,128)(2,1)S(1)}, s32[8,128]{1,0:T(8,128)S(1)}, s32[16,128]{1,0:T(8,128)S(1)}, bf16[128...) custom-call(f32[2,320,128]{2,1,0:T(8,128)S(1)} %get-tuple-element.31.own, f32[336,128]{1,0:T(8,128)S(1)} %collective-permute-done.r_a, ...), custom_call_target="tpu_custom_call" | custom-call | flops 10000 | bytes 10000 | tf_op jit(solution)/shard_map/pallas_call | solution.py:510
  11.2 0.1 collective-permute-start.3
  11.3 1.1 %shard_map.67.part.fld = f32[2,320,128]{2,1,0:T(8,128)S(1)} custom-call(f32[2,320,128]{2,1,0:T(8,128)S(1)} %get-tuple-element.36.fld.rest_0_, s32[6,256]{1,0:T(8,128)S(1)} %get-tuple-element.37.nb_ref, s32[6,256]{1,0:T(8,128)S(1)} %get-tuple-element.38.ori_ref, f32[1,256]{1,0:T(1,128)S(1)} %get-tuple-element.39.coef_ref, ...), custom_call_target="tpu_custom_call" | custom-call | flops 20000 | bytes 20000 | tf_op jit(solution)/shard_map/pallas_call | solution.py:510
  12.4 0.1 collective-permute-done.3.r_a
  12.5 0.4 %shard_map.68 = (bf16[640,128]{1,0:T(8,128)(2,1)S(1)}, f32[80,128]{1,0:T(8,128)S(1)}, f32[80,128]{1,0:T(8,128)S(1)}, f32[16,128]{1,0:T(8,128)S(1)}) custom-call(f32[2,320,128]{2,1,0:T(8,128)S(1)} %shard_map.67.part.fld, f32[80,128]{1,0:T(8,128)S(1)} %get-tuple-element.41.g, f32[80,128]{1,0:T(8,128)S(1)} %collective-permute-done.3.r_a, ...), custom_call_target="tpu_custom_call" | custom-call | flops 10000 | bytes 10000 | tf_op jit(solution)/shard_map/pallas_call | solution.py:510
  12.9 5.8 %collective-permute-start.4 = (f32[80,128]{1,0:T(8,128)S(1)}, f32[80,128]{1,0:T(8,128)S(1)}, u32[]{:S(2)}, u32[]{:S(2)}) collective-permute-start(f32[80,128]{1,0:T(8,128)S(1)} %get-tuple-element.48), channel_id=1, source_target_pairs={{0,31},{1,2},{2,1},{3,4},{4,3},{5,6},{6,5},{7,8},{8,7},{9,10},{10,... | collective-permute-start | bytes 122888 | tf_op jit(solution)/shard_map/ppermute | solution.py:617
  18.7 0.1 shard_map.69.pairs
  18.8 1.6 %collective-permute-done.4.r_b = f32[80,128]{1,0:T(8,128)S(1)} collective-permute-done((f32[80,128]{1,0:T(8,128)S(1)}, f32[80,128]{1,0:T(8,128)S(1)}, u32[]{:S(2)}, u32[]{:S(2)}) %collective-permute-start.4) | collective-permute-done | bytes 40992 | tf_op jit(solution)/shard_map/ppermute | solution.py:617
  20.4 0.3 %shard_map.70 = (f32[80,128]{1,0:T(8,128)S(1)}, bf16[640,128]{1,0:T(8,128)(2,1)S(1)}) custom-call(f32[80,128]{1,0:T(8,128)S(1)} %get-tuple-element.41.g, f32[80,128]{1,0:T(8,128)S(1)} %get-tuple-element.46.after.q1, f32[16,128]{1,0:T(8,128)S(1)} %get-tuple-element.47.unit, f32[80,128]{1,0:T(8,128)S(1)} %collective-permute-done.4.r_b, ...), custom_call_target="tpu_custom_call" | custom-call | flops 10000 | bytes 10000 | tf_op jit(solution)/shard_map/pallas_call | solution.py:510
  20.7 0.1 collective-permute-start.5
  20.8 1.3 %shard_map.71.part = f32[2,320,128]{2,1,0:T(8,128)S(1)} custom-call(f32[2,320,128]{2,1,0:T(8,128)S(1)} %shard_map.67.part.fld, s32[6,256]{1,0:T(8,128)S(1)} %get-tuple-element.37.nb_ref, s32[6,256]{1,0:T(8,128)S(1)} %get-tuple-element.38.ori_ref, f32[1,256]{1,0:T(1,128)S(1)} %get-tuple-element.39.coef_ref, bf16[128,192]{1,0:T(8,128)(2,1)S(1)} %get-tuple-element.40.dd_ref, ...), custom_call_target="tpu_custom_call" | custom-call | flops 20000 | bytes 20000 | tf_op jit(solution)/shard_map/pallas_call | solution.py:510
  22.1 0.0 collective-permute-done.5.r_a
  22.1 1.0 %shard_map.72 = f32[5,64,256]{2,1,0:T(8,128)} custom-call(f32[2,320,128]{2,1,0:T(8,128)S(1)} %shard_map.71.part, f32[80,128]{1,0:T(8,128)S(1)} %get-tuple-element.52.q, f32[80,128]{1,0:T(8,128)S(1)} %collective-permute-done.5.r_a, s32[16,128]{1,0:T(8,128)S(1)} %get-tuple-element.42.info, bf16[128,256]{1,0:T(8,128)(2,1)S(1)} %get-tuple-element.51.rest_2_.ohs, ...), custom_call_target="tpu_custom_call" | custom-call | flops 10000 | bytes 10000 | tf_op jit(solution)/shard_map/pallas_call | solution.py:510
Async XLA Ops:
  1.6 9.3 %collective-permute-start = (f32[336,128]{1,0:T(8,128)S(1)}, f32[336,128]{1,0:T(8,128)S(1)}, u32[]{:S(2)}, u32[]{:S(2)}) collective-permute-start(f32[336,128]{1,0:T(8,128)S(1)} %get-tuple-element.32), channel_id=1, source_target_pairs={{0,1},{1,0},{2,3},{3,2},{4,5},{5,4},{6,7},{7,6},{8,9},{9,8},{10,11... | collective-permute-start | bytes 516104 | tf_op jit(solution)/shard_map/ppermute | solution.py:555
  2.1 8.8 %collective-permute-start.1 = (f32[320,128]{1,0:T(8,128)S(1)}, f32[320,128]{1,0:T(8,128)S(1)}, u32[]{:S(2)}, u32[]{:S(2)}) collective-permute-start(f32[320,128]{1,0:T(8,128)S(1)} %get-tuple-element.33), channel_id=1, source_target_pairs={{1,2},{2,1},{3,4},{4,3},{5,6},{6,5},{7,8},{8,7},{9,10},{10,9},{11,... | collective-permute-start | bytes 491528 | tf_op jit(solution)/shard_map/ppermute | solution.py:557
  2.8 8.1 %collective-permute-start.2 = (f32[16,128]{1,0:T(8,128)S(1)}, f32[16,128]{1,0:T(8,128)S(1)}, u32[]{:S(2)}, u32[]{:S(2)}) collective-permute-start(f32[16,128]{1,0:T(8,128)S(1)} %get-tuple-element.34.rows_ref), channel_id=1, source_target_pairs={{0,31},{1,2},{2,1},{3,4},{4,3},{5,6},{6,5},{7,8},{8,7},{9,10},{10,... | collective-permute-start | bytes 24584 | tf_op jit(solution)/shard_map/ppermute | solution.py:556
  11.2 1.3 %collective-permute-start.3 = (f32[80,128]{1,0:T(8,128)S(1)}, f32[80,128]{1,0:T(8,128)S(1)}, u32[]{:S(2)}, u32[]{:S(2)}) collective-permute-start(f32[80,128]{1,0:T(8,128)S(1)} %get-tuple-element.41.g), channel_id=1, source_target_pairs={{0,1},{1,0},{2,3},{3,2},{4,5},{5,4},{6,7},{7,6},{8,9},{9,8},{10,11... | collective-permute-start | bytes 122888 | tf_op jit(solution)/shard_map/ppermute | solution.py:606
  12.9 7.4 %collective-permute-start.4 = (f32[80,128]{1,0:T(8,128)S(1)}, f32[80,128]{1,0:T(8,128)S(1)}, u32[]{:S(2)}, u32[]{:S(2)}) collective-permute-start(f32[80,128]{1,0:T(8,128)S(1)} %get-tuple-element.48), channel_id=1, source_target_pairs={{0,31},{1,2},{2,1},{3,4},{4,3},{5,6},{6,5},{7,8},{8,7},{9,10},{10,... | collective-permute-start | bytes 122888 | tf_op jit(solution)/shard_map/ppermute | solution.py:617
  20.7 1.4 %collective-permute-start.5 = (f32[80,128]{1,0:T(8,128)S(1)}, f32[80,128]{1,0:T(8,128)S(1)}, u32[]{:S(2)}, u32[]{:S(2)}) collective-permute-start(f32[80,128]{1,0:T(8,128)S(1)} %get-tuple-element.52.q), channel_id=1, source_target_pairs={{0,1},{1,0},{2,3},{3,2},{4,5},{5,4},{6,7},{7,6},{8,9},{9,8},{10,11... | collective-permute-start | bytes 122888 | tf_op jit(solution)/shard_map/ppermute | solution.py:628

commit v8 on v7

--- a/solution.py
+++ b/solution.py
@@ -91,13 +91,17 @@
     return (lax.axis_index("gx") * sizes[1] + lax.axis_index("gy")) * sizes[2] + lax.axis_index("gz")
 
 
-def places(mask):
-    count = mask.shape[0]
+def triangles(count):
     upper = jnp.where(iota((EL, EL), 0) <= iota((EL, EL), 1), 1.0, 0.0).astype(BF)
-    inclusive = mm(mask.astype(BF), upper)
-    total = jnp.broadcast_to(inclusive[:, EL - 1 : EL], (count, LANES)).astype(BF)
     r, c = iota((count, count), 0), iota((count, count), 1)
     lower = jnp.where((c < r) & ((c >> 3) == (r >> 3)), 1.0, 0.0).astype(BF)
+    return upper, lower
+
+
+def places(mask, upper, lower):
+    inclusive = mm(mask.astype(BF), upper)
+    total = jnp.sum(mask, 1, keepdims=True)
+    total = jnp.broadcast_to(total, (mask.shape[0], LANES)).astype(BF)
     offset = mm(lower, total)[:, 0:1]
     return jnp.where(mask > 0.5, inclusive + offset - 1.0, -1.0)
 
@@ -126,12 +130,13 @@
     up = jnp.where(d + 1 == n, 0, d + 1) * EL
     down = jnp.where(d == 0, n - 1, d - 1) * EL
     mk[...] = jnp.zeros((16, EL), F32)
+    upper, lower = triangles(16)
     copies[0].wait()
     nb = nb_v[...]
     rel = [nb - jnp.where(even, up, down), nb - jnp.where(even, down, up)]
     for k in range(2):
         mk[8 * k : 8 * k + FACES, :] = jnp.where((rel[k] >= 0) & (rel[k] < EL), 1.0, 0.0)
-    place = places(mk[...])
+    place = places(mk[...], upper, lower)
     copies[1].wait()
     face = iota((FACES, EL), 0)
     own = (face * EL + iota((FACES, EL), 1) + 2048 * ori_v[...]).astype(F32)

time: 23.4 us -> 23.3 us (level)
  no operation moved by 1% of the time
where the time goes in v8:
time: 23.3 us; the launch traced here: 23 us
  starting transfers between devices  13.7 us (59%)
  Pallas kernels  6.96 us (30%)
  waiting for transfers between devices  2.26 us (10%)
    pallas_call x9, Pallas kernels, call(): pl.pallas_call(body, out_shape=out_shape, in_specs=specs, out_specs=pl.Bl...  6.96 us
    ppermute x1, starting transfers between devices, per_device(): c_b = lax.ppermute(rows, AXES, pairs_b)  6.66 us
    ppermute x1, starting transfers between devices, per_device(): r_b = lax.ppermute(pb, AXES, pairs_b)  5.76 us
    ppermute x1, waiting for transfers between devices, per_device(): r_b = lax.ppermute(pb, AXES, pairs_b)  1.58 us
    ppermute x1, starting transfers between devices, per_device(): r_b = lax.ppermute(s_b, AXES, pairs_b[1:-1])  0.66 us
    ppermute x1, waiting for transfers between devices, per_device(): c_b = lax.ppermute(rows, AXES, pairs_b)  0.53 us
    ppermute x1, starting transfers between devices, per_device(): r_a = lax.ppermute(s_a, AXES, pairs_a)  0.52 us
  transfers between devices with their start and end apart: 6, of which 3 were waited for; matrix products, arithmetic and copies ran while one was open for 0% of the time, Pallas kernels for 15%

profile of v8, /device:TPU:0, one launch (start us, length us, event | category | flops | bytes accessed | tf_op | source)
XLA Modules:
  0.0 23.0 jit_solution(5637545146992380193)
XLA Ops:
  0.0 1.5 %shard_map.64 = (f32[336,128]{1,0:T(8,128)S(1)}, f32[320,128]{1,0:T(8,128)S(1)}, f32[16,128]{1,0:T(8,128)S(1)}, f32[64,128]{1,0:T(8,128)S(1)}, f32[5,64,512]{2,1...) custom-call(s32[33]{0:T(128)} %start_hbm.3, f32[5,64,512]{2,1,0:T(8,128)} %old.1, ...), custom_call_target="tpu_custom_call" | custom-call | flops 10000 | bytes 10000 | tf_op jit(solution)/shard_map/pallas_call | solution.py:515
  1.5 0.5 %collective-permute-start = (f32[336,128]{1,0:T(8,128)S(1)}, f32[336,128]{1,0:T(8,128)S(1)}, u32[]{:S(2)}, u32[]{:S(2)}) collective-permute-start(f32[336,128]{1,0:T(8,128)S(1)} %get-tuple-element.32), channel_id=1, source_target_pairs={{0,1},{1,0},{2,3},{3,2},{4,5},{5,4},{6,7},{7,6},{8,9},{9,8},{10,11... | collective-permute-start | bytes 516104 | tf_op jit(solution)/shard_map/ppermute | solution.py:560
  2.0 0.7 %collective-permute-start.1 = (f32[320,128]{1,0:T(8,128)S(1)}, f32[320,128]{1,0:T(8,128)S(1)}, u32[]{:S(2)}, u32[]{:S(2)}) collective-permute-start(f32[320,128]{1,0:T(8,128)S(1)} %get-tuple-element.33), channel_id=1, source_target_pairs={{1,2},{2,1},{3,4},{4,3},{5,6},{6,5},{7,8},{8,7},{9,10},{10,9},{11,... | collective-permute-start | bytes 491528 | tf_op jit(solution)/shard_map/ppermute | solution.py:562
  2.7 6.7 %collective-permute-start.2 = (f32[16,128]{1,0:T(8,128)S(1)}, f32[16,128]{1,0:T(8,128)S(1)}, u32[]{:S(2)}, u32[]{:S(2)}) collective-permute-start(f32[16,128]{1,0:T(8,128)S(1)} %get-tuple-element.34.rows_ref), channel_id=1, source_target_pairs={{0,31},{1,2},{2,1},{3,4},{4,3},{5,6},{6,5},{7,8},{8,7},{9,10},{10,... | collective-permute-start | bytes 24584 | tf_op jit(solution)/shard_map/ppermute | solution.py:561
  9.3 0.9 %shard_map.65 = (f32[2,320,128]{2,1,0:T(8,128)S(1)}, bf16[128,256]{1,0:T(8,128)(2,1)S(1)}, bf16[128,192]{1,0:T(8,128)(2,1)S(1)}, f32[1,256]{1,0:T(1,128)S(1)}) custom-call(s32[33]{0:T(128)} %start_hbm.3, f32[5,64,512]{2,1,0:T(8,128)S(1)} %get-tuple-element.29.old, f32[64,128]{1,0:T(8,128)S(1)} %get-tuple-element.30.col_ref, f32[64,192]{1,0:T(8,128)} %constant.2.clone.d_hbm, ...), custom_call_target="tpu_custom_call" | custom-call | flops 10000 | bytes 10000 | tf_op jit(solution)/shard_map/pallas_call | solution.py:515
  10.3 0.5 %collective-permute-done.2.c_b = f32[16,128]{1,0:T(8,128)S(1)} collective-permute-done((f32[16,128]{1,0:T(8,128)S(1)}, f32[16,128]{1,0:T(8,128)S(1)}, u32[]{:S(2)}, u32[]{:S(2)}) %collective-permute-start.2) | collective-permute-done | bytes 8224 | tf_op jit(solution)/shard_map/ppermute | solution.py:561
  10.8 0.0 collective-permute-done.1.r_b
  10.8 0.0 collective-permute-done.r_a
  10.8 0.3 %shard_map.66 = (f32[2,320,128]{2,1,0:T(8,128)S(1)}, bf16[256,128]{1,0:T(8,128)(2,1)S(1)}, s32[8,128]{1,0:T(8,128)S(1)}, s32[16,128]{1,0:T(8,128)S(1)}, bf16[128...) custom-call(f32[2,320,128]{2,1,0:T(8,128)S(1)} %get-tuple-element.31.own, f32[336,128]{1,0:T(8,128)S(1)} %collective-permute-done.r_a, ...), custom_call_target="tpu_custom_call" | custom-call | flops 10000 | bytes 10000 | tf_op jit(solution)/shard_map/pallas_call | solution.py:515
  11.1 0.1 collective-permute-start.3
  11.2 1.1 %shard_map.67.part.fld = f32[2,320,128]{2,1,0:T(8,128)S(1)} custom-call(f32[2,320,128]{2,1,0:T(8,128)S(1)} %get-tuple-element.36.fld.rest_0_, s32[6,256]{1,0:T(8,128)S(1)} %get-tuple-element.37.nb_ref, s32[6,256]{1,0:T(8,128)S(1)} %get-tuple-element.38.ori_ref, f32[1,256]{1,0:T(1,128)S(1)} %get-tuple-element.39.coef_ref, ...), custom_call_target="tpu_custom_call" | custom-call | flops 20000 | bytes 20000 | tf_op jit(solution)/shard_map/pallas_call | solution.py:515
  12.2 0.1 collective-permute-done.3.r_a
  12.4 0.4 %shard_map.68 = (bf16[640,128]{1,0:T(8,128)(2,1)S(1)}, f32[80,128]{1,0:T(8,128)S(1)}, f32[80,128]{1,0:T(8,128)S(1)}, f32[16,128]{1,0:T(8,128)S(1)}) custom-call(f32[2,320,128]{2,1,0:T(8,128)S(1)} %shard_map.67.part.fld, f32[80,128]{1,0:T(8,128)S(1)} %get-tuple-element.41.g, f32[80,128]{1,0:T(8,128)S(1)} %collective-permute-done.3.r_a, ...), custom_call_target="tpu_custom_call" | custom-call | flops 10000 | bytes 10000 | tf_op jit(solution)/shard_map/pallas_call | solution.py:515
  12.8 5.8 %collective-permute-start.4 = (f32[80,128]{1,0:T(8,128)S(1)}, f32[80,128]{1,0:T(8,128)S(1)}, u32[]{:S(2)}, u32[]{:S(2)}) collective-permute-start(f32[80,128]{1,0:T(8,128)S(1)} %get-tuple-element.48), channel_id=1, source_target_pairs={{0,31},{1,2},{2,1},{3,4},{4,3},{5,6},{6,5},{7,8},{8,7},{9,10},{10,... | collective-permute-start | bytes 122888 | tf_op jit(solution)/shard_map/ppermute | solution.py:622
  18.6 0.1 shard_map.69.pairs
  18.7 1.6 %collective-permute-done.4.r_b = f32[80,128]{1,0:T(8,128)S(1)} collective-permute-done((f32[80,128]{1,0:T(8,128)S(1)}, f32[80,128]{1,0:T(8,128)S(1)}, u32[]{:S(2)}, u32[]{:S(2)}) %collective-permute-start.4) | collective-permute-done | bytes 40992 | tf_op jit(solution)/shard_map/ppermute | solution.py:622
  20.3 0.3 %shard_map.70 = (f32[80,128]{1,0:T(8,128)S(1)}, bf16[640,128]{1,0:T(8,128)(2,1)S(1)}) custom-call(f32[80,128]{1,0:T(8,128)S(1)} %get-tuple-element.41.g, f32[80,128]{1,0:T(8,128)S(1)} %get-tuple-element.46.after.q1, f32[16,128]{1,0:T(8,128)S(1)} %get-tuple-element.47.unit, f32[80,128]{1,0:T(8,128)S(1)} %collective-permute-done.4.r_b, ...), custom_call_target="tpu_custom_call" | custom-call | flops 10000 | bytes 10000 | tf_op jit(solution)/shard_map/pallas_call | solution.py:515
  20.6 0.1 collective-permute-start.5
  20.7 1.3 %shard_map.71.part = f32[2,320,128]{2,1,0:T(8,128)S(1)} custom-call(f32[2,320,128]{2,1,0:T(8,128)S(1)} %shard_map.67.part.fld, s32[6,256]{1,0:T(8,128)S(1)} %get-tuple-element.37.nb_ref, s32[6,256]{1,0:T(8,128)S(1)} %get-tuple-element.38.ori_ref, f32[1,256]{1,0:T(1,128)S(1)} %get-tuple-element.39.coef_ref, bf16[128,192]{1,0:T(8,128)(2,1)S(1)} %get-tuple-element.40.dd_ref, ...), custom_call_target="tpu_custom_call" | custom-call | flops 20000 | bytes 20000 | tf_op jit(solution)/shard_map/pallas_call | solution.py:515
  22.0 0.0 collective-permute-done.5.r_a
  22.0 1.0 %shard_map.72 = f32[5,64,256]{2,1,0:T(8,128)} custom-call(f32[2,320,128]{2,1,0:T(8,128)S(1)} %shard_map.71.part, f32[80,128]{1,0:T(8,128)S(1)} %get-tuple-element.52.q, f32[80,128]{1,0:T(8,128)S(1)} %collective-permute-done.5.r_a, s32[16,128]{1,0:T(8,128)S(1)} %get-tuple-element.42.info, bf16[128,256]{1,0:T(8,128)(2,1)S(1)} %get-tuple-element.51.rest_2_.ohs, ...), custom_call_target="tpu_custom_call" | custom-call | flops 10000 | bytes 10000 | tf_op jit(solution)/shard_map/pallas_call | solution.py:515
Async XLA Ops:
  1.5 9.3 %collective-permute-start = (f32[336,128]{1,0:T(8,128)S(1)}, f32[336,128]{1,0:T(8,128)S(1)}, u32[]{:S(2)}, u32[]{:S(2)}) collective-permute-start(f32[336,128]{1,0:T(8,128)S(1)} %get-tuple-element.32), channel_id=1, source_target_pairs={{0,1},{1,0},{2,3},{3,2},{4,5},{5,4},{6,7},{7,6},{8,9},{9,8},{10,11... | collective-permute-start | bytes 516104 | tf_op jit(solution)/shard_map/ppermute | solution.py:560
  2.0 8.8 %collective-permute-start.1 = (f32[320,128]{1,0:T(8,128)S(1)}, f32[320,128]{1,0:T(8,128)S(1)}, u32[]{:S(2)}, u32[]{:S(2)}) collective-permute-start(f32[320,128]{1,0:T(8,128)S(1)} %get-tuple-element.33), channel_id=1, source_target_pairs={{1,2},{2,1},{3,4},{4,3},{5,6},{6,5},{7,8},{8,7},{9,10},{10,9},{11,... | collective-permute-start | bytes 491528 | tf_op jit(solution)/shard_map/ppermute | solution.py:562
  2.7 8.1 %collective-permute-start.2 = (f32[16,128]{1,0:T(8,128)S(1)}, f32[16,128]{1,0:T(8,128)S(1)}, u32[]{:S(2)}, u32[]{:S(2)}) collective-permute-start(f32[16,128]{1,0:T(8,128)S(1)} %get-tuple-element.34.rows_ref), channel_id=1, source_target_pairs={{0,31},{1,2},{2,1},{3,4},{4,3},{5,6},{6,5},{7,8},{8,7},{9,10},{10,... | collective-permute-start | bytes 24584 | tf_op jit(solution)/shard_map/ppermute | solution.py:561
  11.1 1.3 %collective-permute-start.3 = (f32[80,128]{1,0:T(8,128)S(1)}, f32[80,128]{1,0:T(8,128)S(1)}, u32[]{:S(2)}, u32[]{:S(2)}) collective-permute-start(f32[80,128]{1,0:T(8,128)S(1)} %get-tuple-element.41.g), channel_id=1, source_target_pairs={{0,1},{1,0},{2,3},{3,2},{4,5},{5,4},{6,7},{7,6},{8,9},{9,8},{10,11... | collective-permute-start | bytes 122888 | tf_op jit(solution)/shard_map/ppermute | solution.py:611
  12.8 7.4 %collective-permute-start.4 = (f32[80,128]{1,0:T(8,128)S(1)}, f32[80,128]{1,0:T(8,128)S(1)}, u32[]{:S(2)}, u32[]{:S(2)}) collective-permute-start(f32[80,128]{1,0:T(8,128)S(1)} %get-tuple-element.48), channel_id=1, source_target_pairs={{0,31},{1,2},{2,1},{3,4},{4,3},{5,6},{6,5},{7,8},{8,7},{9,10},{10,... | collective-permute-start | bytes 122888 | tf_op jit(solution)/shard_map/ppermute | solution.py:622
  20.6 1.4 %collective-permute-start.5 = (f32[80,128]{1,0:T(8,128)S(1)}, f32[80,128]{1,0:T(8,128)S(1)}, u32[]{:S(2)}, u32[]{:S(2)}) collective-permute-start(f32[80,128]{1,0:T(8,128)S(1)} %get-tuple-element.52.q), channel_id=1, source_target_pairs={{0,1},{1,0},{2,3},{3,2},{4,5},{5,4},{6,7},{7,6},{8,9},{9,8},{10,11... | collective-permute-start | bytes 122888 | tf_op jit(solution)/shard_map/ppermute | solution.py:633
